TPU v7x, 32 devices: a whole 2x2x4 slice. The times are simulated.
32 devices in a mesh: lines: 2 (over y), shots: 16 (over z, x, core).
Axes of the slice: x: 2, y: 2, z: 4, core: 2. Of those that a mesh axis runs over, the one named last changes fastest.
Arguments:
- records: bfloat16 [2048, 1024, 256], P(('lines', 'shots')), parts along dimension 0, may hold values from -6 to 6
- missing: int32 [256], P('lines'), parts along dimension 0, may hold values from 0 to 1023, as said below
- neighbours: int32 [256, 3], P('lines'), parts along dimension 0, may hold values from 0 to 1023, as said below
- weights: float32 [256, 3], P('lines'), parts along dimension 0, may hold values from 0.2 to 0.6
- freq_bins: int32 [8], replicated, may hold values from 1 to 127, as said below
Outputs:
- multiples: bfloat16 [2048, 1024, 256], P(('lines', 'shots')), parts along dimension 0
There are 2 independent parts, one for each index of `lines`. A program takes and returns all parts, laid end to end along the dimension named above; an argument that names none is the same for every part. Nothing has to cross between parts.
Inputs may be any that keep to these rules, and one draw needn't show every extreme that they name: `missing`: distinct and ascending; any two missing shots lie 3 or more apart, and every shot within 2 of a missing shot is recorded. `neighbours`: row i names 3 distinct recorded shots, each within 2 of missing[i]. `freq_bins`: 8 distinct bins.
All inputs are finite; a program needn't handle non-finite values.
Results may differ from a plain program's by a relative error of at most 0.0079.
Values may be sent and summed in bfloat16 or wider, within the bound.
No kernel may reach another device: no remote copies, remote signals or barrier semaphores. Data moves between devices by JAX's collectives and lax.ppermute only.
A program may use at most 192 MiB of HBM per device.

v0:
```python
import math

import jax
import jax.numpy as jnp
from jax import lax
from jax.sharding import PartitionSpec as P


def from_partner(array, axis, stride):
    return lax.ppermute(array, axis, [(i, i ^ 1 << stride) for i in range(lax.axis_size(axis))])


def tables(freq_bins, sample_count):
    bin_count = freq_bins.shape[0]
    sample_ids = jnp.arange(sample_count, dtype=jnp.int32)
    phases = freq_bins[None, :] * sample_ids[:, None] % sample_count
    angles = phases.astype(jnp.float32) * (2.0 * math.pi / sample_count)
    trig_pair = jnp.stack([jnp.cos(angles), -jnp.sin(angles)], axis=-1)
    forward = (trig_pair / math.sqrt(sample_count)).astype(jnp.bfloat16)
    inverse = (trig_pair * math.sqrt(2.0 / bin_count)).astype(jnp.bfloat16)
    return (forward, inverse)


def add_block(summed, right_source, block_piece, source_part, width):
    right_rows = lax.dynamic_slice_in_dim(right_source, source_part * width, width, 2)
    right_real = right_rows[:, 0]
    right_imag = right_rows[:, 1]
    left_side = jnp.concatenate([block_piece[:, 0], block_piece[:, 1]], axis=-1)
    right_side = jnp.concatenate(
        [
            jnp.concatenate([right_real, right_imag], axis=-1),
            jnp.concatenate([-right_imag, right_real], axis=-1),
        ],
        axis=1,
    )
    return summed + jnp.einsum(
        "zsk,zkc->zsc", left_side, right_side, preferred_element_type=jnp.float32
    )


def shards(records, missing, neighbours, weights, freq_bins):
    devices = lax.axis_size("shots")
    position = lax.axis_index("shots")
    shot_rows = records.shape[0]
    matrix_order = records.shape[1]
    sample_count = records.shape[2]
    half = matrix_order // 2
    couples = devices // 2
    neigh_count = neighbours.shape[1]
    forward, inverse = tables(freq_bins, sample_count)
    blocked = records.reshape(shot_rows, 2, half, sample_count)
    spectra = jnp.einsum(
        "shrt,tpc->phcsr", blocked, forward, preferred_element_type=jnp.float32
    ).astype(jnp.bfloat16)
    outgoing = spectra.reshape(devices, 2, shot_rows, half)
    incoming = lax.all_to_all(outgoing, "shots", split_axis=0, concat_axis=2, tiled=True)
    own_block = incoming
    filled_rows = jnp.zeros(
        own_block.shape[:2] + (missing.shape[0], own_block.shape[3]), jnp.float32
    )
    for slot_index in range(neigh_count):
        picked = jnp.take(own_block, neighbours[:, slot_index], axis=2)
        filled_rows = filled_rows + weights[:, slot_index][:, None] * picked.astype(jnp.float32)
    own_block = own_block.at[:, :, missing, :].set(filled_rows.astype(jnp.bfloat16))
    factor = -1.0 / math.sqrt(matrix_order)
    member = position % 2
    other_half = from_partner(own_block, "shots", 0)
    summed = jnp.zeros((1, matrix_order, 2 * half), jnp.float32)
    summed = add_block(summed, own_block, own_block, member, half)
    summed = add_block(summed, own_block, other_half, 1 - member, half)
    predicted = (summed * factor).astype(jnp.bfloat16)
    outgoing_back = predicted.reshape(1, 1, matrix_order, 2, half)
    returned = lax.all_to_all(outgoing_back, "shots", split_axis=2, concat_axis=0, tiled=True)
    returned = returned.reshape(couples, 2, shot_rows, 2, half)
    inverse_pair = jnp.transpose(inverse, (1, 2, 0))
    multiples = jnp.einsum(
        "phsir,pit->shrt", returned, inverse_pair, preferred_element_type=jnp.float32
    )
    return multiples.astype(jnp.bfloat16).reshape(shot_rows, matrix_order, sample_count)


def solution(mesh):
    return jax.shard_map(
        shards,
        mesh=mesh,
        in_specs=(
            P(("lines", "shots"), None, None),
            P("lines"),
            P("lines", None),
            P("lines", None),
            P(),
        ),
        out_specs=P(("lines", "shots"), None, None),
        check_vma=False,
    )
```

profile of v0, /device:TPU:1, one launch (start us, length us, event | category | flops | bytes accessed | tf_op | source)
XLA Modules:
  0.0 226.2 jit_solution(15952306101126947677)
XLA Ops:
  0.0 0.8 fusion.33
  0.8 14.2 %convert_bitcast_fusion = bf16[8,2,2,64,512]{4,0,1,3,2:T(8,128)(2,1)S(1)} fusion(bf16[64,2,512,256,1]{3,2,1,0,4:T(8,128)(2,1)} %bitcast.127, f32[256,8,1]{0,1,2:T(8,128)S(1)} %get-tuple-element.30, f32[256,8,1]{0,1,2:T(8,128)S(1)} %get-tuple-element.29), kind=kOutput, calls=%fused_computation.31 | convolution fusion | flops 537931776 | bytes 35667968 | tf_op jit(solution)/shard_map/shrt,tpc->phcsr/dot_general | solution.py:52
  15.0 2.5 %copy.40 = bf16[8,2,2,64,512]{4,3,2,1,0:T(8,128)(2,1)} copy(bf16[8,2,2,64,512]{4,0,1,3,2:T(8,128)(2,1)S(1)} %convert_bitcast_fusion) | data formatting | bytes 4194304 | tf_op jit(solution)/shard_map/convert_element_type | solution.py:54
  17.5 7.4 %all-to-all-start = ((bf16[16,2,64,512]{3,2,1,0:T(8,128)(2,1)}), bf16[16,2,64,512]{3,2,1,0:T(8,128)(2,1)S(1)}, u32[]{:S(2)}, u32[]{:S(2)}) async-start(bf16[16,2,64,512]{3,2,1,0:T(8,128)(2,1)} %bitcast.131), calls=%async_computation | async-start | bytes 4194304 | tf_op jit(solution)/shard_map/all_to_all | solution.py:56
  25.0 41.4 %all-to-all-done = bf16[16,2,64,512]{3,2,1,0:T(8,128)(2,1)S(1)} async-done(((bf16[16,2,64,512]{3,2,1,0:T(8,128)(2,1)}), bf16[16,2,64,512]{3,2,1,0:T(8,128)(2,1)S(1)}, u32[]{:S(2)}, u32[]{:S(2)}) %all-to-all-start) | async-done | bytes 2097184 | tf_op jit(solution)/shard_map/all_to_all | solution.py:56
  66.4 1.3 copy-done
  67.8 3.9 %copy.41 = bf16[1,2,16,64,512]{4,1,3,2,0:T(2,128)(2,1)S(1)} copy(bf16[1,2,16,64,512]{4,3,1,2,0:T(8,128)(2,1)} %bitcast.128) | data formatting | bytes 4194304 | tf_op jit(solution)/shard_map/all_to_all | solution.py:56
  71.9 3.5 %copy.77 = bf16[1,2,1024,512]{3,1,2,0:T(2,128)(2,1)} copy(bf16[1,2,1024,512]{3,2,1,0:T(8,128)(2,1)S(1)} %bitcast.132) | data formatting | bytes 4194304 | tf_op jit(solution)/shard_map/all_to_all | solution.py:56
  75.4 2.7 %gather_fusion.2 = bf16[128,2,512]{2,1,0:T(2,128)(2,1)S(1)} fusion(bf16[2,1024,512]{2,0,1:T(2,128)(2,1)} %bitcast.137, s32[1024]{0:T(1024)S(1)} %get-tuple-element.31), kind=kCustom, calls=%fused_computation.2.clone | custom fusion | bytes 524800 | tf_op jit(solution)/shard_map/jit(_take)/gather | solution.py:62
  78.1 2.7 %gather_fusion.1 = bf16[128,2,512]{2,1,0:T(2,128)(2,1)S(1)} fusion(bf16[2,1024,512]{2,0,1:T(2,128)(2,1)} %bitcast.138, s32[1024]{0:T(1024)S(1)} %get-tuple-element.32), kind=kCustom, calls=%fused_computation.1.clone | custom fusion | bytes 524800 | tf_op jit(solution)/shard_map/jit(_take)/gather | solution.py:62
  80.8 2.7 %gather_fusion = bf16[128,2,512]{2,1,0:T(2,128)(2,1)S(1)} fusion(bf16[2,1024,512]{2,0,1:T(2,128)(2,1)} %bitcast.139, s32[1024]{0:T(1024)S(1)} %pad_clamp_fusion.2), kind=kCustom, calls=%fused_computation.clone | custom fusion | bytes 524800 | tf_op jit(solution)/shard_map/jit(_take)/gather | solution.py:62
  84.1 4.4 %scatter_fusion = bf16[2,1024,512]{2,0,1:T(2,128)(2,1)S(1)} fusion(bf16[2,1024,512]{2,0,1:T(2,128)(2,1)S(1)} %bitcast.124, s32[128]{0:T(128)S(1)} %compare_select_fusion.3, bf16[128,2,512]{2,1,0:T(2,128)(2,1)S(1)} %copy.49), kind=kCustom, calls=%fused_computation.3 | custom fusion | bytes 786944 | tf_op jit(solution)/shard_map/scatter | solution.py:64
  88.5 1.4 constant_dynamic-slice_fusion
  90.4 3.2 %fusion.43 = (bf16[1,1,1024,512]{3,1,2,0:T(2,128)(2,1)S(1)}, bf16[1,1,1024,512]{3,1,2,0:T(2,128)(2,1)S(1)}) fusion(bf16[1,2,1024,512]{3,1,2,0:T(2,128)(2,1)S(1)} %bitcast.126), kind=kLoop, calls=%fused_computation.89 | loop fusion | bytes 4194304 | tf_op jit(solution)/shard_map/slice | solution.py:28
  93.6 0.3 copy.81
  93.9 0.3 copy.80
  94.5 2.5 %fusion.1 = f32[1024,1024]{0,1:T(8,128)S(1)} fusion(bf16[1,1024,512]{2,1,0:T(8,128)(2,1)S(1)} %bitcast.142, bf16[1,1024,512]{2,1,0:T(8,128)(2,1)S(1)} %bitcast.141, bf16[1,512,512]{2,1,0:T(8,128)(2,1)S(1)} %get-tuple-element.21, bf16[1,512,512]{2,1,0:T(8,128)(2,1)S(1)} %fusion.40, bf16[1,512,512]{2,1,0:T(8,128)(2,1)S(1)} %get-tuple-element.20), kind=kOutput, calls=%fused_computation.8 | convolution fusion | flops 2160066560 | bytes 7864320 | tf_op jit(solution)/shard_map/zsk,zkc->zsc/dot_general | solution.py:36
  96.9 3.0 %fusion.42 = (bf16[1,1,1024,512]{3,1,2,0:T(2,128)(2,1)S(1)}, bf16[1,1,1024,512]{3,1,2,0:T(2,128)(2,1)S(1)}) fusion(bf16[1,2,1024,512]{3,1,2,0:T(2,128)(2,1)S(1)} %collective-permute-done), kind=kLoop, calls=%fused_computation.88 | loop fusion | bytes 4194304 | tf_op jit(solution)/shard_map/slice | solution.py:28
  99.9 0.3 copy.79
  100.5 4.0 %multiply_convert_fusion = bf16[1024,1024]{0,1:T(8,128)(2,1)} fusion(f32[1024,1024]{0,1:T(8,128)S(1)} %fusion.1, bf16[1,512,512]{2,1,0:T(8,128)(2,1)S(1)} %get-tuple-element.19, bf16[1,512,512]{2,1,0:T(8,128)(2,1)S(1)} %fusion.41, bf16[1,512,512]{2,1,0:T(8,128)(2,1)S(1)} %get-tuple-element.18, bf16[1,1024,512]{2,1,0:T(8,128)(2,1)S(1)} %bitcast.144, ...), kind=kOutput, calls=%fused_computation.6 | convolution fusion | flops 2163212288 | bytes 9961472 | tf_op jit(solution)/shard_map/zsk,zkc->zsc/dot_general | solution.py:36
  104.5 4.8 %copy.52 = bf16[1,1,1024,2,512]{4,3,1,0,2:T(2,128)(2,1)S(1)} copy(bf16[1,1,1024,2,512]{2,4,3,1,0:T(8,128)(2,1)} %bitcast.140) | data formatting | bytes 4194304 | tf_op jit(solution)/shard_map/reshape | solution.py:72
  109.3 58.5 %all_to_all.27 = bf16[1,1,1024,2,512]{4,3,1,0,2:T(2,128)(2,1)S(1)} all-to-all(bf16[1,1,1024,2,512]{4,3,1,0,2:T(2,128)(2,1)S(1)} %copy.52), channel_id=1, replica_groups=mesh['lines'=2,'shots'=16] {'shots'}, dimensions={2} | all-to-all | bytes 4194304 | tf_op jit(solution)/shard_map/all_to_all | solution.py:73
  167.8 14.1 %fusion = bf16[64,2,512,256]{2,3,0,1:T(8,128)(2,1)} fusion(bf16[8,2,64,2,512]{4,3,2,1,0:T(2,128)(2,1)S(1)} %bitcast.130, f32[256,8,1]{0,1,2:T(8,128)S(1)} %get-tuple-element.30, f32[256,8,1]{0,1,2:T(8,128)S(1)} %get-tuple-element.29), kind=kOutput, calls=%fused_computation.5 | convolution fusion | flops 553660416 | bytes 35667968 | tf_op jit(solution)/shard_map/phsir,pit->shrt/dot_general | solution.py:76
  181.9 44.2 %copy.55 = bf16[64,2,512,256]{3,2,1,0:T(8,128)(2,1)} copy(bf16[64,2,512,256]{2,3,0,1:T(8,128)(2,1)} %fusion) | data formatting | bytes 67108864 | tf_op jit(solution)/shard_map/convert_element_type | solution.py:79
  (26 shorter events, 1.7 us)
Async XLA Ops:
  17.5 7.5 %copy-start.3 = (s32[128,3]{0,1:T(4,128)S(1)}, s32[128,3]{0,1:T(4,128)}, u32[]{:S(2)}) copy-start(s32[128,3]{0,1:T(4,128)} %param.9) | copy-start | bytes 4612
  17.5 7.5 %copy-start.4 = (s32[128]{0:T(128)S(1)}, s32[128]{0:T(128)}, u32[]{:S(2)}) copy-start(s32[128]{0:T(128)} %param.8) | copy-start | bytes 1540
  17.5 7.5 %copy-start.2 = (f32[128,3]{0,1:T(4,128)S(1)}, f32[128,3]{0,1:T(4,128)}, u32[]{:S(2)}) copy-start(f32[128,3]{0,1:T(4,128)} %param.10) | copy-start | bytes 4612
  17.5 49.0 %all-to-all-start = ((bf16[16,2,64,512]{3,2,1,0:T(8,128)(2,1)}), bf16[16,2,64,512]{3,2,1,0:T(8,128)(2,1)S(1)}, u32[]{:S(2)}, u32[]{:S(2)}) async-start(bf16[16,2,64,512]{3,2,1,0:T(8,128)(2,1)} %bitcast.131), calls=%async_computation | async-start | bytes 4194304 | tf_op jit(solution)/shard_map/all_to_all | solution.py:56
  66.4 1.3 copy-start
  67.8 3.9 %copy-start.1 = (bf16[16,2,64,512]{3,2,1,0:T(8,128)(2,1)S(1)}, bf16[16,2,64,512]{3,2,1,0:T(8,128)(2,1)}, u32[]{:S(2)}) copy-start(bf16[16,2,64,512]{3,2,1,0:T(8,128)(2,1)} %copy-done) | copy-start | bytes 6291460
  90.3 6.6 %collective-permute-start = (bf16[1,2,1024,512]{3,1,2,0:T(2,128)(2,1)S(1)}, bf16[1,2,1024,512]{3,1,2,0:T(2,128)(2,1)S(1)}, u32[]{:S(2)}, u32[]{:S(2)}) collective-permute-start(bf16[1,2,1024,512]{3,1,2,0:T(2,128)(2,1)S(1)} %bitcast.125), channel_id=1, source_target_pairs={{0,1},{1,0},{2,3},{3,2},{4,5},{5,4},{6,7},{7,6},{8,9},{9,8},{10,11... | collective-permute-start | bytes 6291464 | tf_op jit(solution)/shard_map/ppermute | solution.py:10
where the time goes:
time: 228 us; the launch traced here: 226 us
  local copies, waits for them, and re-layouts  82.5 us (36%)
  blocking collectives  58.5 us (26%)
  waiting for transfers between devices  41.4 us (18%)
  matrix products  34.7 us (15%)
  starting transfers between devices  7.51 us (3%)
    all_to_all x1, blocking collectives, shards(): lax.all_to_all(outgoing_back, 'shots', split_axis=2, concat_axis=0, tiled...  58.5 us
    convert_element_type x1, local copies, waits for them, and re-layouts, shards(): multiples.astype(jnp.bfloat16)  44.2 us
    all_to_all x1, waiting for transfers between devices, shards(): lax.all_to_all(outgoing, 'shots', split_axis=0, concat_axis=2, tiled=True)  41.4 us
    dot_general x1, matrix products, shards(): jnp.einsum('shrt,tpc->phcsr', blocked, forward, preferred_element_type=jn...  14.2 us
    dot_general x1, matrix products, shards(): jnp.einsum('phsir,pit->shrt', returned, inverse_pair, preferred_element_t...  14.1 us
    gather x3, local copies, waits for them, and re-layouts, shards(): picked = jnp.take(own_block, neighbours[:, slot_index], axis=2)  8.18 us
    all_to_all x3, local copies, waits for them, and re-layouts, shards(): lax.all_to_all(outgoing, 'shots', split_axis=0, concat_axis=2, tiled=True)  7.59 us
    all_to_all x1, starting transfers between devices, shards(): lax.all_to_all(outgoing, 'shots', split_axis=0, concat_axis=2, tiled=True)  7.44 us
  transfers between devices with their start and end apart: 2, of which 1 were waited for; matrix products, arithmetic and copies ran while one was open for 3% of the time, Pallas kernels for 0%

commit v1 on v0

v1 whole, which is shorter than its diff:
```python
import functools
import math

import jax
import jax.numpy as jnp
from jax import lax
from jax.experimental import pallas as pl
from jax.experimental.pallas import tpu as pltpu
from jax.sharding import PartitionSpec as P

CHUNKS = 4
LANES = 128
VMEM_LIMIT = 48 * 1024 * 1024


def tables(freq_bins, sample_count):
    bin_count = freq_bins.shape[0]
    sample_ids = jnp.arange(sample_count, dtype=jnp.int32)
    phases = freq_bins[None, :] * sample_ids[:, None] % sample_count
    angles = phases.astype(jnp.float32) * (2.0 * math.pi / sample_count)
    trig_pair = jnp.stack([jnp.cos(angles), -jnp.sin(angles)], axis=-1)
    forward = (trig_pair / math.sqrt(sample_count)).astype(jnp.bfloat16)
    inverse = (trig_pair * math.sqrt(2.0 / bin_count)).astype(jnp.bfloat16)
    rows = lambda table: jnp.transpose(table, (1, 2, 0)).reshape(2 * bin_count, sample_count)
    return rows(forward), rows(inverse)


def shot_step(shot_rows):
    return math.gcd(shot_rows, 16)


def forward_body(records_ref, table_ref, out_ref, rows_ref):
    steps, halves, width, samples = records_ref.shape
    planes = table_ref.shape[0]
    flat = records_ref[...].reshape(steps * halves * width, samples)
    spectra = lax.dot_general(
        table_ref[...], flat, (((1,), (1,)), ((), ())), preferred_element_type=jnp.float32
    )
    for shot in range(steps):
        for half in range(halves):
            start = (shot * halves + half) * width
            rows_ref[half, :, shot, :] = spectra[:, start : start + width]
    for half in range(halves):
        out_ref[:, half] = (
            rows_ref[half].astype(jnp.bfloat16).reshape(planes // 2, 2, steps, width)
        )


def forward_chunk(records, table, chunk, width):
    shot_rows, halves, half, samples = records.shape
    planes = table.shape[0]
    step = shot_step(shot_rows)
    bins = planes // 2
    return pl.pallas_call(
        forward_body,
        grid=(shot_rows // step,),
        in_specs=[
            pl.BlockSpec((step, halves, width, samples), lambda i: (i, 0, chunk, 0)),
            pl.BlockSpec((planes, samples), lambda i: (0, 0)),
        ],
        out_specs=pl.BlockSpec((bins, halves, 2, step, width), lambda i: (0, 0, 0, i, 0)),
        out_shape=jax.ShapeDtypeStruct((bins, halves, 2, shot_rows, width), jnp.bfloat16),
        scratch_shapes=[pltpu.VMEM((halves, planes, step, width), jnp.float32)],
        compiler_params=pltpu.CompilerParams(vmem_limit_bytes=VMEM_LIMIT),
        cost_estimate=pl.CostEstimate(
            flops=2 * shot_rows * halves * width * samples * planes,
            bytes_accessed=2 * shot_rows * halves * width * samples,
            transcendentals=0,
        ),
        name=f"forward_{chunk}",
    )(records, table)


def inverse_body(planes_ref, table_ref, kept_ref, out_ref, rows_ref):
    bins, halves, parts, steps, width = planes_ref.shape
    planes = bins * parts
    samples = table_ref.shape[1]
    for half in range(halves):
        rows_ref[half] = (
            planes_ref[:, half].astype(jnp.float32).reshape(planes, steps, width)
        )
    for shot in range(steps):
        for half in range(halves):
            left = rows_ref[half, :, shot, :].astype(jnp.bfloat16)
            out_ref[shot, half] = lax.dot_general(
                left, table_ref[...], (((0,), (0,)), ((), ())), preferred_element_type=jnp.float32
            ).astype(jnp.bfloat16)


def inverse_first(planes_ref, table_ref, out_ref, rows_ref):
    inverse_body(planes_ref, table_ref, None, out_ref, rows_ref)


def inverse_chunk(returned, table, kept, chunk, half):
    bins, halves, parts, shot_rows, width = returned.shape
    planes, samples = table.shape
    step = shot_step(shot_rows)
    in_specs = [
        pl.BlockSpec((bins, halves, parts, step, width), lambda i: (0, 0, 0, i, 0)),
        pl.BlockSpec((planes, samples), lambda i: (0, 0)),
    ]
    operands = [returned, table]
    if kept is not None:
        in_specs.append(pl.BlockSpec(memory_space=pl.ANY))
        operands.append(kept)
    return pl.pallas_call(
        inverse_first if kept is None else inverse_body,
        grid=(shot_rows // step,),
        in_specs=in_specs,
        out_specs=pl.BlockSpec((step, halves, width, samples), lambda i: (i, 0, chunk, 0)),
        out_shape=jax.ShapeDtypeStruct((shot_rows, halves, half, samples), jnp.bfloat16),
        scratch_shapes=[pltpu.VMEM((halves, planes, step, width), jnp.float32)],
        input_output_aliases={} if kept is None else {2: 0},
        compiler_params=pltpu.CompilerParams(vmem_limit_bytes=VMEM_LIMIT),
        cost_estimate=pl.CostEstimate(
            flops=2 * shot_rows * halves * width * samples * planes,
            bytes_accessed=2 * shot_rows * halves * width * samples,
            transcendentals=0,
        ),
        name=f"inverse_{chunk}",
    )(*operands)


def fill_body(spectra_ref, pick_ref, place_ref, keep_ref, out_ref):
    devices, parts, rows, width = spectra_ref.shape
    count = pick_ref.shape[0] // 2
    for part in range(parts):
        recorded = spectra_ref[:, part].reshape(devices * rows, width)
        both = jnp.dot(pick_ref[...], recorded, preferred_element_type=jnp.float32)
        replaced = (both[:count] + both[count:]).astype(jnp.bfloat16)
        placed = jnp.dot(place_ref[...], replaced, preferred_element_type=jnp.float32)
        kept = recorded.astype(jnp.float32) * keep_ref[...]
        out_ref[part] = (placed + kept).astype(jnp.bfloat16)


def fill(spectra, pick, place, keep):
    devices, parts, rows, width = spectra.shape
    order = devices * rows
    return pl.pallas_call(
        fill_body,
        out_shape=jax.ShapeDtypeStruct((parts, order, width), jnp.bfloat16),
        compiler_params=pltpu.CompilerParams(vmem_limit_bytes=VMEM_LIMIT),
        cost_estimate=pl.CostEstimate(
            flops=8 * pick.shape[0] * order * width,
            bytes_accessed=8 * order * width,
            transcendentals=0,
        ),
        name="fill",
    )(spectra, pick, place, keep)


def product_body(member_ref, *refs, chunks, scale):
    own_refs, other_refs = refs[:chunks], refs[chunks : 2 * chunks]
    right_ref, out_ref = refs[2 * chunks], refs[2 * chunks + 1]
    devices, parts, rows, width = out_ref.shape
    order = devices * rows
    half = chunks * width
    member = member_ref[0]
    total = jnp.zeros((order, 2 * width), jnp.float32)
    for source, lefts in enumerate((own_refs, other_refs)):
        first = (member if source == 0 else 1 - member) * half
        for index in range(chunks):
            start = pl.multiple_of(first + index * width, width)
            real = right_ref[0, pl.ds(start, width), :]
            imag = right_ref[1, pl.ds(start, width), :]
            left = lefts[index]
            total += jnp.dot(
                left[0], jnp.concatenate([real, imag], axis=1), preferred_element_type=jnp.float32
            )
            total += jnp.dot(
                left[1], jnp.concatenate([-imag, real], axis=1), preferred_element_type=jnp.float32
            )
    total = total * scale
    for part in range(parts):
        out_ref[:, part] = (
            total[:, part * width : (part + 1) * width]
            .astype(jnp.bfloat16)
            .reshape(devices, rows, width)
        )


def product(member, own, other, chunk, devices):
    chunks = len(own)
    parts, order, width = own[0].shape
    scale = -1.0 / math.sqrt(order)
    vmem = pl.BlockSpec(memory_space=pltpu.VMEM)
    return pl.pallas_call(
        functools.partial(product_body, chunks=chunks, scale=scale),
        in_specs=[pl.BlockSpec(memory_space=pltpu.SMEM)] + [vmem] * (2 * chunks + 1),
        out_specs=vmem,
        out_shape=jax.ShapeDtypeStruct((devices, parts, order // devices, width), jnp.bfloat16),
        compiler_params=pltpu.CompilerParams(vmem_limit_bytes=VMEM_LIMIT),
        cost_estimate=pl.CostEstimate(
            flops=16 * order * order * width, bytes_accessed=8 * order * order, transcendentals=0
        ),
        name=f"product_{chunk}",
    )(member, *own, *other, own[chunk])


def fill_tables(missing, neighbours, weights, order):
    shots = jnp.arange(order, dtype=jnp.int32)
    pick = jnp.zeros((missing.shape[0], order), jnp.float32)
    for slot in range(neighbours.shape[1]):
        pick = pick + jnp.where(
            neighbours[:, slot][:, None] == shots[None, :], weights[:, slot][:, None], 0.0
        )
    high = pick.astype(jnp.bfloat16)
    low = (pick - high.astype(jnp.float32)).astype(jnp.bfloat16)
    found = shots[:, None] == missing[None, :]
    keep = 1.0 - jnp.any(found, axis=1, keepdims=True).astype(jnp.float32)
    return jnp.concatenate([high, low], axis=0), found.astype(jnp.bfloat16), keep


def exchange(blocks):
    return lax.all_to_all(blocks, "shots", split_axis=0, concat_axis=0, tiled=True)


def shards(records, missing, neighbours, weights, freq_bins):
    devices = lax.axis_size("shots")
    position = lax.axis_index("shots")
    shot_rows, order, samples = records.shape
    half = order // 2
    chunks = CHUNKS
    width = half // chunks
    bins = freq_bins.shape[0]
    forward, inverse = tables(freq_bins, samples)
    pick, place, keep = fill_tables(missing, neighbours, weights, order)
    split = records.reshape(shot_rows, 2, half, samples)
    own = []
    for chunk in range(chunks):
        outgoing = forward_chunk(split, forward, chunk, width)
        incoming = exchange(outgoing.reshape(devices, 2, shot_rows, width))
        own.append(fill(incoming, pick, place, keep))
    pairs = [(i, i ^ 1) for i in range(devices)]
    other = [lax.ppermute(block, "shots", pairs) for block in own]
    member = (position % 2).astype(jnp.int32).reshape(1)
    result = None
    for chunk in range(chunks):
        predicted = product(member, own, other, chunk, devices)
        returned = exchange(predicted).reshape(bins, 2, 2, shot_rows, width)
        result = inverse_chunk(returned, inverse, result, chunk, half)
    return result.reshape(shot_rows, order, samples)


def solution(mesh):
    return jax.shard_map(
        shards,
        mesh=mesh,
        in_specs=(
            P(("lines", "shots"), None, None),
            P("lines"),
            P("lines", None),
            P("lines", None),
            P(),
        ),
        out_specs=P(("lines", "shots"), None, None),
        check_vma=False,
    )
```

time: 228 us -> 173 us (0.76)
  local copies, waits for them, and re-layouts: 82.5 us -> 2.37 us
  Pallas kernels: 0 us -> 68.4 us
  blocking collectives: 58.5 us -> 0 us
  matrix products: 34.7 us -> 0 us
  starting transfers between devices: 7.51 us -> 39.6 us
  waiting for transfers between devices: 41.4 us -> 59.7 us
    pallas_call x0 -> x16, Pallas kernels: none -> 68.4 us  [the longest x4 24.9 us: forward_chunk(): pl.pallas_call(forward_body, grid=(shot_rows // step,), in_specs=[pl.Bloc...]
    all_to_all x1 -> x0, blocking collectives: 58.5 us -> none  [shards(): lax.all_to_all(outgoing_back, 'shots', split_axis=2, concat_axis=0, tiled...]
    convert_element_type x3 -> x0, local copies, waits for them, and re-layouts: 47 us -> none  [the longest x1 44.2 us: shards(): multiples.astype(jnp.bfloat16)]
    dot_general x4 -> x0, matrix products: 34.7 us -> none  [the longest x1 14.2 us: shards(): jnp.einsum('shrt,tpc->phcsr', blocked, forward, preferred_element_type=jn...]
    all_to_all x1 -> x8, starting transfers between devices: 7.44 us -> 38.4 us  [exchange(): lax.all_to_all(blocks, 'shots', split_axis=0, concat_axis=0, tiled=True)]
    all_to_all x1 -> x8, waiting for transfers between devices: 41.4 us -> 58.2 us  [exchange(): lax.all_to_all(blocks, 'shots', split_axis=0, concat_axis=0, tiled=True)]
    gather x3 -> x0, local copies, waits for them, and re-layouts: 8.18 us -> none  [shards(): picked = jnp.take(own_block, neighbours[:, slot_index], axis=2)]
    all_to_all x3 -> x0, local copies, waits for them, and re-layouts: 7.59 us -> none  [shards(): lax.all_to_all(outgoing, 'shots', split_axis=0, concat_axis=2, tiled=True)]
  transfers between devices with their start and end apart: 2 -> 12, of which waited for: 1 -> 8; matrix products, arithmetic and copies ran while one was open for 3% -> 0% of each run, Pallas kernels for 0% -> 30%
where the time goes in v1:
time: 173 us; the launch traced here: 172 us
  Pallas kernels  68.4 us (40%)
  waiting for transfers between devices  59.7 us (35%)
  starting transfers between devices  39.6 us (23%)
  local copies, waits for them, and re-layouts  2.37 us (1%)
    all_to_all x8, waiting for transfers between devices, exchange(): lax.all_to_all(blocks, 'shots', split_axis=0, concat_axis=0, tiled=True)  58.2 us
    all_to_all x8, starting transfers between devices, exchange(): lax.all_to_all(blocks, 'shots', split_axis=0, concat_axis=0, tiled=True)  38.4 us
    pallas_call x4, Pallas kernels, forward_chunk(): pl.pallas_call(forward_body, grid=(shot_rows // step,), in_specs=[pl.Bloc...  24.9 us
    pallas_call x4, Pallas kernels, inverse_chunk(): pl.pallas_call(inverse_first if kept is None else inverse_body, grid=(sho...  20.1 us
    pallas_call x4, Pallas kernels, product(): pl.pallas_call(functools.partial(product_body, chunks=chunks, scale=scale...  18.9 us
    pallas_call x4, Pallas kernels, fill(): pl.pallas_call(fill_body, out_shape=jax.ShapeDtypeStruct((parts, order, w...  4.52 us
  transfers between devices with their start and end apart: 12, of which 8 were waited for; matrix products, arithmetic and copies ran while one was open for 0% of the time, Pallas kernels for 30%

profile of v1, /device:TPU:1, one launch (start us, length us, event | category | flops | bytes accessed | tf_op | source)
XLA Modules:
  0.0 171.5 jit_solution(3927951623989978488)
XLA Ops:
  0.8 6.2 %forward_2.1 = bf16[8,2,2,64,128]{4,3,2,1,0:T(8,128)(2,1)} custom-call(bf16[64,2,512,256]{3,2,1,0:T(8,128)(2,1)} %bitcast.32, bf16[16,256]{1,0:T(8,128)(2,1)S(1)} %reshape.153.table_ref), custom_call_target="tpu_custom_call" | custom-call | flops 134217728 | bytes 8388608 | tf_op jit(solution)/shard_map/forward_2/pallas_call | solution.py:54
  7.0 7.3 %all-to-all-start.2 = ((bf16[16,2,64,128]{3,2,1,0:T(8,128)(2,1)}), bf16[16,2,64,128]{3,2,1,0:T(8,128)(2,1)S(1)}, u32[]{:S(2)}, u32[]{:S(2)}) async-start(bf16[16,2,64,128]{3,2,1,0:T(8,128)(2,1)} %bitcast.12), calls=%async_computation.2 | async-start | bytes 1048576 | tf_op jit(solution)/shard_map/all_to_all | solution.py:215
  14.4 6.2 %forward_1.1 = bf16[8,2,2,64,128]{4,3,2,1,0:T(8,128)(2,1)} custom-call(bf16[64,2,512,256]{3,2,1,0:T(8,128)(2,1)} %bitcast.33, bf16[16,256]{1,0:T(8,128)(2,1)S(1)} %reshape.153.table_ref), custom_call_target="tpu_custom_call" | custom-call | flops 134217728 | bytes 8388608 | tf_op jit(solution)/shard_map/forward_1/pallas_call | solution.py:54
  20.6 7.8 %all-to-all-done.2.spectra_ref = bf16[16,2,64,128]{3,2,1,0:T(8,128)(2,1)S(1)} async-done(((bf16[16,2,64,128]{3,2,1,0:T(8,128)(2,1)}), bf16[16,2,64,128]{3,2,1,0:T(8,128)(2,1)S(1)}, u32[]{:S(2)}, u32[]{:S(2)}) %all-to-all-start.2) | async-done | bytes 524320 | tf_op jit(solution)/shard_map/all_to_all | solution.py:215
  28.4 4.4 %all-to-all-start.1 = ((bf16[16,2,64,128]{3,2,1,0:T(8,128)(2,1)}), bf16[16,2,64,128]{3,2,1,0:T(8,128)(2,1)S(1)}, u32[]{:S(2)}, u32[]{:S(2)}) async-start(bf16[16,2,64,128]{3,2,1,0:T(8,128)(2,1)} %bitcast.11), calls=%async_computation.1 | async-start | bytes 1048576 | tf_op jit(solution)/shard_map/all_to_all | solution.py:215
  32.8 6.2 %forward_0.1 = bf16[8,2,2,64,128]{4,3,2,1,0:T(8,128)(2,1)} custom-call(bf16[64,2,512,256]{3,2,1,0:T(8,128)(2,1)} %bitcast.34, bf16[16,256]{1,0:T(8,128)(2,1)S(1)} %reshape.153.table_ref), custom_call_target="tpu_custom_call" | custom-call | flops 134217728 | bytes 8388608 | tf_op jit(solution)/shard_map/forward_0/pallas_call | solution.py:54
  39.1 7.8 %all-to-all-done.1.spectra_ref = bf16[16,2,64,128]{3,2,1,0:T(8,128)(2,1)S(1)} async-done(((bf16[16,2,64,128]{3,2,1,0:T(8,128)(2,1)}), bf16[16,2,64,128]{3,2,1,0:T(8,128)(2,1)S(1)}, u32[]{:S(2)}, u32[]{:S(2)}) %all-to-all-start.1) | async-done | bytes 524320 | tf_op jit(solution)/shard_map/all_to_all | solution.py:215
  51.2 6.2 %forward_3.1 = bf16[8,2,2,64,128]{4,3,2,1,0:T(8,128)(2,1)} custom-call(bf16[64,2,512,256]{3,2,1,0:T(8,128)(2,1)} %bitcast.35, bf16[16,256]{1,0:T(8,128)(2,1)S(1)} %reshape.153.table_ref), custom_call_target="tpu_custom_call" | custom-call | flops 134217728 | bytes 8388608 | tf_op jit(solution)/shard_map/forward_3/pallas_call | solution.py:54
  57.7 7.5 %all-to-all-done.spectra_ref = bf16[16,2,64,128]{3,2,1,0:T(8,128)(2,1)S(1)} async-done(((bf16[16,2,64,128]{3,2,1,0:T(8,128)(2,1)}), bf16[16,2,64,128]{3,2,1,0:T(8,128)(2,1)S(1)}, u32[]{:S(2)}, u32[]{:S(2)}) %all-to-all-start) | async-done | bytes 524320 | tf_op jit(solution)/shard_map/all_to_all | solution.py:215
  74.6 9.1 %all-to-all-done.3.spectra_ref = bf16[16,2,64,128]{3,2,1,0:T(8,128)(2,1)S(1)} async-done(((bf16[16,2,64,128]{3,2,1,0:T(8,128)(2,1)}), bf16[16,2,64,128]{3,2,1,0:T(8,128)(2,1)S(1)}, u32[]{:S(2)}, u32[]{:S(2)}) %all-to-all-start.3) | async-done | bytes 524320 | tf_op jit(solution)/shard_map/all_to_all | solution.py:215
  86.6 5.0 %product_0.1 = bf16[16,2,64,128]{3,2,1,0:T(8,128)(2,1)} custom-call(s32[1]{0:T(128)} %bitcast.member_ref, bf16[2,1024,128]{2,1,0:T(8,128)(2,1)} %fill.4.refs_0_.refs_8_, bf16[2,1024,128]{2,1,0:T(8,128)(2,1)S(1)} %fill.5.refs_1_.refs_8_, bf16[2,1024,128]{2,1,0:T(8,128)(2,1)S(1)} %fill.6.refs_2_.refs_8_, bf16[2,1024,128]{2,1,0:T(8,128)(2,1)S(1)} %fill.7.refs_3_.refs_8_, ...), custom_call_target="tpu_custom_call" | custom-call | flops 2147483648 | bytes 8388608 | tf_op jit(solution)/shard_map/product_0/pallas_call | solution.py:187
  91.6 4.5 %all-to-all-start.7 = ((bf16[16,2,64,128]{3,2,1,0:T(8,128)(2,1)}), bf16[16,2,64,128]{3,2,1,0:T(8,128)(2,1)S(1)}, u32[]{:S(2)}, u32[]{:S(2)}) async-start(bf16[16,2,64,128]{3,2,1,0:T(8,128)(2,1)} %product_0.1), calls=%async_computation.7 | async-start | bytes 1048576 | tf_op jit(solution)/shard_map/all_to_all | solution.py:215
  96.1 4.6 %product_1.1 = bf16[16,2,64,128]{3,2,1,0:T(8,128)(2,1)} custom-call(s32[1]{0:T(128)} %bitcast.member_ref, bf16[2,1024,128]{2,1,0:T(8,128)(2,1)} %fill.4.refs_0_.refs_8_, bf16[2,1024,128]{2,1,0:T(8,128)(2,1)S(1)} %fill.5.refs_1_.refs_8_, bf16[2,1024,128]{2,1,0:T(8,128)(2,1)S(1)} %fill.6.refs_2_.refs_8_, bf16[2,1024,128]{2,1,0:T(8,128)(2,1)S(1)} %fill.7.refs_3_.refs_8_, ...), custom_call_target="tpu_custom_call" | custom-call | flops 2147483648 | bytes 8388608 | tf_op jit(solution)/shard_map/product_1/pallas_call | solution.py:187
  100.7 9.4 %all-to-all-done.7 = bf16[16,2,64,128]{3,2,1,0:T(8,128)(2,1)S(1)} async-done(((bf16[16,2,64,128]{3,2,1,0:T(8,128)(2,1)}), bf16[16,2,64,128]{3,2,1,0:T(8,128)(2,1)S(1)}, u32[]{:S(2)}, u32[]{:S(2)}) %all-to-all-start.7) | async-done | bytes 524320 | tf_op jit(solution)/shard_map/all_to_all | solution.py:215
  110.1 4.4 %all-to-all-start.6 = ((bf16[16,2,64,128]{3,2,1,0:T(8,128)(2,1)}), bf16[16,2,64,128]{3,2,1,0:T(8,128)(2,1)S(1)}, u32[]{:S(2)}, u32[]{:S(2)}) async-start(bf16[16,2,64,128]{3,2,1,0:T(8,128)(2,1)} %product_1.1), calls=%async_computation.6 | async-start | bytes 1048576 | tf_op jit(solution)/shard_map/all_to_all | solution.py:215
  114.5 4.6 %product_2.1 = bf16[16,2,64,128]{3,2,1,0:T(8,128)(2,1)} custom-call(s32[1]{0:T(128)} %bitcast.member_ref, bf16[2,1024,128]{2,1,0:T(8,128)(2,1)} %fill.4.refs_0_.refs_8_, bf16[2,1024,128]{2,1,0:T(8,128)(2,1)S(1)} %fill.5.refs_1_.refs_8_, bf16[2,1024,128]{2,1,0:T(8,128)(2,1)S(1)} %fill.6.refs_2_.refs_8_, bf16[2,1024,128]{2,1,0:T(8,128)(2,1)S(1)} %fill.7.refs_3_.refs_8_, ...), custom_call_target="tpu_custom_call" | custom-call | flops 2147483648 | bytes 8388608 | tf_op jit(solution)/shard_map/product_2/pallas_call | solution.py:187
  119.1 9.4 %all-to-all-done.6 = bf16[16,2,64,128]{3,2,1,0:T(8,128)(2,1)S(1)} async-done(((bf16[16,2,64,128]{3,2,1,0:T(8,128)(2,1)}), bf16[16,2,64,128]{3,2,1,0:T(8,128)(2,1)S(1)}, u32[]{:S(2)}, u32[]{:S(2)}) %all-to-all-start.6) | async-done | bytes 524320 | tf_op jit(solution)/shard_map/all_to_all | solution.py:215
  128.5 4.4 %all-to-all-start.5 = ((bf16[16,2,64,128]{3,2,1,0:T(8,128)(2,1)}), bf16[16,2,64,128]{3,2,1,0:T(8,128)(2,1)S(1)}, u32[]{:S(2)}, u32[]{:S(2)}) async-start(bf16[16,2,64,128]{3,2,1,0:T(8,128)(2,1)} %product_2.1), calls=%async_computation.5 | async-start | bytes 1048576 | tf_op jit(solution)/shard_map/all_to_all | solution.py:215
  135.0 4.6 %product_3.1 = bf16[16,2,64,128]{3,2,1,0:T(8,128)(2,1)} custom-call(s32[1]{0:T(128)} %bitcast.member_ref, bf16[2,1024,128]{2,1,0:T(8,128)(2,1)} %fill.4.refs_0_.refs_8_, bf16[2,1024,128]{2,1,0:T(8,128)(2,1)S(1)} %fill.5.refs_1_.refs_8_, bf16[2,1024,128]{2,1,0:T(8,128)(2,1)S(1)} %fill.6.refs_2_.refs_8_, bf16[2,1024,128]{2,1,0:T(8,128)(2,1)S(1)} %copy-done.1, ...), custom_call_target="tpu_custom_call" | custom-call | flops 2147483648 | bytes 8388608 | tf_op jit(solution)/shard_map/product_3/pallas_call | solution.py:187
  139.7 7.3 %all-to-all-done.5 = bf16[16,2,64,128]{3,2,1,0:T(8,128)(2,1)S(1)} async-done(((bf16[16,2,64,128]{3,2,1,0:T(8,128)(2,1)}), bf16[16,2,64,128]{3,2,1,0:T(8,128)(2,1)S(1)}, u32[]{:S(2)}, u32[]{:S(2)}) %all-to-all-start.5) | async-done | bytes 524320 | tf_op jit(solution)/shard_map/all_to_all | solution.py:215
  151.4 5.0 %inverse_0.1.kept_ref = bf16[64,2,512,256]{3,2,1,0:T(8,128)(2,1)} custom-call(bf16[8,2,2,64,128]{4,3,2,1,0:T(8,128)(2,1)S(1)} %bitcast.28, bf16[16,256]{1,0:T(8,128)(2,1)S(1)} %reshape.159.table_ref), custom_call_target="tpu_custom_call" | custom-call | flops 134217728 | bytes 8388608 | tf_op jit(solution)/shard_map/inverse_0/pallas_call | solution.py:106
  156.5 5.0 %inverse_1.1.kept_ref = bf16[64,2,512,256]{3,2,1,0:T(8,128)(2,1)} custom-call(bf16[8,2,2,64,128]{4,3,2,1,0:T(8,128)(2,1)S(1)} %bitcast.29, bf16[16,256]{1,0:T(8,128)(2,1)S(1)} %reshape.159.table_ref, bf16[64,2,512,256]{3,2,1,0:T(8,128)(2,1)} %inverse_0.1.kept_ref), custom_call_target="tpu_custom_call", output_to_operand_aliasing={{}: (2, {})} | custom-call | flops 134217728 | bytes 8388608 | tf_op jit(solution)/shard_map/inverse_1/pallas_call | solution.py:106
  161.5 5.0 %inverse_2.1.kept_ref = bf16[64,2,512,256]{3,2,1,0:T(8,128)(2,1)} custom-call(bf16[8,2,2,64,128]{4,3,2,1,0:T(8,128)(2,1)S(1)} %bitcast.30, bf16[16,256]{1,0:T(8,128)(2,1)S(1)} %reshape.159.table_ref, bf16[64,2,512,256]{3,2,1,0:T(8,128)(2,1)} %inverse_1.1.kept_ref), custom_call_target="tpu_custom_call", output_to_operand_aliasing={{}: (2, {})} | custom-call | flops 134217728 | bytes 8388608 | tf_op jit(solution)/shard_map/inverse_2/pallas_call | solution.py:106
  166.5 5.0 %inverse_3.1 = bf16[64,2,512,256]{3,2,1,0:T(8,128)(2,1)} custom-call(bf16[8,2,2,64,128]{4,3,2,1,0:T(8,128)(2,1)S(1)} %bitcast.31, bf16[16,256]{1,0:T(8,128)(2,1)S(1)} %reshape.159.table_ref, bf16[64,2,512,256]{3,2,1,0:T(8,128)(2,1)} %inverse_2.1.kept_ref), custom_call_target="tpu_custom_call", output_to_operand_aliasing={{}: (2, {})} | custom-call | flops 134217728 | bytes 8388608 | tf_op jit(solution)/shard_map/inverse_3/pallas_call | solution.py:106
  (43 shorter events, 24.2 us)
Async XLA Ops:
  7.0 21.3 %all-to-all-start.2 = ((bf16[16,2,64,128]{3,2,1,0:T(8,128)(2,1)}), bf16[16,2,64,128]{3,2,1,0:T(8,128)(2,1)S(1)}, u32[]{:S(2)}, u32[]{:S(2)}) async-start(bf16[16,2,64,128]{3,2,1,0:T(8,128)(2,1)} %bitcast.12), calls=%async_computation.2 | async-start | bytes 1048576 | tf_op jit(solution)/shard_map/all_to_all | solution.py:215
  28.4 18.4 %all-to-all-start.1 = ((bf16[16,2,64,128]{3,2,1,0:T(8,128)(2,1)}), bf16[16,2,64,128]{3,2,1,0:T(8,128)(2,1)S(1)}, u32[]{:S(2)}, u32[]{:S(2)}) async-start(bf16[16,2,64,128]{3,2,1,0:T(8,128)(2,1)} %bitcast.11), calls=%async_computation.1 | async-start | bytes 1048576 | tf_op jit(solution)/shard_map/all_to_all | solution.py:215
  32.8 24.7 %copy-start.6 = (s32[128]{0:T(128)S(1)}, s32[128]{0:T(128)}, u32[]{:S(2)}) copy-start(s32[128]{0:T(128)} %param.6) | copy-start | bytes 1540
  32.8 37.1 %copy-start.4 = (s32[128,3]{0,1:T(4,128)S(1)}, s32[128,3]{0,1:T(4,128)}, u32[]{:S(2)}) copy-start(s32[128,3]{0,1:T(4,128)} %param.7) | copy-start | bytes 4612
  32.8 37.1 %copy-start.5 = (f32[128,3]{0,1:T(4,128)S(1)}, f32[128,3]{0,1:T(4,128)}, u32[]{:S(2)}) copy-start(f32[128,3]{0,1:T(4,128)} %param.8) | copy-start | bytes 4612
  46.8 18.4 %all-to-all-start = ((bf16[16,2,64,128]{3,2,1,0:T(8,128)(2,1)}), bf16[16,2,64,128]{3,2,1,0:T(8,128)(2,1)S(1)}, u32[]{:S(2)}, u32[]{:S(2)}) async-start(bf16[16,2,64,128]{3,2,1,0:T(8,128)(2,1)} %bitcast.3), calls=%async_computation | async-start | bytes 1048576 | tf_op jit(solution)/shard_map/all_to_all | solution.py:215
  65.2 18.4 %all-to-all-start.3 = ((bf16[16,2,64,128]{3,2,1,0:T(8,128)(2,1)}), bf16[16,2,64,128]{3,2,1,0:T(8,128)(2,1)S(1)}, u32[]{:S(2)}, u32[]{:S(2)}) async-start(bf16[16,2,64,128]{3,2,1,0:T(8,128)(2,1)} %bitcast.13), calls=%async_computation.3 | async-start | bytes 1048576 | tf_op jit(solution)/shard_map/all_to_all | solution.py:215
  72.0 13.1 %collective-permute-start = (bf16[2,1024,128]{2,1,0:T(8,128)(2,1)}, bf16[2,1024,128]{2,1,0:T(8,128)(2,1)}, u32[]{:S(2)}, u32[]{:S(2)}) collective-permute-start(bf16[2,1024,128]{2,1,0:T(8,128)(2,1)} %fill.4.refs_0_.refs_8_), channel_id=1, source_target_pairs={{0,1},{1,0},{2,3},{3,2},{4,5},{5,4},{6,7},{7,6},{8,9},{9,8},{10,11... | collective-permute-start | bytes 1572872 | tf_op jit(solution)/shard_map/ppermute | solution.py:235
  73.1 12.0 %collective-permute-start.1 = (bf16[2,1024,128]{2,1,0:T(8,128)(2,1)S(1)}, bf16[2,1024,128]{2,1,0:T(8,128)(2,1)}, u32[]{:S(2)}, u32[]{:S(2)}) collective-permute-start(bf16[2,1024,128]{2,1,0:T(8,128)(2,1)S(1)} %fill.5.refs_1_.refs_8_), channel_id=1, source_target_pairs={{0,1},{1,0},{2,3},{3,2},{4,5},{5,4},{6,7},{7,6},{8,9},{9,8},{10,11... | collective-permute-start | bytes 1572872 | tf_op jit(solution)/shard_map/ppermute | solution.py:235
  74.5 10.6 %collective-permute-start.2 = (bf16[2,1024,128]{2,1,0:T(8,128)(2,1)S(1)}, bf16[2,1024,128]{2,1,0:T(8,128)(2,1)}, u32[]{:S(2)}, u32[]{:S(2)}) collective-permute-start(bf16[2,1024,128]{2,1,0:T(8,128)(2,1)S(1)} %fill.6.refs_2_.refs_8_), channel_id=1, source_target_pairs={{0,1},{1,0},{2,3},{3,2},{4,5},{5,4},{6,7},{7,6},{8,9},{9,8},{10,11... | collective-permute-start | bytes 1572872 | tf_op jit(solution)/shard_map/ppermute | solution.py:235
  84.6 43.9 %copy-start = (bf16[2,1024,128]{2,1,0:T(8,128)(2,1)}, bf16[2,1024,128]{2,1,0:T(8,128)(2,1)S(1)}, u32[]{:S(2)}) copy-start(bf16[2,1024,128]{2,1,0:T(8,128)(2,1)S(1)} %fill.7.refs_3_.refs_8_) | copy-start | bytes 1572868
  84.6 2.0 %collective-permute-start.3 = (bf16[2,1024,128]{2,1,0:T(8,128)(2,1)S(1)}, bf16[2,1024,128]{2,1,0:T(8,128)(2,1)S(1)}, u32[]{:S(2)}, u32[]{:S(2)}) collective-permute-start(bf16[2,1024,128]{2,1,0:T(8,128)(2,1)S(1)} %fill.7.refs_3_.refs_8_), channel_id=1, source_target_pairs={{0,1},{1,0},{2,3},{3,2},{4,5},{5,4},{6,7},{7,6},{8,9},{9,8},{10,11... | collective-permute-start | bytes 1572872 | tf_op jit(solution)/shard_map/ppermute | solution.py:235
  86.6 41.9 %copy-start.2 = (bf16[2,1024,128]{2,1,0:T(8,128)(2,1)}, bf16[2,1024,128]{2,1,0:T(8,128)(2,1)S(1)}, u32[]{:S(2)}) copy-start(bf16[2,1024,128]{2,1,0:T(8,128)(2,1)S(1)} %collective-permute-done.3.refs_7_) | copy-start | bytes 1572868
  91.6 18.5 %all-to-all-start.7 = ((bf16[16,2,64,128]{3,2,1,0:T(8,128)(2,1)}), bf16[16,2,64,128]{3,2,1,0:T(8,128)(2,1)S(1)}, u32[]{:S(2)}, u32[]{:S(2)}) async-start(bf16[16,2,64,128]{3,2,1,0:T(8,128)(2,1)} %product_0.1), calls=%async_computation.7 | async-start | bytes 1048576 | tf_op jit(solution)/shard_map/all_to_all | solution.py:215
  110.1 18.4 %all-to-all-start.6 = ((bf16[16,2,64,128]{3,2,1,0:T(8,128)(2,1)}), bf16[16,2,64,128]{3,2,1,0:T(8,128)(2,1)S(1)}, u32[]{:S(2)}, u32[]{:S(2)}) async-start(bf16[16,2,64,128]{3,2,1,0:T(8,128)(2,1)} %product_1.1), calls=%async_computation.6 | async-start | bytes 1048576 | tf_op jit(solution)/shard_map/all_to_all | solution.py:215
  128.5 18.4 %all-to-all-start.5 = ((bf16[16,2,64,128]{3,2,1,0:T(8,128)(2,1)}), bf16[16,2,64,128]{3,2,1,0:T(8,128)(2,1)S(1)}, u32[]{:S(2)}, u32[]{:S(2)}) async-start(bf16[16,2,64,128]{3,2,1,0:T(8,128)(2,1)} %product_2.1), calls=%async_computation.5 | async-start | bytes 1048576 | tf_op jit(solution)/shard_map/all_to_all | solution.py:215
  132.9 1.0 copy-start.1
  134.0 1.0 copy-start.3
  147.0 19.6 %all-to-all-start.4 = ((bf16[16,2,64,128]{3,2,1,0:T(8,128)(2,1)}), bf16[16,2,64,128]{3,2,1,0:T(8,128)(2,1)S(1)}, u32[]{:S(2)}, u32[]{:S(2)}) async-start(bf16[16,2,64,128]{3,2,1,0:T(8,128)(2,1)} %product_3.1), calls=%async_computation.4 | async-start | bytes 1048576 | tf_op jit(solution)/shard_map/all_to_all | solution.py:215

commit v2 on v0

v2 whole, which is shorter than its diff:
```python
import functools
import math

import jax
import jax.numpy as jnp
from jax import lax
from jax.experimental import pallas as pl
from jax.experimental.pallas import tpu as pltpu
from jax.sharding import PartitionSpec as P


SHARES = (1, 2, 2, 2, 1)
STREAM_VMEM = 36 * 1024 * 1024
VMEM_LIMIT = 16 * 1024 * 1024


def tables(freq_bins, sample_count):
    bin_count = freq_bins.shape[0]
    sample_ids = jnp.arange(sample_count, dtype=jnp.int32)
    phases = freq_bins[None, :] * sample_ids[:, None] % sample_count
    angles = phases.astype(jnp.float32) * (2.0 * math.pi / sample_count)
    trig_pair = jnp.stack([jnp.cos(angles), -jnp.sin(angles)], axis=-1)
    forward = (trig_pair / math.sqrt(sample_count)).astype(jnp.bfloat16)
    inverse = (trig_pair * math.sqrt(2.0 / bin_count)).astype(jnp.bfloat16)
    rows = lambda table: jnp.transpose(table, (1, 2, 0)).reshape(2 * bin_count, sample_count)
    return rows(forward), rows(inverse)


def shot_step(shot_rows):
    return math.gcd(shot_rows, 16)


def forward_body(records_ref, table_ref, out_ref, rows_ref):
    steps, width, samples = records_ref.shape
    planes = table_ref.shape[0]
    flat = records_ref[...].reshape(steps * width, samples)
    spectra = lax.dot_general(
        table_ref[...], flat, (((1,), (1,)), ((), ())), preferred_element_type=jnp.float32
    )
    for shot in range(steps):
        rows_ref[:, shot, :] = spectra[:, shot * width : (shot + 1) * width]
    out_ref[...] = rows_ref[...].astype(jnp.bfloat16).reshape(planes // 2, 2, steps, width)


def forward_chunk(records, table, first, width):
    shot_rows, _, samples = records.shape
    planes = table.shape[0]
    step = shot_step(shot_rows)
    return pl.pallas_call(
        forward_body,
        grid=(shot_rows // step,),
        in_specs=[
            pl.BlockSpec(
                (pl.Element(step), pl.Element(width), pl.Element(samples)),
                lambda i: (i * step, first, 0),
            ),
            pl.BlockSpec((planes, samples), lambda i: (0, 0)),
        ],
        out_specs=pl.BlockSpec((planes // 2, 2, step, width), lambda i: (0, 0, i, 0)),
        out_shape=jax.ShapeDtypeStruct((planes // 2, 2, shot_rows, width), jnp.bfloat16),
        scratch_shapes=[pltpu.VMEM((planes, step, width), jnp.float32)],
        compiler_params=pltpu.CompilerParams(vmem_limit_bytes=STREAM_VMEM),
        cost_estimate=pl.CostEstimate(
            flops=2 * shot_rows * width * samples * planes,
            bytes_accessed=2 * shot_rows * width * samples,
            transcendentals=0,
        ),
    )(records, table)


def inverse_body(planes_ref, table_ref, *refs):
    out_ref, rows_ref = refs[-2:]
    bins, parts, steps, width = planes_ref.shape
    rows_ref[...] = planes_ref[...].astype(jnp.float32).reshape(bins * parts, steps, width)
    for shot in range(steps):
        left = rows_ref[:, shot, :].astype(jnp.bfloat16)
        out_ref[shot] = lax.dot_general(
            left, table_ref[...], (((0,), (0,)), ((), ())), preferred_element_type=jnp.float32
        ).astype(jnp.bfloat16)


def inverse_chunk(returned, table, kept, first, order):
    bins, parts, shot_rows, width = returned.shape
    planes, samples = table.shape
    step = shot_step(shot_rows)
    in_specs = [
        pl.BlockSpec((bins, parts, step, width), lambda i: (0, 0, i, 0)),
        pl.BlockSpec((planes, samples), lambda i: (0, 0)),
    ]
    operands = [returned, table]
    if kept is not None:
        in_specs.append(pl.BlockSpec(memory_space=pl.ANY))
        operands.append(kept)
    return pl.pallas_call(
        inverse_body,
        grid=(shot_rows // step,),
        in_specs=in_specs,
        out_specs=pl.BlockSpec(
            (pl.Element(step), pl.Element(width), pl.Element(samples)),
            lambda i: (i * step, first, 0),
        ),
        out_shape=jax.ShapeDtypeStruct((shot_rows, order, samples), jnp.bfloat16),
        scratch_shapes=[pltpu.VMEM((planes, step, width), jnp.float32)],
        input_output_aliases={} if kept is None else {2: 0},
        compiler_params=pltpu.CompilerParams(vmem_limit_bytes=STREAM_VMEM),
        cost_estimate=pl.CostEstimate(
            flops=2 * shot_rows * width * samples * planes,
            bytes_accessed=2 * shot_rows * width * samples,
            transcendentals=0,
        ),
    )(*operands)


def filled_rows(recorded, edge, pick, place, keep):
    count = pick.shape[0] // 2
    known = jnp.concatenate([recorded, edge], axis=0)
    both = jnp.dot(pick, known, preferred_element_type=jnp.float32)
    replaced = (both[:count] + both[count:]).astype(jnp.bfloat16)
    placed = jnp.dot(place, replaced, preferred_element_type=jnp.float32)
    return (placed + recorded.astype(jnp.float32) * keep).astype(jnp.bfloat16)


def fill_body(*refs, firsts):
    own_refs = refs[: len(firsts)]
    edge_ref, pick_ref, place_ref, keep_ref, out_ref = refs[len(firsts) :]
    order = edge_ref.shape[2]
    for own_ref, first in zip(own_refs, firsts):
        sources, parts, rows, width = own_ref.shape
        for part in range(parts):
            recorded = own_ref[:, part].reshape(sources * rows, width)
            edge = edge_ref[part, :, first : first + width]
            start = part * order + first
            out_ref[:, start : start + width] = filled_rows(
                recorded, edge, pick_ref[...], place_ref[...], keep_ref[...]
            )


def fill_own(own, edge, tables_own, firsts):
    sources, parts, rows, _ = own[0].shape
    order = edge.shape[2]
    return pl.pallas_call(
        functools.partial(fill_body, firsts=firsts),
        out_shape=jax.ShapeDtypeStruct((sources * rows, parts * order), jnp.bfloat16),
        compiler_params=pltpu.CompilerParams(vmem_limit_bytes=VMEM_LIMIT),
        cost_estimate=pl.CostEstimate(
            flops=8 * tables_own[0].shape[0] * sources * rows * order,
            bytes_accessed=8 * sources * rows * order,
            transcendentals=0,
        ),
        name="fill_own",
    )(*own, edge, *tables_own)


def product_body(
    side_ref, other_ref, edge_ref, pick_ref, place_ref, keep_ref, left_ref, out_ref, right_ref, *, first, scale
):
    sources, parts, rows, width = other_ref.shape
    half = sources * rows
    order = left_ref.shape[1] // 2
    side = side_ref[0]
    other = [
        filled_rows(
            other_ref[:, part].reshape(half, width),
            edge_ref[part],
            pick_ref[...],
            place_ref[...],
            keep_ref[...],
        )
        for part in range(parts)
    ]
    own = [left_ref[:, part * order + first : part * order + first + width] for part in range(parts)]
    for real, imag, at in ((own[0], own[1], side), (other[0], other[1], 1 - side)):
        start = pl.multiple_of(at * half, half)
        right_ref[pl.ds(start, half), :width] = real
        right_ref[pl.ds(start, half), width:] = imag
        start = pl.multiple_of(at * half + order, half)
        right_ref[pl.ds(start, half), :width] = -imag
        right_ref[pl.ds(start, half), width:] = real
    total = jnp.dot(left_ref[...], right_ref[...], preferred_element_type=jnp.float32) * scale
    for part in range(parts):
        out_ref[:, part] = (
            total[:, part * width : (part + 1) * width]
            .astype(jnp.bfloat16)
            .reshape(sources, rows, width)
        )


def product(side, other, edge, tables_other, left, first):
    sources, parts, rows, width = other.shape
    half = sources * rows
    order = left.shape[1] // parts
    vmem = pl.BlockSpec(memory_space=pltpu.VMEM)
    return pl.pallas_call(
        functools.partial(product_body, first=first, scale=-1.0 / math.sqrt(order)),
        in_specs=[pl.BlockSpec(memory_space=pltpu.SMEM)] + [vmem] * 6,
        out_specs=vmem,
        out_shape=jax.ShapeDtypeStruct((sources, parts, rows, width), jnp.bfloat16),
        scratch_shapes=[pltpu.VMEM((2 * order, 2 * width), jnp.bfloat16)],
        compiler_params=pltpu.CompilerParams(vmem_limit_bytes=VMEM_LIMIT),
        cost_estimate=pl.CostEstimate(
            flops=16 * half * order * width, bytes_accessed=8 * order * half, transcendentals=0
        ),
    )(side, other, edge, *tables_other, left)


def pick_rows(missing, neighbours, weights, shots):
    pick = jnp.zeros((missing.shape[0], shots.shape[0]), jnp.float32)
    for slot in range(neighbours.shape[1]):
        pick = pick + jnp.where(
            neighbours[:, slot][:, None] == shots[None, :], weights[:, slot][:, None], 0.0
        )
    high = lax.reduce_precision(pick, 8, 7)
    return jnp.concatenate([high, pick - high], axis=0).astype(jnp.bfloat16)


def fill_tables(missing, neighbours, weights, start, half, edge_start, edge_rows):
    inside = start + jnp.arange(half, dtype=jnp.int32)
    beyond = edge_start + jnp.arange(edge_rows, dtype=jnp.int32)
    pick = pick_rows(missing, neighbours, weights, jnp.concatenate([inside, beyond]))
    found = inside[:, None] == missing[None, :]
    keep = 1.0 - jnp.any(found, axis=1, keepdims=True).astype(jnp.float32)
    return pick, found.astype(jnp.bfloat16), keep


def predict(records, missing, neighbours, weights, freq_bins):
    devices = lax.axis_size("shots")
    position = lax.axis_index("shots")
    shot_rows, order, samples = records.shape
    members = devices // 2
    half = order // 2
    edge_rows = shot_step(shot_rows)
    side = (position // members).astype(jnp.int32)
    groups = [list(range(members)), list(range(members, devices))]
    pairs = [(i, (i + members) % devices) for i in range(devices)]
    exchange = lambda blocks: lax.all_to_all(
        blocks, "shots", split_axis=0, concat_axis=0, axis_index_groups=groups, tiled=True
    )
    across = lambda block: lax.ppermute(block, "shots", pairs)
    widths = [order * share // sum(SHARES) for share in SHARES]
    firsts = [sum(widths[:index]) for index in range(len(widths))]
    forward, inverse = tables(freq_bins, samples)
    last_edge, next_edge = half - edge_rows, half
    own_start, other_start = side * half, (1 - side) * half
    own_edge_start = jnp.where(side == 0, last_edge, next_edge)
    other_edge_start = jnp.where(side == 0, next_edge, last_edge)
    fill = functools.partial(fill_tables, missing, neighbours, weights)
    tables_own = fill(own_start, half, other_edge_start, edge_rows)
    tables_other = fill(other_start, half, own_edge_start, edge_rows)
    own, other, edges = [], [], []
    for first, width in zip(firsts, widths):
        block = forward_chunk(records, forward, first, width)
        block = exchange(block)
        own.append(block)
        other.append(across(block))
        edges.append(
            jnp.where(side == 0, block[members - 1, :, shot_rows - edge_rows :], block[0, :, :edge_rows])
        )
    beyond = across(jnp.concatenate(edges, axis=-1))
    left = fill_own(own, beyond, tables_own, tuple(firsts))
    result = None
    for index, first in enumerate(firsts):
        predicted = product(side.reshape(1), other[index], edges[index], tables_other, left, first)
        predicted = exchange(predicted)
        result = inverse_chunk(predicted, inverse, result, first, order)
    return result


def solution(mesh):
    return jax.shard_map(
        predict,
        mesh=mesh,
        in_specs=(
            P(("lines", "shots"), None, None),
            P("lines"),
            P("lines", None),
            P("lines", None),
            P(),
        ),
        out_specs=P(("lines", "shots"), None, None),
        check_vma=False,
    )
```

time: 228 us -> 224 us (0.982)
  local copies, waits for them, and re-layouts: 82.5 us -> 8.04 us
  Pallas kernels: 0 us -> 68.8 us
  blocking collectives: 58.5 us -> 0 us
  starting transfers between devices: 7.51 us -> 57.3 us
  waiting for transfers between devices: 41.4 us -> 81.9 us
  matrix products: 34.7 us -> 0 us
  other arithmetic: 1.16 us -> 6.7 us
    ppermute x1 -> x6, waiting for transfers between devices: 0.01 us -> 71 us  [predict(): across = lambda block: lax.ppermute(block, 'shots', pairs)]
    pallas_call x0 -> x16, Pallas kernels: none -> 68.8 us  [the longest x5 27.8 us: forward_chunk(): pl.pallas_call(forward_body, grid=(shot_rows // step,), in_specs=[pl.Bloc...]
    all_to_all x1 -> x0, blocking collectives: 58.5 us -> none  [shards(): lax.all_to_all(outgoing_back, 'shots', split_axis=2, concat_axis=0, tiled...]
    convert_element_type x3 -> x0, local copies, waits for them, and re-layouts: 47 us -> none  [the longest x1 44.2 us: shards(): multiples.astype(jnp.bfloat16)]
    all_to_all x1 -> x10, starting transfers between devices: 7.44 us -> 47.5 us  [predict(): lax.all_to_all(blocks, 'shots', split_axis=0, concat_axis=0, axis_index_g...]
    dot_general x4 -> x0, matrix products: 34.7 us -> none  [the longest x1 14.2 us: shards(): jnp.einsum('shrt,tpc->phcsr', blocked, forward, preferred_element_type=jn...]
    all_to_all x1 -> x10, waiting for transfers between devices: 41.4 us -> 10.9 us  [predict(): lax.all_to_all(blocks, 'shots', split_axis=0, concat_axis=0, axis_index_g...]
    ppermute x1 -> x6, starting transfers between devices: 0.07 us -> 9.74 us  [predict(): across = lambda block: lax.ppermute(block, 'shots', pairs)]
  transfers between devices with their start and end apart: 2 -> 16, of which waited for: 1 -> 7; matrix products, arithmetic and copies ran while one was open for 3% -> 3% of each run, Pallas kernels for 0% -> 27%
where the time goes in v2:
time: 224 us; the launch traced here: 223 us
  waiting for transfers between devices  81.9 us (37%)
  Pallas kernels  68.8 us (31%)
  starting transfers between devices  57.3 us (26%)
  local copies, waits for them, and re-layouts  8.04 us (4%)
  other arithmetic  6.7 us (3%)
    ppermute x6, waiting for transfers between devices, predict(): across = lambda block: lax.ppermute(block, 'shots', pairs)  71 us
    all_to_all x10, starting transfers between devices, predict(): lax.all_to_all(blocks, 'shots', split_axis=0, concat_axis=0, axis_index_g...  47.5 us
    pallas_call x5, Pallas kernels, forward_chunk(): pl.pallas_call(forward_body, grid=(shot_rows // step,), in_specs=[pl.Bloc...  27.8 us
    pallas_call x5, Pallas kernels, inverse_chunk(): pl.pallas_call(inverse_body, grid=(shot_rows // step,), in_specs=in_specs...  22.1 us
    pallas_call x5, Pallas kernels, product(): pl.pallas_call(functools.partial(product_body, first=first, scale=-1.0 /...  15.1 us
    all_to_all x10, waiting for transfers between devices, predict(): lax.all_to_all(blocks, 'shots', split_axis=0, concat_axis=0, axis_index_g...  10.9 us
    ppermute x6, starting transfers between devices, predict(): across = lambda block: lax.ppermute(block, 'shots', pairs)  9.74 us
    unnamed x16, local copies, waits for them, and re-layouts  7.69 us
  transfers between devices with their start and end apart: 16, of which 7 were waited for; matrix products, arithmetic and copies ran while one was open for 3% of the time, Pallas kernels for 27%

profile of v2, /device:TPU:1, one launch (start us, length us, event | category | flops | bytes accessed | tf_op | source)
XLA Modules:
  0.0 222.9 jit_solution(7854164184555349888)
XLA Ops:
  0.8 4.6 %shard_map.56 = bf16[8,2,64,128]{3,2,1,0:T(8,128)(2,1)} custom-call(bf16[64,1024,256]{2,1,0:T(8,128)(2,1)} %records_ref.9, bf16[16,256]{1,0:T(8,128)(2,1)S(1)} %reshape.161.table_ref), custom_call_target="tpu_custom_call" | custom-call | flops 67108864 | bytes 4194304 | tf_op jit(solution)/shard_map/pallas_call | solution.py:49
  5.5 5.3 %all-to-all-start.1 = ((bf16[8,2,64,128]{3,2,1,0:T(8,128)(2,1)}), bf16[8,2,64,128]{3,2,1,0:T(8,128)(2,1)S(1)}, u32[]{:S(2)}, u32[]{:S(2)}) async-start(bf16[8,2,64,128]{3,2,1,0:T(8,128)(2,1)} %shard_map.56), calls=%async_computation.1 | async-start | bytes 524288 | tf_op jit(solution)/shard_map/all_to_all | solution.py:235
  10.7 6.2 %shard_map.59 = bf16[8,2,64,256]{3,2,1,0:T(8,128)(2,1)} custom-call(bf16[64,1024,256]{2,1,0:T(8,128)(2,1)} %records_ref.9, bf16[16,256]{1,0:T(8,128)(2,1)S(1)} %reshape.161.table_ref), custom_call_target="tpu_custom_call" | custom-call | flops 134217728 | bytes 8388608 | tf_op jit(solution)/shard_map/pallas_call | solution.py:49
  16.9 4.2 %all-to-all-start.4 = ((bf16[8,2,64,256]{3,2,1,0:T(8,128)(2,1)}), bf16[8,2,64,256]{3,2,1,0:T(8,128)(2,1)S(1)}, u32[]{:S(2)}, u32[]{:S(2)}) async-start(bf16[8,2,64,256]{3,2,1,0:T(8,128)(2,1)} %shard_map.59), calls=%async_computation.4 | async-start | bytes 1048576 | tf_op jit(solution)/shard_map/all_to_all | solution.py:235
  21.1 6.2 %shard_map.58 = bf16[8,2,64,256]{3,2,1,0:T(8,128)(2,1)} custom-call(bf16[64,1024,256]{2,1,0:T(8,128)(2,1)} %records_ref.9, bf16[16,256]{1,0:T(8,128)(2,1)S(1)} %reshape.161.table_ref), custom_call_target="tpu_custom_call" | custom-call | flops 134217728 | bytes 8388608 | tf_op jit(solution)/shard_map/pallas_call | solution.py:49
  29.0 4.4 %all-to-all-start.3 = ((bf16[8,2,64,256]{3,2,1,0:T(8,128)(2,1)}), bf16[8,2,64,256]{3,2,1,0:T(8,128)(2,1)S(1)}, u32[]{:S(2)}, u32[]{:S(2)}) async-start(bf16[8,2,64,256]{3,2,1,0:T(8,128)(2,1)} %shard_map.58), calls=%async_computation.3 | async-start | bytes 1048576 | tf_op jit(solution)/shard_map/all_to_all | solution.py:235
  33.4 6.2 %shard_map.57 = bf16[8,2,64,256]{3,2,1,0:T(8,128)(2,1)} custom-call(bf16[64,1024,256]{2,1,0:T(8,128)(2,1)} %records_ref.9, bf16[16,256]{1,0:T(8,128)(2,1)S(1)} %reshape.161.table_ref), custom_call_target="tpu_custom_call" | custom-call | flops 134217728 | bytes 8388608 | tf_op jit(solution)/shard_map/pallas_call | solution.py:49
  41.3 4.4 %all-to-all-start.2 = ((bf16[8,2,64,256]{3,2,1,0:T(8,128)(2,1)}), bf16[8,2,64,256]{3,2,1,0:T(8,128)(2,1)S(1)}, u32[]{:S(2)}, u32[]{:S(2)}) async-start(bf16[8,2,64,256]{3,2,1,0:T(8,128)(2,1)} %shard_map.57), calls=%async_computation.2 | async-start | bytes 1048576 | tf_op jit(solution)/shard_map/all_to_all | solution.py:235
  45.7 4.6 %shard_map.55 = bf16[8,2,64,128]{3,2,1,0:T(8,128)(2,1)} custom-call(bf16[64,1024,256]{2,1,0:T(8,128)(2,1)} %records_ref.9, bf16[16,256]{1,0:T(8,128)(2,1)S(1)} %reshape.161.table_ref), custom_call_target="tpu_custom_call" | custom-call | flops 67108864 | bytes 4194304 | tf_op jit(solution)/shard_map/pallas_call | solution.py:49
  54.8 4.5 %all-to-all-start = ((bf16[8,2,64,128]{3,2,1,0:T(8,128)(2,1)}), bf16[8,2,64,128]{3,2,1,0:T(8,128)(2,1)S(1)}, u32[]{:S(2)}, u32[]{:S(2)}) async-start(bf16[8,2,64,128]{3,2,1,0:T(8,128)(2,1)} %shard_map.55), calls=%async_computation | async-start | bytes 524288 | tf_op jit(solution)/shard_map/all_to_all | solution.py:235
  61.2 7.9 %all-to-all-done.refs_4_ = bf16[8,2,64,128]{3,2,1,0:T(8,128)(2,1)S(1)} async-done(((bf16[8,2,64,128]{3,2,1,0:T(8,128)(2,1)}), bf16[8,2,64,128]{3,2,1,0:T(8,128)(2,1)S(1)}, u32[]{:S(2)}, u32[]{:S(2)}) %all-to-all-start) | async-done | bytes 262176 | tf_op jit(solution)/shard_map/all_to_all | solution.py:235
  73.3 13.3 %collective-permute-done.1.refs_5_ = bf16[2,16,1024]{2,1,0:T(8,128)(2,1)S(1)} collective-permute-done((bf16[2,16,1024]{2,1,0:T(8,128)(2,1)}, bf16[2,16,1024]{2,1,0:T(8,128)(2,1)S(1)}, u32[]{:S(2)}, u32[]{:S(2)}) %collective-permute-start.1) | collective-permute-done | bytes 65568 | tf_op jit(solution)/shard_map/ppermute | solution.py:238
  94.0 4.5 %all-to-all-start.9 = ((bf16[8,2,64,128]{3,2,1,0:T(8,128)(2,1)}), bf16[8,2,64,128]{3,2,1,0:T(8,128)(2,1)S(1)}, u32[]{:S(2)}, u32[]{:S(2)}) async-start(bf16[8,2,64,128]{3,2,1,0:T(8,128)(2,1)} %shard_map.64), calls=%async_computation.9 | async-start | bytes 524288 | tf_op jit(solution)/shard_map/all_to_all | solution.py:235
  100.1 4.2 %shard_map.61 = bf16[8,2,64,256]{3,2,1,0:T(8,128)(2,1)} custom-call(s32[1]{0:T(128)} %bitcast.side_ref, bf16[8,2,64,256]{3,2,1,0:T(8,128)(2,1)} %collective-permute-done.2.other_ref, bf16[2,16,256]{2,1,0:T(8,128)(2,1)S(1)} %get-tuple-element.10.edge_ref, bf16[256,528]{1,0:T(8,128)(2,1)S(1)} %get-tuple-element.35.pick_ref, ...), custom_call_target="tpu_custom_call" | custom-call | flops 2147483648 | bytes 4194304 | tf_op jit(solution)/shard_map/pallas_call | solution.py:193
  104.3 4.2 %all-to-all-start.6 = ((bf16[8,2,64,256]{3,2,1,0:T(8,128)(2,1)}), bf16[8,2,64,256]{3,2,1,0:T(8,128)(2,1)S(1)}, u32[]{:S(2)}, u32[]{:S(2)}) async-start(bf16[8,2,64,256]{3,2,1,0:T(8,128)(2,1)} %shard_map.61), calls=%async_computation.6 | async-start | bytes 1048576 | tf_op jit(solution)/shard_map/all_to_all | solution.py:235
  109.8 24.4 %collective-permute-done.3.other_ref = bf16[8,2,64,256]{3,2,1,0:T(8,128)(2,1)S(1)} collective-permute-done((bf16[8,2,64,256]{3,2,1,0:T(8,128)(2,1)S(1)}, bf16[8,2,64,256]{3,2,1,0:T(8,128)(2,1)S(1)}, u32[]{:S(2)}, u32[]{:S(2)}) %collective-permute-start.3) | collective-permute-done | bytes 524320 | tf_op jit(solution)/shard_map/ppermute | solution.py:238
  139.0 4.3 %all-to-all-start.7 = ((bf16[8,2,64,256]{3,2,1,0:T(8,128)(2,1)}), bf16[8,2,64,256]{3,2,1,0:T(8,128)(2,1)S(1)}, u32[]{:S(2)}, u32[]{:S(2)}) async-start(bf16[8,2,64,256]{3,2,1,0:T(8,128)(2,1)} %shard_map.62), calls=%async_computation.7 | async-start | bytes 1048576 | tf_op jit(solution)/shard_map/all_to_all | solution.py:235
  145.0 23.6 %collective-permute-done.4.other_ref = bf16[8,2,64,256]{3,2,1,0:T(8,128)(2,1)S(1)} collective-permute-done((bf16[8,2,64,256]{3,2,1,0:T(8,128)(2,1)S(1)}, bf16[8,2,64,256]{3,2,1,0:T(8,128)(2,1)S(1)}, u32[]{:S(2)}, u32[]{:S(2)}) %collective-permute-start.4) | collective-permute-done | bytes 524320 | tf_op jit(solution)/shard_map/ppermute | solution.py:238
  173.3 4.6 %all-to-all-start.8 = ((bf16[8,2,64,256]{3,2,1,0:T(8,128)(2,1)}), bf16[8,2,64,256]{3,2,1,0:T(8,128)(2,1)S(1)}, u32[]{:S(2)}, u32[]{:S(2)}) async-start(bf16[8,2,64,256]{3,2,1,0:T(8,128)(2,1)} %shard_map.63), calls=%async_computation.8 | async-start | bytes 1048576 | tf_op jit(solution)/shard_map/all_to_all | solution.py:235
  180.0 9.7 %collective-permute-done.other_ref = bf16[8,2,64,128]{3,2,1,0:T(8,128)(2,1)S(1)} collective-permute-done((bf16[8,2,64,128]{3,2,1,0:T(8,128)(2,1)S(1)}, bf16[8,2,64,128]{3,2,1,0:T(8,128)(2,1)S(1)}, u32[]{:S(2)}, u32[]{:S(2)}) %collective-permute-start) | collective-permute-done | bytes 262176 | tf_op jit(solution)/shard_map/ppermute | solution.py:238
  193.6 7.2 %all-to-all-start.5 = ((bf16[8,2,64,128]{3,2,1,0:T(8,128)(2,1)}), bf16[8,2,64,128]{3,2,1,0:T(8,128)(2,1)S(1)}, u32[]{:S(2)}, u32[]{:S(2)}) async-start(bf16[8,2,64,128]{3,2,1,0:T(8,128)(2,1)} %shard_map.60), calls=%async_computation.5 | async-start | bytes 524288 | tf_op jit(solution)/shard_map/all_to_all | solution.py:235
  204.3 5.0 %shard_map.66.refs_0_ = bf16[64,1024,256]{2,1,0:T(8,128)(2,1)} custom-call(bf16[8,2,64,256]{3,2,1,0:T(8,128)(2,1)S(1)} %all-to-all-done.8.planes_ref, bf16[16,256]{1,0:T(8,128)(2,1)S(1)} %reshape.162.table_ref, bf16[64,1024,256]{2,1,0:T(8,128)(2,1)} %shard_map.65.refs_0_), custom_call_target="tpu_custom_call", output_to_operand_aliasing={{}: (2, {})} | custom-call | flops 134217728 | bytes 8388608 | tf_op jit(solution)/shard_map/pallas_call | solution.py:94
  209.4 5.0 %shard_map.67.refs_0_ = bf16[64,1024,256]{2,1,0:T(8,128)(2,1)} custom-call(bf16[8,2,64,256]{3,2,1,0:T(8,128)(2,1)S(1)} %all-to-all-done.7.planes_ref, bf16[16,256]{1,0:T(8,128)(2,1)S(1)} %reshape.162.table_ref, bf16[64,1024,256]{2,1,0:T(8,128)(2,1)} %shard_map.66.refs_0_), custom_call_target="tpu_custom_call", output_to_operand_aliasing={{}: (2, {})} | custom-call | flops 134217728 | bytes 8388608 | tf_op jit(solution)/shard_map/pallas_call | solution.py:94
  214.4 5.0 %shard_map.68.refs_0_ = bf16[64,1024,256]{2,1,0:T(8,128)(2,1)} custom-call(bf16[8,2,64,256]{3,2,1,0:T(8,128)(2,1)S(1)} %all-to-all-done.6.planes_ref, bf16[16,256]{1,0:T(8,128)(2,1)S(1)} %reshape.162.table_ref, bf16[64,1024,256]{2,1,0:T(8,128)(2,1)} %shard_map.67.refs_0_), custom_call_target="tpu_custom_call", output_to_operand_aliasing={{}: (2, {})} | custom-call | flops 134217728 | bytes 8388608 | tf_op jit(solution)/shard_map/pallas_call | solution.py:94
  (65 shorter events, 49.2 us)
Async XLA Ops:
  5.5 11.4 %all-to-all-start.1 = ((bf16[8,2,64,128]{3,2,1,0:T(8,128)(2,1)}), bf16[8,2,64,128]{3,2,1,0:T(8,128)(2,1)S(1)}, u32[]{:S(2)}, u32[]{:S(2)}) async-start(bf16[8,2,64,128]{3,2,1,0:T(8,128)(2,1)} %shard_map.56), calls=%async_computation.1 | async-start | bytes 524288 | tf_op jit(solution)/shard_map/all_to_all | solution.py:235
  16.9 12.1 %all-to-all-start.4 = ((bf16[8,2,64,256]{3,2,1,0:T(8,128)(2,1)}), bf16[8,2,64,256]{3,2,1,0:T(8,128)(2,1)S(1)}, u32[]{:S(2)}, u32[]{:S(2)}) async-start(bf16[8,2,64,256]{3,2,1,0:T(8,128)(2,1)} %shard_map.59), calls=%async_computation.4 | async-start | bytes 1048576 | tf_op jit(solution)/shard_map/all_to_all | solution.py:235
  21.1 18.5 %copy-start.7 = (s32[128]{0:T(128)S(1)}, s32[128]{0:T(128)}, u32[]{:S(2)}) copy-start(s32[128]{0:T(128)} %param.6) | copy-start | bytes 1540
  29.0 12.3 %all-to-all-start.3 = ((bf16[8,2,64,256]{3,2,1,0:T(8,128)(2,1)}), bf16[8,2,64,256]{3,2,1,0:T(8,128)(2,1)S(1)}, u32[]{:S(2)}, u32[]{:S(2)}) async-start(bf16[8,2,64,256]{3,2,1,0:T(8,128)(2,1)} %shard_map.58), calls=%async_computation.3 | async-start | bytes 1048576 | tf_op jit(solution)/shard_map/all_to_all | solution.py:235
  33.4 17.2 %copy-start.5 = (s32[128,3]{0,1:T(4,128)S(1)}, s32[128,3]{0,1:T(4,128)}, u32[]{:S(2)}) copy-start(s32[128,3]{0,1:T(4,128)} %param.7) | copy-start | bytes 4612
  33.4 17.3 %copy-start.6 = (f32[128,3]{0,1:T(4,128)S(1)}, f32[128,3]{0,1:T(4,128)}, u32[]{:S(2)}) copy-start(f32[128,3]{0,1:T(4,128)} %param.8) | copy-start | bytes 4612
  41.3 13.5 %all-to-all-start.2 = ((bf16[8,2,64,256]{3,2,1,0:T(8,128)(2,1)}), bf16[8,2,64,256]{3,2,1,0:T(8,128)(2,1)S(1)}, u32[]{:S(2)}, u32[]{:S(2)}) async-start(bf16[8,2,64,256]{3,2,1,0:T(8,128)(2,1)} %shard_map.57), calls=%async_computation.2 | async-start | bytes 1048576 | tf_op jit(solution)/shard_map/all_to_all | solution.py:235
  51.9 38.5 %collective-permute-start.5 = (bf16[8,2,64,128]{3,2,1,0:T(8,128)(2,1)S(1)}, bf16[8,2,64,128]{3,2,1,0:T(8,128)(2,1)S(1)}, u32[]{:S(2)}, u32[]{:S(2)}) collective-permute-start(bf16[8,2,64,128]{3,2,1,0:T(8,128)(2,1)S(1)} %all-to-all-done.1.refs_0_), channel_id=1, source_target_pairs={{0,8},{1,9},{2,10},{3,11},{4,12},{5,13},{6,14},{7,15},{8,0},{9,1},... | collective-permute-start | bytes 786440 | tf_op jit(solution)/shard_map/ppermute | solution.py:238
  54.8 14.2 %all-to-all-start = ((bf16[8,2,64,128]{3,2,1,0:T(8,128)(2,1)}), bf16[8,2,64,128]{3,2,1,0:T(8,128)(2,1)S(1)}, u32[]{:S(2)}, u32[]{:S(2)}) async-start(bf16[8,2,64,128]{3,2,1,0:T(8,128)(2,1)} %shard_map.55), calls=%async_computation | async-start | bytes 524288 | tf_op jit(solution)/shard_map/all_to_all | solution.py:235
  69.7 16.9 %collective-permute-start.1 = (bf16[2,16,1024]{2,1,0:T(8,128)(2,1)}, bf16[2,16,1024]{2,1,0:T(8,128)(2,1)S(1)}, u32[]{:S(2)}, u32[]{:S(2)}) collective-permute-start(bf16[2,16,1024]{2,1,0:T(8,128)(2,1)} %get-tuple-element.7), channel_id=1, source_target_pairs={{0,8},{1,9},{2,10},{3,11},{4,12},{5,13},{6,14},{7,15},{8,0},{9,1},... | collective-permute-start | bytes 196616 | tf_op jit(solution)/shard_map/ppermute | solution.py:238
  69.7 28.8 %collective-permute-start.2 = (bf16[8,2,64,256]{3,2,1,0:T(8,128)(2,1)S(1)}, bf16[8,2,64,256]{3,2,1,0:T(8,128)(2,1)}, u32[]{:S(2)}, u32[]{:S(2)}) collective-permute-start(bf16[8,2,64,256]{3,2,1,0:T(8,128)(2,1)S(1)} %all-to-all-done.4.refs_3_), channel_id=1, source_target_pairs={{0,8},{1,9},{2,10},{3,11},{4,12},{5,13},{6,14},{7,15},{8,0},{9,1},... | collective-permute-start | bytes 1572872 | tf_op jit(solution)/shard_map/ppermute | solution.py:238
  92.7 1.3 copy-start
  94.0 10.3 %all-to-all-start.9 = ((bf16[8,2,64,128]{3,2,1,0:T(8,128)(2,1)}), bf16[8,2,64,128]{3,2,1,0:T(8,128)(2,1)S(1)}, u32[]{:S(2)}, u32[]{:S(2)}) async-start(bf16[8,2,64,128]{3,2,1,0:T(8,128)(2,1)} %shard_map.64), calls=%async_computation.9 | async-start | bytes 524288 | tf_op jit(solution)/shard_map/all_to_all | solution.py:235
  98.5 1.6 copy-start.1
  104.3 34.7 %all-to-all-start.6 = ((bf16[8,2,64,256]{3,2,1,0:T(8,128)(2,1)}), bf16[8,2,64,256]{3,2,1,0:T(8,128)(2,1)S(1)}, u32[]{:S(2)}, u32[]{:S(2)}) async-start(bf16[8,2,64,256]{3,2,1,0:T(8,128)(2,1)} %shard_map.61), calls=%async_computation.6 | async-start | bytes 1048576 | tf_op jit(solution)/shard_map/all_to_all | solution.py:235
  108.5 25.7 %collective-permute-start.3 = (bf16[8,2,64,256]{3,2,1,0:T(8,128)(2,1)S(1)}, bf16[8,2,64,256]{3,2,1,0:T(8,128)(2,1)S(1)}, u32[]{:S(2)}, u32[]{:S(2)}) collective-permute-start(bf16[8,2,64,256]{3,2,1,0:T(8,128)(2,1)S(1)} %all-to-all-done.3.refs_2_), channel_id=1, source_target_pairs={{0,8},{1,9},{2,10},{3,11},{4,12},{5,13},{6,14},{7,15},{8,0},{9,1},... | collective-permute-start | bytes 1572872 | tf_op jit(solution)/shard_map/ppermute | solution.py:238
  134.2 1.6 copy-start.2
  139.0 34.3 %all-to-all-start.7 = ((bf16[8,2,64,256]{3,2,1,0:T(8,128)(2,1)}), bf16[8,2,64,256]{3,2,1,0:T(8,128)(2,1)S(1)}, u32[]{:S(2)}, u32[]{:S(2)}) async-start(bf16[8,2,64,256]{3,2,1,0:T(8,128)(2,1)} %shard_map.62), calls=%async_computation.7 | async-start | bytes 1048576 | tf_op jit(solution)/shard_map/all_to_all | solution.py:235
  143.3 25.3 %collective-permute-start.4 = (bf16[8,2,64,256]{3,2,1,0:T(8,128)(2,1)S(1)}, bf16[8,2,64,256]{3,2,1,0:T(8,128)(2,1)S(1)}, u32[]{:S(2)}, u32[]{:S(2)}) collective-permute-start(bf16[8,2,64,256]{3,2,1,0:T(8,128)(2,1)S(1)} %all-to-all-done.2.refs_1_), channel_id=1, source_target_pairs={{0,8},{1,9},{2,10},{3,11},{4,12},{5,13},{6,14},{7,15},{8,0},{9,1},... | collective-permute-start | bytes 1572872 | tf_op jit(solution)/shard_map/ppermute | solution.py:238
  168.6 1.6 copy-start.3
  173.3 20.2 %all-to-all-start.8 = ((bf16[8,2,64,256]{3,2,1,0:T(8,128)(2,1)}), bf16[8,2,64,256]{3,2,1,0:T(8,128)(2,1)S(1)}, u32[]{:S(2)}, u32[]{:S(2)}) async-start(bf16[8,2,64,256]{3,2,1,0:T(8,128)(2,1)} %shard_map.63), calls=%async_computation.8 | async-start | bytes 1048576 | tf_op jit(solution)/shard_map/all_to_all | solution.py:235
  177.9 11.8 %collective-permute-start = (bf16[8,2,64,128]{3,2,1,0:T(8,128)(2,1)S(1)}, bf16[8,2,64,128]{3,2,1,0:T(8,128)(2,1)S(1)}, u32[]{:S(2)}, u32[]{:S(2)}) collective-permute-start(bf16[8,2,64,128]{3,2,1,0:T(8,128)(2,1)S(1)} %all-to-all-done.refs_4_), channel_id=1, source_target_pairs={{0,8},{1,9},{2,10},{3,11},{4,12},{5,13},{6,14},{7,15},{8,0},{9,1},... | collective-permute-start | bytes 786440 | tf_op jit(solution)/shard_map/ppermute | solution.py:238
  189.8 1.6 copy-start.4
  193.6 25.8 %all-to-all-start.5 = ((bf16[8,2,64,128]{3,2,1,0:T(8,128)(2,1)}), bf16[8,2,64,128]{3,2,1,0:T(8,128)(2,1)S(1)}, u32[]{:S(2)}, u32[]{:S(2)}) async-start(bf16[8,2,64,128]{3,2,1,0:T(8,128)(2,1)} %shard_map.60), calls=%async_computation.5 | async-start | bytes 524288 | tf_op jit(solution)/shard_map/all_to_all | solution.py:235

commit v3 on v1

v3 whole, which is shorter than its diff:
```python
import functools
import math

import jax
import jax.numpy as jnp
from jax import lax
from jax.experimental import pallas as pl
from jax.experimental.pallas import tpu as pltpu
from jax.sharding import PartitionSpec as P


PARTS = 4
OUTWARD = (1, 3)
HOMEWARD = (3, 1)
STREAM_VMEM = 36 * 1024 * 1024
VMEM_LIMIT = 24 * 1024 * 1024


def tables(freq_bins, sample_count):
    bin_count = freq_bins.shape[0]
    sample_ids = jnp.arange(sample_count, dtype=jnp.int32)
    phases = freq_bins[None, :] * sample_ids[:, None] % sample_count
    angles = phases.astype(jnp.float32) * (2.0 * math.pi / sample_count)
    trig_pair = jnp.stack([jnp.cos(angles), -jnp.sin(angles)], axis=-1)
    forward = (trig_pair / math.sqrt(sample_count)).astype(jnp.bfloat16)
    inverse = (trig_pair * math.sqrt(2.0 / bin_count)).astype(jnp.bfloat16)
    rows = lambda table: jnp.transpose(table, (1, 2, 0)).reshape(2 * bin_count, sample_count)
    return rows(forward), rows(inverse)


def shot_step(shot_rows):
    return math.gcd(shot_rows, 16)


def forward_body(records_ref, table_ref, out_ref, held_ref, rows_ref, semaphores, *, first):
    pieces, step, width, samples = held_ref.shape
    planes = table_ref.shape[0]
    halves = records_ref.shape[1]
    places = [(shot * step, half) for shot in range(pieces // halves) for half in range(halves)]
    copies = [
        pltpu.make_async_copy(
            records_ref.at[pl.ds(shot, step), half, pl.ds(first, width), :],
            held_ref.at[piece],
            semaphores.at[piece],
        )
        for piece, (shot, half) in enumerate(places)
    ]
    for copy in copies:
        copy.start()
    for piece, (shot, half) in enumerate(places):
        copies[piece].wait()
        spectra = lax.dot_general(
            table_ref[...],
            held_ref[piece].reshape(step * width, samples),
            (((1,), (1,)), ((), ())),
            preferred_element_type=jnp.float32,
        )
        for row in range(step):
            rows_ref[:, row, :] = spectra[:, row * width : (row + 1) * width]
        out_ref[:, half, :, shot : shot + step, :] = (
            rows_ref[...].astype(jnp.bfloat16).reshape(planes // 2, 2, step, width)
        )


def forward_chunk(records, table, first, width):
    shot_rows, halves, _, samples = records.shape
    planes = table.shape[0]
    step = shot_step(shot_rows)
    pieces = halves * shot_rows // step
    vmem = pl.BlockSpec(memory_space=pltpu.VMEM)
    return pl.pallas_call(
        functools.partial(forward_body, first=first),
        in_specs=[pl.BlockSpec(memory_space=pl.ANY), vmem],
        out_specs=vmem,
        out_shape=jax.ShapeDtypeStruct((planes // 2, halves, 2, shot_rows, width), jnp.bfloat16),
        scratch_shapes=[
            pltpu.VMEM((pieces, step, width, samples), jnp.bfloat16),
            pltpu.VMEM((planes, step, width), jnp.float32),
            pltpu.SemaphoreType.DMA((pieces,)),
        ],
        compiler_params=pltpu.CompilerParams(vmem_limit_bytes=STREAM_VMEM),
        cost_estimate=pl.CostEstimate(
            flops=2 * shot_rows * halves * width * samples * planes,
            bytes_accessed=2 * shot_rows * halves * width * samples,
            transcendentals=0,
        ),
    )(records, table)


def inverse_body(planes_ref, table_ref, *refs, first):
    out_ref, held_ref, rows_ref, semaphores = refs[-4:]
    bins, halves, parts, _, width = planes_ref.shape
    pieces, step = held_ref.shape[:2]
    copies = []
    for piece in range(pieces):
        shot, half = piece // halves * step, piece % halves
        rows_ref[...] = (
            planes_ref[:, half, :, shot : shot + step, :]
            .astype(jnp.float32)
            .reshape(bins * parts, step, width)
        )
        for row in range(step):
            left = rows_ref[:, row, :].astype(jnp.bfloat16)
            held_ref[piece, row] = lax.dot_general(
                left, table_ref[...], (((0,), (0,)), ((), ())), preferred_element_type=jnp.float32
            ).astype(jnp.bfloat16)
        copy = pltpu.make_async_copy(
            held_ref.at[piece],
            out_ref.at[pl.ds(shot, step), half, pl.ds(first, width), :],
            semaphores.at[piece],
        )
        copy.start()
        copies.append(copy)
    for copy in copies:
        copy.wait()


def inverse_chunk(returned, table, kept, first, half):
    _, halves, _, shot_rows, width = returned.shape
    planes, samples = table.shape
    step = shot_step(shot_rows)
    pieces = halves * shot_rows // step
    vmem = pl.BlockSpec(memory_space=pltpu.VMEM)
    operands = [returned, table] + ([] if kept is None else [kept])
    return pl.pallas_call(
        functools.partial(inverse_body, first=first),
        in_specs=[vmem, vmem] + [pl.BlockSpec(memory_space=pl.ANY)] * (len(operands) - 2),
        out_specs=pl.BlockSpec(memory_space=pl.ANY),
        out_shape=jax.ShapeDtypeStruct((shot_rows, halves, half, samples), jnp.bfloat16),
        scratch_shapes=[
            pltpu.VMEM((pieces, step, width, samples), jnp.bfloat16),
            pltpu.VMEM((planes, step, width), jnp.float32),
            pltpu.SemaphoreType.DMA((pieces,)),
        ],
        input_output_aliases={} if kept is None else {2: 0},
        compiler_params=pltpu.CompilerParams(vmem_limit_bytes=STREAM_VMEM),
        cost_estimate=pl.CostEstimate(
            flops=2 * shot_rows * halves * width * samples * planes,
            bytes_accessed=2 * shot_rows * halves * width * samples,
            transcendentals=0,
        ),
    )(*operands)


def fill_body(spectra_ref, pick_ref, place_ref, keep_ref, out_ref):
    devices, parts, rows, width = spectra_ref.shape
    count = pick_ref.shape[0] // 2
    for part in range(parts):
        recorded = spectra_ref[:, part].reshape(devices * rows, width)
        both = jnp.dot(pick_ref[...], recorded, preferred_element_type=jnp.float32)
        replaced = (both[:count] + both[count:]).astype(jnp.bfloat16)
        placed = jnp.dot(place_ref[...], replaced, preferred_element_type=jnp.float32)
        out_ref[part] = (placed + recorded.astype(jnp.float32) * keep_ref[...]).astype(jnp.bfloat16)


def fill(spectra, pick, place, keep):
    devices, parts, rows, width = spectra.shape
    order = devices * rows
    return pl.pallas_call(
        fill_body,
        out_shape=jax.ShapeDtypeStruct((parts, order, width), jnp.bfloat16),
        compiler_params=pltpu.CompilerParams(vmem_limit_bytes=VMEM_LIMIT),
        cost_estimate=pl.CostEstimate(
            flops=8 * pick.shape[0] * order * width,
            bytes_accessed=8 * order * width,
            transcendentals=0,
        ),
        name="fill",
    )(spectra, pick, place, keep)


def product_body(member_ref, *refs, count, first, scale):
    sources, out_ref, right_ref = refs[: 2 * count], refs[2 * count], refs[2 * count + 1]
    devices, parts, rows, width = out_ref.shape
    order = devices * rows
    half = order // 2
    member = member_ref[0]
    spans = []
    start = 0
    for ref in sources[:count]:
        size = ref.shape[2]
        low, high = max(start, first), min(start + size, first + width)
        if low < high:
            spans.append((ref, low - start, low - first, high - low))
        start += size
    for ref, begin, at, size in spans:
        real = ref[0, :, begin : begin + size]
        imag = ref[1, :, begin : begin + size]
        right_ref[0, :, at : at + size] = real
        right_ref[0, :, width + at : width + at + size] = imag
        right_ref[1, :, at : at + size] = -imag
        right_ref[1, :, width + at : width + at + size] = real
    total = None
    for owner in range(2):
        offset = (member if owner == 0 else 1 - member) * half
        for part in range(parts):
            start = 0
            for ref in sources[owner * count : (owner + 1) * count]:
                size = ref.shape[2]
                rows_at = pl.multiple_of(offset + start, 128)
                term = jnp.dot(
                    ref[part], right_ref[part, pl.ds(rows_at, size), :], preferred_element_type=jnp.float32
                )
                total = term if total is None else total + term
                start += size
    total = total * scale
    for part in range(parts):
        out_ref[:, part] = (
            total[:, part * width : (part + 1) * width]
            .astype(jnp.bfloat16)
            .reshape(devices, rows, width)
        )


def product(member, own, other, first, width, devices):
    parts, order, _ = own[0].shape
    vmem = pl.BlockSpec(memory_space=pltpu.VMEM)
    return pl.pallas_call(
        functools.partial(
            product_body, count=len(own), first=first, scale=-1.0 / math.sqrt(order)
        ),
        in_specs=[pl.BlockSpec(memory_space=pltpu.SMEM)] + [vmem] * (2 * len(own)),
        out_specs=vmem,
        out_shape=jax.ShapeDtypeStruct((devices, parts, order // devices, width), jnp.bfloat16),
        scratch_shapes=[pltpu.VMEM((parts, order, 2 * width), jnp.bfloat16)],
        compiler_params=pltpu.CompilerParams(vmem_limit_bytes=VMEM_LIMIT),
        cost_estimate=pl.CostEstimate(
            flops=16 * order * order * width, bytes_accessed=8 * order * order, transcendentals=0
        ),
    )(member, *own, *other)


def fill_tables(missing, neighbours, weights, order):
    shots = jnp.arange(order, dtype=jnp.int32)
    pick = jnp.zeros((missing.shape[0], order), jnp.float32)
    for slot in range(neighbours.shape[1]):
        pick = pick + jnp.where(
            neighbours[:, slot][:, None] == shots[None, :], weights[:, slot][:, None], 0.0
        )
    high = lax.reduce_precision(pick, 8, 7)
    found = shots[:, None] == missing[None, :]
    keep = 1.0 - jnp.any(found, axis=1, keepdims=True).astype(jnp.float32)
    both = jnp.concatenate([high, pick - high], axis=0).astype(jnp.bfloat16)
    return both, found.astype(jnp.bfloat16), keep


def spread(total, shares):
    widths = [total * share // PARTS for share in shares]
    return [(sum(widths[:index]), width) for index, width in enumerate(widths)]


def predict(records, missing, neighbours, weights, freq_bins):
    devices = lax.axis_size("shots")
    position = lax.axis_index("shots")
    shot_rows, order, samples = records.shape
    half = order // 2
    bins = freq_bins.shape[0]
    member = (position % 2).astype(jnp.int32).reshape(1)
    pairs = [(i, i ^ 1) for i in range(devices)]

    def exchange(blocks):
        return lax.all_to_all(blocks, "shots", split_axis=0, concat_axis=0, tiled=True)

    forward, inverse = tables(freq_bins, samples)
    pick, place, keep = fill_tables(missing, neighbours, weights, order)
    split = records.reshape(shot_rows, 2, half, samples)
    own, other = [], []
    for first, width in spread(half, OUTWARD):
        block = forward_chunk(split, forward, first, width)
        block = exchange(block.reshape(devices, 2, shot_rows, width))
        block = fill(block, pick, place, keep)
        own.append(block)
        other.append(lax.ppermute(block, "shots", pairs))
    result = None
    for first, width in spread(half, HOMEWARD):
        block = product(member, own, other, first, width, devices)
        block = exchange(block)
        block = block.reshape(bins, 2, 2, shot_rows, width)
        result = inverse_chunk(block, inverse, result, first, half)
    return result.reshape(shot_rows, order, samples)


def solution(mesh):
    return jax.shard_map(
        predict,
        mesh=mesh,
        in_specs=(
            P(("lines", "shots"), None, None),
            P("lines"),
            P("lines", None),
            P("lines", None),
            P(),
        ),
        out_specs=P(("lines", "shots"), None, None),
        check_vma=False,
    )
```

time: 173 us -> 157 us (0.908)
  Pallas kernels: 68.4 us -> 45.4 us
  blocking collectives: 0 us -> 22.8 us
  starting transfers between devices: 39.6 us -> 20.9 us
  waiting for transfers between devices: 59.7 us -> 64.2 us
    all_to_all x0 -> x1, blocking collectives: none -> 22.8 us  [exchange(): lax.all_to_all(blocks, 'shots', split_axis=0, concat_axis=0, tiled=True)]
    pallas_call x12 -> x6, Pallas kernels: 63.9 us -> 41.9 us  [the longest x2 15.6 us: forward_chunk(): pl.pallas_call(functools.partial(forward_body, first=first), in_specs=[pl...]
    all_to_all x8 -> x3, starting transfers between devices: 38.4 us -> 20.5 us  [exchange(): lax.all_to_all(blocks, 'shots', split_axis=0, concat_axis=0, tiled=True)]
    all_to_all x8 -> x3, waiting for transfers between devices: 58.2 us -> 62.6 us  [exchange(): lax.all_to_all(blocks, 'shots', split_axis=0, concat_axis=0, tiled=True)]
    pallas_call x4 -> x2, Pallas kernels: 4.52 us -> 3.52 us  [fill(): pl.pallas_call(fill_body, out_shape=jax.ShapeDtypeStruct((parts, order, w...]
  transfers between devices with their start and end apart: 12 -> 5, of which waited for: 8 -> 4; matrix products, arithmetic and copies ran while one was open for 0% -> 1% of each run, Pallas kernels for 30% -> 12%
where the time goes in v3:
time: 157 us
  waiting for transfers between devices  64.2 us (41%)
  Pallas kernels  45.4 us (29%)
  blocking collectives  22.8 us (15%)
  starting transfers between devices  20.9 us (13%)
  local copies, waits for them, and re-layouts  1.7 us (1%)
    all_to_all x3, waiting for transfers between devices, exchange(): lax.all_to_all(blocks, 'shots', split_axis=0, concat_axis=0, tiled=True)  62.6 us
    all_to_all x1, blocking collectives, exchange(): lax.all_to_all(blocks, 'shots', split_axis=0, concat_axis=0, tiled=True)  22.8 us
    all_to_all x3, starting transfers between devices, exchange(): lax.all_to_all(blocks, 'shots', split_axis=0, concat_axis=0, tiled=True)  20.5 us
    pallas_call x2, Pallas kernels, forward_chunk(): pl.pallas_call(functools.partial(forward_body, first=first), in_specs=[pl...  15.6 us
    pallas_call x2, Pallas kernels, inverse_chunk(): pl.pallas_call(functools.partial(inverse_body, first=first), in_specs=[vm...  13.6 us
    pallas_call x2, Pallas kernels, product(): pl.pallas_call(functools.partial(product_body, count=len(own), first=firs...  12.7 us
    pallas_call x2, Pallas kernels, fill(): pl.pallas_call(fill_body, out_shape=jax.ShapeDtypeStruct((parts, order, w...  3.52 us
  transfers between devices with their start and end apart: 5, of which 4 were waited for; matrix products, arithmetic and copies ran while one was open for 1% of the time, Pallas kernels for 12%

profile of v3, /device:TPU:1, one launch (start us, length us, event | category | flops | bytes accessed | tf_op | source)
XLA Modules:
  0.0 156.6 jit_solution(14436235378961033854)
XLA Ops:
  0.0 0.8 fusion.11
  0.8 11.0 %shard_map.56 = bf16[8,2,2,64,384]{4,3,2,1,0:T(8,128)(2,1)} custom-call(bf16[64,2,512,256]{3,2,1,0:T(8,128)(2,1)} %bitcast.27, bf16[16,256]{1,0:T(8,128)(2,1)S(1)} %reshape.141.table_ref), custom_call_target="tpu_custom_call" | custom-call | flops 402653184 | bytes 25165824 | tf_op jit(solution)/shard_map/pallas_call | solution.py:71
  11.8 0.0 copy-start.4
  11.8 0.0 copy-start.2
  11.9 7.5 %all-to-all-start.1 = ((bf16[16,2,64,384]{3,2,1,0:T(8,128)(2,1)}), bf16[16,2,64,384]{3,2,1,0:T(8,128)(2,1)S(1)}, u32[]{:S(2)}, u32[]{:S(2)}) async-start(bf16[16,2,64,384]{3,2,1,0:T(8,128)(2,1)} %bitcast.11), calls=%async_computation.1 | async-start | bytes 3145728 | tf_op jit(solution)/shard_map/all_to_all | solution.py:262
  19.3 0.2 fusion.1
  19.6 0.2 copy.10.keep_ref
  19.8 0.3 reduce-precision_convert_fusion
  20.2 31.5 %all-to-all-done.1.spectra_ref = bf16[16,2,64,384]{3,2,1,0:T(8,128)(2,1)S(1)} async-done(((bf16[16,2,64,384]{3,2,1,0:T(8,128)(2,1)}), bf16[16,2,64,384]{3,2,1,0:T(8,128)(2,1)S(1)}, u32[]{:S(2)}, u32[]{:S(2)}) %all-to-all-start.1) | async-done | bytes 1572896 | tf_op jit(solution)/shard_map/all_to_all | solution.py:262
  51.7 2.6 %fill.3.refs_1_ = bf16[2,1024,384]{2,1,0:T(8,128)(2,1)} custom-call(bf16[16,2,64,384]{3,2,1,0:T(8,128)(2,1)S(1)} %all-to-all-done.1.spectra_ref, bf16[256,1024]{1,0:T(8,128)(2,1)S(1)} %pad_maximum_fusion.pick_ref, bf16[1024,128]{1,0:T(8,128)(2,1)S(1)} %get-tuple-element.16.place_ref, f32[1024,1]{1,0:T(8,128)S(1)} %copy.10.keep_ref), custom_call_target="tpu_custom_call" | custom-call | flops 805306368 | bytes 3145728 | tf_op jit(solution)/shard_map/fill/pallas_call | solution.py:159
  54.3 4.7 %shard_map.55 = bf16[8,2,2,64,128]{4,3,2,1,0:T(8,128)(2,1)S(1)} custom-call(bf16[64,2,512,256]{3,2,1,0:T(8,128)(2,1)} %bitcast.28, bf16[16,256]{1,0:T(8,128)(2,1)S(1)} %reshape.141.table_ref), custom_call_target="tpu_custom_call" | custom-call | flops 134217728 | bytes 8388608 | tf_op jit(solution)/shard_map/pallas_call | solution.py:71
  59.0 22.8 %all_to_all.20.spectra_ref = bf16[16,2,64,128]{3,2,1,0:T(8,128)(2,1)S(1)} all-to-all(bf16[16,2,64,128]{3,2,1,0:T(8,128)(2,1)S(1)} %bitcast.26), channel_id=1, replica_groups=mesh['lines'=2,'shots'=16] {'shots'}, dimensions={0} | all-to-all | bytes 1048576 | tf_op jit(solution)/shard_map/all_to_all | solution.py:262
  81.7 0.9 fill.2.refs_0_
  82.7 0.4 collective-permute-start
  83.1 1.5 collective-permute-done.refs_2_
  84.6 8.5 %shard_map.58 = bf16[16,2,64,384]{3,2,1,0:T(8,128)(2,1)} custom-call(s32[1]{0:T(128)} %bitcast.member_ref, bf16[2,1024,128]{2,1,0:T(8,128)(2,1)S(1)} %fill.2.refs_0_, bf16[2,1024,384]{2,1,0:T(8,128)(2,1)} %fill.3.refs_1_, bf16[2,1024,128]{2,1,0:T(8,128)(2,1)S(1)} %collective-permute-done.refs_2_, bf16[2,1024,384]{2,1,0:T(8,128)(2,1)S(1)} %collective-permute-done.1.refs_3_), custom_call_target="tpu_custom_call" | custom-call | flops 6442450944 | bytes 8388608 | tf_op jit(solution)/shard_map/pallas_call | solution.py:218
  93.2 4.5 %all-to-all-start.3 = ((bf16[16,2,64,384]{3,2,1,0:T(8,128)(2,1)}), bf16[16,2,64,384]{3,2,1,0:T(8,128)(2,1)S(1)}, u32[]{:S(2)}, u32[]{:S(2)}) async-start(bf16[16,2,64,384]{3,2,1,0:T(8,128)(2,1)} %shard_map.58), calls=%async_computation.3 | async-start | bytes 3145728 | tf_op jit(solution)/shard_map/all_to_all | solution.py:262
  97.6 1.4 copy-done.1
  99.0 4.2 %shard_map.57 = bf16[16,2,64,128]{3,2,1,0:T(8,128)(2,1)} custom-call(s32[1]{0:T(128)} %bitcast.member_ref, bf16[2,1024,128]{2,1,0:T(8,128)(2,1)S(1)} %fill.2.refs_0_, bf16[2,1024,384]{2,1,0:T(8,128)(2,1)} %fill.3.refs_1_, bf16[2,1024,128]{2,1,0:T(8,128)(2,1)S(1)} %collective-permute-done.refs_2_, bf16[2,1024,384]{2,1,0:T(8,128)(2,1)S(1)} %copy-done.1), custom_call_target="tpu_custom_call" | custom-call | flops 2147483648 | bytes 8388608 | tf_op jit(solution)/shard_map/pallas_call | solution.py:218
  103.2 26.8 %all-to-all-done.3 = bf16[16,2,64,384]{3,2,1,0:T(8,128)(2,1)S(1)} async-done(((bf16[16,2,64,384]{3,2,1,0:T(8,128)(2,1)}), bf16[16,2,64,384]{3,2,1,0:T(8,128)(2,1)S(1)}, u32[]{:S(2)}, u32[]{:S(2)}) %all-to-all-start.3) | async-done | bytes 1572896 | tf_op jit(solution)/shard_map/all_to_all | solution.py:262
  130.0 8.6 %all-to-all-start.2 = ((bf16[16,2,64,128]{3,2,1,0:T(8,128)(2,1)}), bf16[16,2,64,128]{3,2,1,0:T(8,128)(2,1)S(1)}, u32[]{:S(2)}, u32[]{:S(2)}) async-start(bf16[16,2,64,128]{3,2,1,0:T(8,128)(2,1)} %shard_map.57), calls=%async_computation.2 | async-start | bytes 1048576 | tf_op jit(solution)/shard_map/all_to_all | solution.py:262
  138.6 9.7 %shard_map.59.refs_0_ = bf16[64,2,512,256]{3,2,1,0:T(8,128)(2,1)} custom-call(bf16[8,2,2,64,384]{4,3,2,1,0:T(8,128)(2,1)S(1)} %bitcast.24, bf16[16,256]{1,0:T(8,128)(2,1)S(1)} %reshape.145.table_ref), custom_call_target="tpu_custom_call" | custom-call | flops 402653184 | bytes 25165824 | tf_op jit(solution)/shard_map/pallas_call | solution.py:125
  148.3 4.3 %all-to-all-done.2 = bf16[16,2,64,128]{3,2,1,0:T(8,128)(2,1)S(1)} async-done(((bf16[16,2,64,128]{3,2,1,0:T(8,128)(2,1)}), bf16[16,2,64,128]{3,2,1,0:T(8,128)(2,1)S(1)}, u32[]{:S(2)}, u32[]{:S(2)}) %all-to-all-start.2) | async-done | bytes 524320 | tf_op jit(solution)/shard_map/all_to_all | solution.py:262
  152.6 3.9 %shard_map.60 = bf16[64,2,512,256]{3,2,1,0:T(8,128)(2,1)} custom-call(bf16[8,2,2,64,128]{4,3,2,1,0:T(8,128)(2,1)S(1)} %bitcast.25, bf16[16,256]{1,0:T(8,128)(2,1)S(1)} %reshape.145.table_ref, bf16[64,2,512,256]{3,2,1,0:T(8,128)(2,1)} %shard_map.59.refs_0_), custom_call_target="tpu_custom_call", output_to_operand_aliasing={{}: (2, {})} | custom-call | flops 134217728 | bytes 8388608 | tf_op jit(solution)/shard_map/pallas_call | solution.py:125
  (18 shorter events, 0.1 us)
Async XLA Ops:
  11.8 7.5 %copy-start.4 = (s32[128]{0:T(128)S(1)}, s32[128]{0:T(128)}, u32[]{:S(2)}) copy-start(s32[128]{0:T(128)} %param.6) | copy-start | bytes 1540
  11.8 8.0 %copy-start.2 = (s32[128,3]{0,1:T(4,128)S(1)}, s32[128,3]{0,1:T(4,128)}, u32[]{:S(2)}) copy-start(s32[128,3]{0,1:T(4,128)} %param.7) | copy-start | bytes 4612
  11.9 8.0 %copy-start.3 = (f32[128,3]{0,1:T(4,128)S(1)}, f32[128,3]{0,1:T(4,128)}, u32[]{:S(2)}) copy-start(f32[128,3]{0,1:T(4,128)} %param.8) | copy-start | bytes 4612
  11.9 39.9 %all-to-all-start.1 = ((bf16[16,2,64,384]{3,2,1,0:T(8,128)(2,1)}), bf16[16,2,64,384]{3,2,1,0:T(8,128)(2,1)S(1)}, u32[]{:S(2)}, u32[]{:S(2)}) async-start(bf16[16,2,64,384]{3,2,1,0:T(8,128)(2,1)} %bitcast.11), calls=%async_computation.1 | async-start | bytes 3145728 | tf_op jit(solution)/shard_map/all_to_all | solution.py:262
  54.3 30.3 %collective-permute-start.1 = (bf16[2,1024,384]{2,1,0:T(8,128)(2,1)}, bf16[2,1024,384]{2,1,0:T(8,128)(2,1)S(1)}, u32[]{:S(2)}, u32[]{:S(2)}) collective-permute-start(bf16[2,1024,384]{2,1,0:T(8,128)(2,1)} %fill.3.refs_1_), channel_id=1, source_target_pairs={{0,1},{1,0},{2,3},{3,2},{4,5},{5,4},{6,7},{7,6},{8,9},{9,8},{10,11... | collective-permute-start | bytes 4718600 | tf_op jit(solution)/shard_map/ppermute | solution.py:273
  82.7 2.0 %collective-permute-start = (bf16[2,1024,128]{2,1,0:T(8,128)(2,1)S(1)}, bf16[2,1024,128]{2,1,0:T(8,128)(2,1)S(1)}, u32[]{:S(2)}, u32[]{:S(2)}) collective-permute-start(bf16[2,1024,128]{2,1,0:T(8,128)(2,1)S(1)} %fill.2.refs_0_), channel_id=1, source_target_pairs={{0,1},{1,0},{2,3},{3,2},{4,5},{5,4},{6,7},{7,6},{8,9},{9,8},{10,11... | collective-permute-start | bytes 1572872 | tf_op jit(solution)/shard_map/ppermute | solution.py:273
  84.6 8.5 %copy-start = (bf16[2,1024,384]{2,1,0:T(8,128)(2,1)}, bf16[2,1024,384]{2,1,0:T(8,128)(2,1)S(1)}, u32[]{:S(2)}) copy-start(bf16[2,1024,384]{2,1,0:T(8,128)(2,1)S(1)} %collective-permute-done.1.refs_3_) | copy-start | bytes 4718596
  93.2 36.9 %all-to-all-start.3 = ((bf16[16,2,64,384]{3,2,1,0:T(8,128)(2,1)}), bf16[16,2,64,384]{3,2,1,0:T(8,128)(2,1)S(1)}, u32[]{:S(2)}, u32[]{:S(2)}) async-start(bf16[16,2,64,384]{3,2,1,0:T(8,128)(2,1)} %shard_map.58), calls=%async_computation.3 | async-start | bytes 3145728 | tf_op jit(solution)/shard_map/all_to_all | solution.py:262
  97.6 1.4 copy-start.1
  130.0 22.6 %all-to-all-start.2 = ((bf16[16,2,64,128]{3,2,1,0:T(8,128)(2,1)}), bf16[16,2,64,128]{3,2,1,0:T(8,128)(2,1)S(1)}, u32[]{:S(2)}, u32[]{:S(2)}) async-start(bf16[16,2,64,128]{3,2,1,0:T(8,128)(2,1)} %shard_map.57), calls=%async_computation.2 | async-start | bytes 1048576 | tf_op jit(solution)/shard_map/all_to_all | solution.py:262

commit v4 on v3

--- a/solution.py
+++ b/solution.py
@@ -11,7 +11,9 @@
 
 PARTS = 4
 OUTWARD = (1, 3)
-HOMEWARD = (3, 1)
+HOMEWARD = (1, 2, 1)
+LOOSE = 1
+LOOSE_DEVICES = 16
 STREAM_VMEM = 36 * 1024 * 1024
 VMEM_LIMIT = 24 * 1024 * 1024
 
@@ -142,6 +144,62 @@
     )(*operands)
 
 
+def loose_body(place_ref, table_ref, kept_ref, *refs, first):
+    pieces_refs, (out_ref, held_ref, planes_ref, semaphores) = refs[:-4], refs[-4:]
+    pieces, step = held_ref.shape[:2]
+    halves = out_ref.shape[1]
+    position = place_ref[0]
+    for index, piece_ref in enumerate(pieces_refs):
+        source = jnp.bitwise_xor(position, index)
+        for part in range(piece_ref.shape[0]):
+            planes_ref[source % 2, source // 2 * 2 + part] = piece_ref[part].astype(jnp.float32)
+    copies = []
+    for piece in range(pieces):
+        shot, half = piece // halves * step, piece % halves
+        for row in range(step):
+            left = planes_ref[half, :, shot + row, :].astype(jnp.bfloat16)
+            held_ref[piece, row] = lax.dot_general(
+                left, table_ref[...], (((0,), (0,)), ((), ())), preferred_element_type=jnp.float32
+            ).astype(jnp.bfloat16)
+        copy = pltpu.make_async_copy(
+            held_ref.at[piece],
+            out_ref.at[pl.ds(shot, step), half, pl.ds(first, held_ref.shape[2]), :],
+            semaphores.at[piece],
+        )
+        copy.start()
+        copies.append(copy)
+    for copy in copies:
+        copy.wait()
+
+
+def loose_inverse(place, returned, table, kept, first):
+    _, shot_rows, width = returned[0].shape
+    halves = kept.shape[1]
+    planes, samples = table.shape
+    step = shot_step(shot_rows)
+    pieces = halves * shot_rows // step
+    vmem = pl.BlockSpec(memory_space=pltpu.VMEM)
+    anywhere = pl.BlockSpec(memory_space=pl.ANY)
+    return pl.pallas_call(
+        functools.partial(loose_body, first=first),
+        in_specs=[pl.BlockSpec(memory_space=pltpu.SMEM), vmem, anywhere] + [vmem] * len(returned),
+        out_specs=anywhere,
+        out_shape=jax.ShapeDtypeStruct(kept.shape, kept.dtype),
+        scratch_shapes=[
+            pltpu.VMEM((pieces, step, width, samples), jnp.bfloat16),
+            pltpu.VMEM((halves, planes, shot_rows, width), jnp.float32),
+            pltpu.SemaphoreType.DMA((pieces,)),
+        ],
+        input_output_aliases={2: 0},
+        compiler_params=pltpu.CompilerParams(vmem_limit_bytes=STREAM_VMEM),
+        cost_estimate=pl.CostEstimate(
+            flops=2 * shot_rows * halves * width * samples * planes,
+            bytes_accessed=2 * shot_rows * halves * width * samples,
+            transcendentals=0,
+        ),
+    )(place, table, kept, *returned)
+
+
 def fill_body(spectra_ref, pick_ref, place_ref, keep_ref, out_ref):
     devices, parts, rows, width = spectra_ref.shape
     count = pick_ref.shape[0] // 2
@@ -150,7 +208,9 @@
         both = jnp.dot(pick_ref[...], recorded, preferred_element_type=jnp.float32)
         replaced = (both[:count] + both[count:]).astype(jnp.bfloat16)
         placed = jnp.dot(place_ref[...], replaced, preferred_element_type=jnp.float32)
-        out_ref[part] = (placed + recorded.astype(jnp.float32) * keep_ref[...]).astype(jnp.bfloat16)
+        out_ref[:, part * width : (part + 1) * width] = (
+            placed + recorded.astype(jnp.float32) * keep_ref[...]
+        ).astype(jnp.bfloat16)
 
 
 def fill(spectra, pick, place, keep):
@@ -158,7 +218,7 @@
     order = devices * rows
     return pl.pallas_call(
         fill_body,
-        out_shape=jax.ShapeDtypeStruct((parts, order, width), jnp.bfloat16),
+        out_shape=jax.ShapeDtypeStruct((order, parts * width), jnp.bfloat16),
         compiler_params=pltpu.CompilerParams(vmem_limit_bytes=VMEM_LIMIT),
         cost_estimate=pl.CostEstimate(
             flops=8 * pick.shape[0] * order * width,
@@ -169,65 +229,92 @@
     )(spectra, pick, place, keep)
 
 
-def product_body(member_ref, *refs, count, first, scale):
-    sources, out_ref, right_ref = refs[: 2 * count], refs[2 * count], refs[2 * count + 1]
-    devices, parts, rows, width = out_ref.shape
-    order = devices * rows
+def product_body(place_ref, *refs, count, first, width, scale, loose):
+    sources, out_refs, right_ref, total_ref = refs[: 2 * count], refs[2 * count : -2], refs[-2], refs[-1]
+    order = right_ref.shape[0] // 2
     half = order // 2
-    member = member_ref[0]
+    position = place_ref[0]
+    member = position % 2
     spans = []
     start = 0
     for ref in sources[:count]:
-        size = ref.shape[2]
+        size = ref.shape[1] // 2
         low, high = max(start, first), min(start + size, first + width)
         if low < high:
-            spans.append((ref, low - start, low - first, high - low))
+            spans.append((ref, size, low - start, low - first, high - low))
         start += size
-    for ref, begin, at, size in spans:
-        real = ref[0, :, begin : begin + size]
-        imag = ref[1, :, begin : begin + size]
-        right_ref[0, :, at : at + size] = real
-        right_ref[0, :, width + at : width + at + size] = imag
-        right_ref[1, :, at : at + size] = -imag
-        right_ref[1, :, width + at : width + at + size] = real
-    total = None
+    line = 0
     for owner in range(2):
         offset = (member if owner == 0 else 1 - member) * half
+        start = 0
+        for source in sources[:count]:
+            rows = source.shape[1] // 2
+            lines = pl.ds(pl.multiple_of(offset + start, 128), rows)
+            for ref, size, begin, at, span in spans:
+                real = ref[lines, begin : begin + span]
+                imag = ref[lines, size + begin : size + begin + span]
+                right_ref[line : line + rows, at : at + span] = real
+                right_ref[line : line + rows, width + at : width + at + span] = imag
+                right_ref[line + rows : line + 2 * rows, at : at + span] = -imag
+                right_ref[line + rows : line + 2 * rows, width + at : width + at + span] = real
+            line += 2 * rows
+            start += rows
+    block = math.gcd(order, 256)
+    for row in range(0, order, block):
+        total = None
+        line = 0
+        for ref in sources:
+            depth = ref.shape[1]
+            term = jnp.dot(
+                ref[row : row + block], right_ref[line : line + depth], preferred_element_type=jnp.float32
+            )
+            total = term if total is None else total + term
+            line += depth
+        total_ref[row : row + block] = (total * scale).astype(jnp.bfloat16)
+    if loose:
+        rows = order // len(out_refs)
+        for index, out_ref in enumerate(out_refs):
+            target = jnp.bitwise_xor(position, index)
+            lines = pl.ds(pl.multiple_of(target * rows, rows), rows)
+            for part in range(2):
+                out_ref[part] = total_ref[lines, part * width : (part + 1) * width]
+    else:
+        (out_ref,) = out_refs
+        devices, parts, rows, _ = out_ref.shape
         for part in range(parts):
-            start = 0
-            for ref in sources[owner * count : (owner + 1) * count]:
-                size = ref.shape[2]
-                rows_at = pl.multiple_of(offset + start, 128)
-                term = jnp.dot(
-                    ref[part], right_ref[part, pl.ds(rows_at, size), :], preferred_element_type=jnp.float32
-                )
-                total = term if total is None else total + term
-                start += size
-    total = total * scale
-    for part in range(parts):
-        out_ref[:, part] = (
-            total[:, part * width : (part + 1) * width]
-            .astype(jnp.bfloat16)
-            .reshape(devices, rows, width)
-        )
-
-
-def product(member, own, other, first, width, devices):
-    parts, order, _ = own[0].shape
+            out_ref[:, part] = total_ref[:, part * width : (part + 1) * width].reshape(
+                devices, rows, width
+            )
+
+
+def product(place, own, other, first, width, devices, loose):
+    order, _ = own[0].shape
+    rows = order // devices
     vmem = pl.BlockSpec(memory_space=pltpu.VMEM)
+    shape = jax.ShapeDtypeStruct((devices, 2, rows, width), jnp.bfloat16)
+    if loose:
+        shape = [jax.ShapeDtypeStruct((2, rows, width), jnp.bfloat16)] * devices
     return pl.pallas_call(
         functools.partial(
-            product_body, count=len(own), first=first, scale=-1.0 / math.sqrt(order)
+            product_body,
+            count=len(own),
+            first=first,
+            width=width,
+            scale=-1.0 / math.sqrt(order),
+            loose=loose,
         ),
         in_specs=[pl.BlockSpec(memory_space=pltpu.SMEM)] + [vmem] * (2 * len(own)),
-        out_specs=vmem,
-        out_shape=jax.ShapeDtypeStruct((devices, parts, order // devices, width), jnp.bfloat16),
-        scratch_shapes=[pltpu.VMEM((parts, order, 2 * width), jnp.bfloat16)],
+        out_specs=[vmem] * devices if loose else vmem,
+        out_shape=shape,
+        scratch_shapes=[
+            pltpu.VMEM((2 * order, 2 * width), jnp.bfloat16),
+            pltpu.VMEM((order, 2 * width), jnp.bfloat16),
+        ],
         compiler_params=pltpu.CompilerParams(vmem_limit_bytes=VMEM_LIMIT),
         cost_estimate=pl.CostEstimate(
             flops=16 * order * order * width, bytes_accessed=8 * order * order, transcendentals=0
         ),
-    )(member, *own, *other)
+    )(place, *own, *other)
 
 
 def fill_tables(missing, neighbours, weights, order):
@@ -255,7 +342,7 @@
     shot_rows, order, samples = records.shape
     half = order // 2
     bins = freq_bins.shape[0]
-    member = (position % 2).astype(jnp.int32).reshape(1)
+    place_of = position.astype(jnp.int32).reshape(1)
     pairs = [(i, i ^ 1) for i in range(devices)]
 
     def exchange(blocks):
@@ -272,11 +359,19 @@
         own.append(block)
         other.append(lax.ppermute(block, "shots", pairs))
     result = None
-    for first, width in spread(half, HOMEWARD):
-        block = product(member, own, other, first, width, devices)
-        block = exchange(block)
-        block = block.reshape(bins, 2, 2, shot_rows, width)
-        result = inverse_chunk(block, inverse, result, first, half)
+    for index, (first, width) in enumerate(spread(half, HOMEWARD)):
+        loose = index == LOOSE and devices <= LOOSE_DEVICES
+        block = product(place_of, own, other, first, width, devices, loose)
+        if loose:
+            arrived = [block[0]]
+            for step in range(1, devices):
+                route = [(i, i ^ step) for i in range(devices)]
+                arrived.append(lax.ppermute(block[step], "shots", route))
+            result = loose_inverse(place_of, arrived, inverse, result, first)
+        else:
+            block = exchange(block)
+            block = block.reshape(bins, 2, 2, shot_rows, width)
+            result = inverse_chunk(block, inverse, result, first, half)
     return result.reshape(shot_rows, order, samples)
 
 

time: 157 us -> 161 us (1.025); the launches traced: 157 us -> 159 us
  starting transfers between devices: 20.9 us -> 42.5 us
  waiting for transfers between devices: 64.2 us -> 45.5 us
    ppermute x0 -> x15, starting transfers between devices: none -> 25.8 us  [predict(): arrived.append(lax.ppermute(block[step], 'shots', route))]
    all_to_all x3, waiting for transfers between devices: 62.6 us -> 41.5 us  [exchange(): lax.all_to_all(blocks, 'shots', split_axis=0, concat_axis=0, tiled=True)]
    pallas_call x2 -> x3, Pallas kernels: 3.52 us -> 10.4 us  [the longest x1 6.84 us: loose_inverse(): pl.pallas_call(functools.partial(loose_body, first=first), in_specs=[pl.B...]
    pallas_call x2, Pallas kernels: 13.6 us -> 7.75 us  [inverse_chunk(): pl.pallas_call(functools.partial(inverse_body, first=first), in_specs=[vm...]
    all_to_all x3, starting transfers between devices: 20.5 us -> 16.2 us  [exchange(): lax.all_to_all(blocks, 'shots', split_axis=0, concat_axis=0, tiled=True)]
    ppermute x0 -> x15, waiting for transfers between devices: none -> 2.49 us  [predict(): arrived.append(lax.ppermute(block[step], 'shots', route))]
    pallas_call x2 -> x3, Pallas kernels: 12.7 us -> 12.4 us  [product(): pl.pallas_call(functools.partial(product_body, count=len(own), first=firs...]
  transfers between devices with their start and end apart: 5 -> 20, of which waited for: 4 -> 6; matrix products, arithmetic and copies ran while one was open for 1% -> 1% of each run, Pallas kernels for 12% -> 15%
where the time goes in v4:
time: 161 us; the launch traced here: 159 us
  Pallas kernels  46.2 us (29%)
  waiting for transfers between devices  45.5 us (28%)
  starting transfers between devices  42.5 us (26%)
  blocking collectives  22.7 us (14%)
    all_to_all x3, waiting for transfers between devices, exchange(): lax.all_to_all(blocks, 'shots', split_axis=0, concat_axis=0, tiled=True)  41.5 us
    ppermute x15, starting transfers between devices, predict(): arrived.append(lax.ppermute(block[step], 'shots', route))  25.8 us
    all_to_all x1, blocking collectives, exchange(): lax.all_to_all(blocks, 'shots', split_axis=0, concat_axis=0, tiled=True)  22.7 us
    all_to_all x3, starting transfers between devices, exchange(): lax.all_to_all(blocks, 'shots', split_axis=0, concat_axis=0, tiled=True)  16.2 us
    pallas_call x2, Pallas kernels, forward_chunk(): pl.pallas_call(functools.partial(forward_body, first=first), in_specs=[pl...  15.6 us
    pallas_call x3, Pallas kernels, product(): pl.pallas_call(functools.partial(product_body, count=len(own), first=firs...  12.4 us
    pallas_call x2, Pallas kernels, inverse_chunk(): pl.pallas_call(functools.partial(inverse_body, first=first), in_specs=[vm...  7.75 us
    pallas_call x1, Pallas kernels, loose_inverse(): pl.pallas_call(functools.partial(loose_body, first=first), in_specs=[pl.B...  6.84 us
  transfers between devices with their start and end apart: 20, of which 6 were waited for; matrix products, arithmetic and copies ran while one was open for 1% of the time, Pallas kernels for 15%

profile of v4, /device:TPU:1, one launch (start us, length us, event | category | flops | bytes accessed | tf_op | source)
XLA Modules:
  0.0 159.0 jit_solution(3170058319431476225)
XLA Ops:
  0.9 11.0 %shard_map.56 = bf16[8,2,2,64,384]{4,3,2,1,0:T(8,128)(2,1)} custom-call(bf16[64,2,512,256]{3,2,1,0:T(8,128)(2,1)} %bitcast.27, bf16[16,256]{1,0:T(8,128)(2,1)S(1)} %reshape.141.table_ref), custom_call_target="tpu_custom_call" | custom-call | flops 402653184 | bytes 25165824 | tf_op jit(solution)/shard_map/pallas_call | solution.py:73
  11.9 7.3 %all-to-all-start.1 = ((bf16[16,2,64,384]{3,2,1,0:T(8,128)(2,1)}), bf16[16,2,64,384]{3,2,1,0:T(8,128)(2,1)S(1)}, u32[]{:S(2)}, u32[]{:S(2)}) async-start(bf16[16,2,64,384]{3,2,1,0:T(8,128)(2,1)} %bitcast.11), calls=%async_computation.1 | async-start | bytes 3145728 | tf_op jit(solution)/shard_map/all_to_all | solution.py:349
  20.1 31.5 %all-to-all-done.1.spectra_ref = bf16[16,2,64,384]{3,2,1,0:T(8,128)(2,1)S(1)} async-done(((bf16[16,2,64,384]{3,2,1,0:T(8,128)(2,1)}), bf16[16,2,64,384]{3,2,1,0:T(8,128)(2,1)S(1)}, u32[]{:S(2)}, u32[]{:S(2)}) %all-to-all-start.1) | async-done | bytes 1572896 | tf_op jit(solution)/shard_map/all_to_all | solution.py:349
  51.6 2.6 %fill.3.refs_1_ = bf16[1024,768]{1,0:T(8,128)(2,1)} custom-call(bf16[16,2,64,384]{3,2,1,0:T(8,128)(2,1)S(1)} %all-to-all-done.1.spectra_ref, bf16[256,1024]{1,0:T(8,128)(2,1)S(1)} %pad_maximum_fusion.pick_ref, bf16[1024,128]{1,0:T(8,128)(2,1)S(1)} %get-tuple-element.48.place_ref, f32[1024,1]{1,0:T(8,128)S(1)} %copy.11.keep_ref), custom_call_target="tpu_custom_call" | custom-call | flops 805306368 | bytes 3145728 | tf_op jit(solution)/shard_map/fill/pallas_call | solution.py:219
  54.2 4.7 %shard_map.55 = bf16[8,2,2,64,128]{4,3,2,1,0:T(8,128)(2,1)S(1)} custom-call(bf16[64,2,512,256]{3,2,1,0:T(8,128)(2,1)} %bitcast.28, bf16[16,256]{1,0:T(8,128)(2,1)S(1)} %reshape.141.table_ref), custom_call_target="tpu_custom_call" | custom-call | flops 134217728 | bytes 8388608 | tf_op jit(solution)/shard_map/pallas_call | solution.py:73
  58.9 22.7 %all_to_all.20.spectra_ref = bf16[16,2,64,128]{3,2,1,0:T(8,128)(2,1)S(1)} all-to-all(bf16[16,2,64,128]{3,2,1,0:T(8,128)(2,1)S(1)} %bitcast.26), channel_id=1, replica_groups=mesh['lines'=2,'shots'=16] {'shots'}, dimensions={0} | all-to-all | bytes 1048576 | tf_op jit(solution)/shard_map/all_to_all | solution.py:349
  83.0 1.5 collective-permute-done.refs_2_
  84.5 4.1 %shard_map.58 = bf16[16,2,64,128]{3,2,1,0:T(8,128)(2,1)} custom-call(s32[1]{0:T(128)} %bitcast.place_ref, bf16[1024,256]{1,0:T(8,128)(2,1)S(1)} %fill.2.refs_0_, bf16[1024,768]{1,0:T(8,128)(2,1)} %fill.3.refs_1_, bf16[1024,256]{1,0:T(8,128)(2,1)S(1)} %collective-permute-done.refs_2_, bf16[1024,768]{1,0:T(8,128)(2,1)} %collective-permute-done.1.refs_3_), custom_call_target="tpu_custom_call" | custom-call | flops 2147483648 | bytes 8388608 | tf_op jit(solution)/shard_map/pallas_call | solution.py:297
  88.6 4.5 %all-to-all-start.3 = ((bf16[16,2,64,128]{3,2,1,0:T(8,128)(2,1)}), bf16[16,2,64,128]{3,2,1,0:T(8,128)(2,1)S(1)}, u32[]{:S(2)}, u32[]{:S(2)}) async-start(bf16[16,2,64,128]{3,2,1,0:T(8,128)(2,1)} %shard_map.58), calls=%async_computation.3 | async-start | bytes 1048576 | tf_op jit(solution)/shard_map/all_to_all | solution.py:349
  93.0 4.0 %shard_map.57 = bf16[16,2,64,128]{3,2,1,0:T(8,128)(2,1)} custom-call(s32[1]{0:T(128)} %bitcast.place_ref, bf16[1024,256]{1,0:T(8,128)(2,1)S(1)} %fill.2.refs_0_, bf16[1024,768]{1,0:T(8,128)(2,1)} %fill.3.refs_1_, bf16[1024,256]{1,0:T(8,128)(2,1)S(1)} %collective-permute-done.refs_2_, bf16[1024,768]{1,0:T(8,128)(2,1)} %collective-permute-done.1.refs_3_), custom_call_target="tpu_custom_call" | custom-call | flops 2147483648 | bytes 8388608 | tf_op jit(solution)/shard_map/pallas_call | solution.py:297
  97.1 10.0 %all-to-all-done.3 = bf16[16,2,64,128]{3,2,1,0:T(8,128)(2,1)S(1)} async-done(((bf16[16,2,64,128]{3,2,1,0:T(8,128)(2,1)}), bf16[16,2,64,128]{3,2,1,0:T(8,128)(2,1)S(1)}, u32[]{:S(2)}, u32[]{:S(2)}) %all-to-all-start.3) | async-done | bytes 524320 | tf_op jit(solution)/shard_map/all_to_all | solution.py:349
  107.1 4.4 %all-to-all-start.2 = ((bf16[16,2,64,128]{3,2,1,0:T(8,128)(2,1)}), bf16[16,2,64,128]{3,2,1,0:T(8,128)(2,1)S(1)}, u32[]{:S(2)}, u32[]{:S(2)}) async-start(bf16[16,2,64,128]{3,2,1,0:T(8,128)(2,1)} %shard_map.57), calls=%async_computation.2 | async-start | bytes 1048576 | tf_op jit(solution)/shard_map/all_to_all | solution.py:349
  111.5 4.3 %shard_map.60 = (bf16[2,64,256]{2,1,0:T(8,128)(2,1)S(1)}, bf16[2,64,256]{2,1,0:T(8,128)(2,1)S(1)}, bf16[2,64,256]{2,1,0:T(8,128)(2,1)S(1)}, bf16[2,64,256]{2,1,0...) custom-call(s32[1]{0:T(128)} %bitcast.place_ref, ...), custom_call_target="tpu_custom_call" | custom-call | flops 4294967296 | bytes 8388608 | tf_op jit(solution)/shard_map/pallas_call | solution.py:297
  119.6 2.4 %collective-permute-start.7 = (bf16[2,64,256]{2,1,0:T(8,128)(2,1)S(1)}, bf16[2,64,256]{2,1,0:T(8,128)(2,1)S(1)}, u32[]{:S(2)}, u32[]{:S(2)}) collective-permute-start(bf16[2,64,256]{2,1,0:T(8,128)(2,1)S(1)} %get-tuple-element.27), channel_id=1, source_target_pairs={{0,6},{1,7},{2,4},{3,5},{4,2},{5,3},{6,0},{7,1},{8,14},{9,15},{10,... | collective-permute-start | bytes 196616 | tf_op jit(solution)/shard_map/ppermute | solution.py:369
  122.0 1.6 %collective-permute-start.8 = (bf16[2,64,256]{2,1,0:T(8,128)(2,1)S(1)}, bf16[2,64,256]{2,1,0:T(8,128)(2,1)S(1)}, u32[]{:S(2)}, u32[]{:S(2)}) collective-permute-start(bf16[2,64,256]{2,1,0:T(8,128)(2,1)S(1)} %get-tuple-element.28), channel_id=1, source_target_pairs={{0,7},{1,6},{2,5},{3,4},{4,3},{5,2},{6,1},{7,0},{8,15},{9,14},{10,... | collective-permute-start | bytes 196616 | tf_op jit(solution)/shard_map/ppermute | solution.py:369
  123.6 2.2 %collective-permute-start.9 = (bf16[2,64,256]{2,1,0:T(8,128)(2,1)S(1)}, bf16[2,64,256]{2,1,0:T(8,128)(2,1)S(1)}, u32[]{:S(2)}, u32[]{:S(2)}) collective-permute-start(bf16[2,64,256]{2,1,0:T(8,128)(2,1)S(1)} %get-tuple-element.29), channel_id=1, source_target_pairs={{0,8},{1,9},{2,10},{3,11},{4,12},{5,13},{6,14},{7,15},{8,0},{9,1},... | collective-permute-start | bytes 196616 | tf_op jit(solution)/shard_map/ppermute | solution.py:369
  127.1 1.9 %collective-permute-start.11 = (bf16[2,64,256]{2,1,0:T(8,128)(2,1)S(1)}, bf16[2,64,256]{2,1,0:T(8,128)(2,1)S(1)}, u32[]{:S(2)}, u32[]{:S(2)}) collective-permute-start(bf16[2,64,256]{2,1,0:T(8,128)(2,1)S(1)} %get-tuple-element.31), channel_id=1, source_target_pairs={{0,10},{1,11},{2,8},{3,9},{4,14},{5,15},{6,12},{7,13},{8,2},{9,3},... | collective-permute-start | bytes 196616 | tf_op jit(solution)/shard_map/ppermute | solution.py:369
  129.0 1.8 %collective-permute-start.12 = (bf16[2,64,256]{2,1,0:T(8,128)(2,1)S(1)}, bf16[2,64,256]{2,1,0:T(8,128)(2,1)S(1)}, u32[]{:S(2)}, u32[]{:S(2)}) collective-permute-start(bf16[2,64,256]{2,1,0:T(8,128)(2,1)S(1)} %get-tuple-element.32), channel_id=1, source_target_pairs={{0,11},{1,10},{2,9},{3,8},{4,15},{5,14},{6,13},{7,12},{8,3},{9,2},... | collective-permute-start | bytes 196616 | tf_op jit(solution)/shard_map/ppermute | solution.py:369
  133.4 4.2 %collective-permute-start.14 = (bf16[2,64,256]{2,1,0:T(8,128)(2,1)S(1)}, bf16[2,64,256]{2,1,0:T(8,128)(2,1)S(1)}, u32[]{:S(2)}, u32[]{:S(2)}) collective-permute-start(bf16[2,64,256]{2,1,0:T(8,128)(2,1)S(1)} %get-tuple-element.34), channel_id=1, source_target_pairs={{0,13},{1,12},{2,15},{3,14},{4,9},{5,8},{6,11},{7,10},{8,5},{9,4},... | collective-permute-start | bytes 196616 | tf_op jit(solution)/shard_map/ppermute | solution.py:369
  138.1 2.2 %collective-permute-start.15 = (bf16[2,64,256]{2,1,0:T(8,128)(2,1)S(1)}, bf16[2,64,256]{2,1,0:T(8,128)(2,1)S(1)}, u32[]{:S(2)}, u32[]{:S(2)}) collective-permute-start(bf16[2,64,256]{2,1,0:T(8,128)(2,1)S(1)} %get-tuple-element.35), channel_id=1, source_target_pairs={{0,14},{1,15},{2,12},{3,13},{4,10},{5,11},{6,8},{7,9},{8,6},{9,7},... | collective-permute-start | bytes 196616 | tf_op jit(solution)/shard_map/ppermute | solution.py:369
  140.9 3.2 %collective-permute-start.16 = (bf16[2,64,256]{2,1,0:T(8,128)(2,1)S(1)}, bf16[2,64,256]{2,1,0:T(8,128)(2,1)S(1)}, u32[]{:S(2)}, u32[]{:S(2)}) collective-permute-start(bf16[2,64,256]{2,1,0:T(8,128)(2,1)S(1)} %get-tuple-element.36), channel_id=1, source_target_pairs={{0,15},{1,14},{2,13},{3,12},{4,11},{5,10},{6,9},{7,8},{8,7},{9,6},... | collective-permute-start | bytes 196616 | tf_op jit(solution)/shard_map/ppermute | solution.py:369
  144.1 3.9 %shard_map.59.kept_ref = bf16[64,2,512,256]{3,2,1,0:T(8,128)(2,1)} custom-call(bf16[8,2,2,64,128]{4,3,2,1,0:T(8,128)(2,1)S(1)} %bitcast.25, bf16[16,256]{1,0:T(8,128)(2,1)S(1)} %reshape.145.table_ref), custom_call_target="tpu_custom_call" | custom-call | flops 134217728 | bytes 8388608 | tf_op jit(solution)/shard_map/pallas_call | solution.py:127
  148.1 6.8 %shard_map.61.refs_0_ = bf16[64,2,512,256]{3,2,1,0:T(8,128)(2,1)} custom-call(s32[1]{0:T(128)} %bitcast.place_ref, bf16[16,256]{1,0:T(8,128)(2,1)S(1)} %reshape.145.table_ref, bf16[64,2,512,256]{3,2,1,0:T(8,128)(2,1)} %shard_map.59.kept_ref, bf16[2,64,256]{2,1,0:T(8,128)(2,1)S(1)} %get-tuple-element.21.refs_0_, ...), custom_call_target="tpu_custom_call", output_to_operand_aliasing={{}: (2, {})} | custom-call | flops 268435456 | bytes 16777216 | tf_op jit(solution)/shard_map/pallas_call | solution.py:183
  154.9 3.9 %shard_map.62 = bf16[64,2,512,256]{3,2,1,0:T(8,128)(2,1)} custom-call(bf16[8,2,2,64,128]{4,3,2,1,0:T(8,128)(2,1)S(1)} %bitcast.24, bf16[16,256]{1,0:T(8,128)(2,1)S(1)} %reshape.145.table_ref, bf16[64,2,512,256]{3,2,1,0:T(8,128)(2,1)} %shard_map.61.refs_0_), custom_call_target="tpu_custom_call", output_to_operand_aliasing={{}: (2, {})} | custom-call | flops 134217728 | bytes 8388608 | tf_op jit(solution)/shard_map/pallas_call | solution.py:127
  (46 shorter events, 11.9 us)
Async XLA Ops:
  0.0 19.2 %copy-start.2 = (s32[128]{0:T(128)S(1)}, s32[128]{0:T(128)}, u32[]{:S(2)}) copy-start(s32[128]{0:T(128)} %param.6) | copy-start | bytes 1540
  0.0 19.7 %copy-start = (s32[128,3]{0,1:T(4,128)S(1)}, s32[128,3]{0,1:T(4,128)}, u32[]{:S(2)}) copy-start(s32[128,3]{0,1:T(4,128)} %param.7) | copy-start | bytes 4612
  0.0 19.7 %copy-start.1 = (f32[128,3]{0,1:T(4,128)S(1)}, f32[128,3]{0,1:T(4,128)}, u32[]{:S(2)}) copy-start(f32[128,3]{0,1:T(4,128)} %param.8) | copy-start | bytes 4612
  11.9 39.7 %all-to-all-start.1 = ((bf16[16,2,64,384]{3,2,1,0:T(8,128)(2,1)}), bf16[16,2,64,384]{3,2,1,0:T(8,128)(2,1)S(1)}, u32[]{:S(2)}, u32[]{:S(2)}) async-start(bf16[16,2,64,384]{3,2,1,0:T(8,128)(2,1)} %bitcast.11), calls=%async_computation.1 | async-start | bytes 3145728 | tf_op jit(solution)/shard_map/all_to_all | solution.py:349
  54.2 30.3 %collective-permute-start.1 = (bf16[1024,768]{1,0:T(8,128)(2,1)}, bf16[1024,768]{1,0:T(8,128)(2,1)}, u32[]{:S(2)}, u32[]{:S(2)}) collective-permute-start(bf16[1024,768]{1,0:T(8,128)(2,1)} %fill.3.refs_1_), channel_id=1, source_target_pairs={{0,1},{1,0},{2,3},{3,2},{4,5},{5,4},{6,7},{7,6},{8,9},{9,8},{10,11... | collective-permute-start | bytes 4718600 | tf_op jit(solution)/shard_map/ppermute | solution.py:360
  82.5 2.0 %collective-permute-start = (bf16[1024,256]{1,0:T(8,128)(2,1)S(1)}, bf16[1024,256]{1,0:T(8,128)(2,1)S(1)}, u32[]{:S(2)}, u32[]{:S(2)}) collective-permute-start(bf16[1024,256]{1,0:T(8,128)(2,1)S(1)} %fill.2.refs_0_), channel_id=1, source_target_pairs={{0,1},{1,0},{2,3},{3,2},{4,5},{5,4},{6,7},{7,6},{8,9},{9,8},{10,11... | collective-permute-start | bytes 1572872 | tf_op jit(solution)/shard_map/ppermute | solution.py:360
  88.6 18.5 %all-to-all-start.3 = ((bf16[16,2,64,128]{3,2,1,0:T(8,128)(2,1)}), bf16[16,2,64,128]{3,2,1,0:T(8,128)(2,1)S(1)}, u32[]{:S(2)}, u32[]{:S(2)}) async-start(bf16[16,2,64,128]{3,2,1,0:T(8,128)(2,1)} %shard_map.58), calls=%async_computation.3 | async-start | bytes 1048576 | tf_op jit(solution)/shard_map/all_to_all | solution.py:349
  107.1 47.9 %all-to-all-start.2 = ((bf16[16,2,64,128]{3,2,1,0:T(8,128)(2,1)}), bf16[16,2,64,128]{3,2,1,0:T(8,128)(2,1)S(1)}, u32[]{:S(2)}, u32[]{:S(2)}) async-start(bf16[16,2,64,128]{3,2,1,0:T(8,128)(2,1)} %shard_map.57), calls=%async_computation.2 | async-start | bytes 1048576 | tf_op jit(solution)/shard_map/all_to_all | solution.py:349
  115.8 3.8 %collective-permute-start.2 = (bf16[2,64,256]{2,1,0:T(8,128)(2,1)S(1)}, bf16[2,64,256]{2,1,0:T(8,128)(2,1)S(1)}, u32[]{:S(2)}, u32[]{:S(2)}) collective-permute-start(bf16[2,64,256]{2,1,0:T(8,128)(2,1)S(1)} %get-tuple-element.22), channel_id=1, source_target_pairs={{0,1},{1,0},{2,3},{3,2},{4,5},{5,4},{6,7},{7,6},{8,9},{9,8},{10,11... | collective-permute-start | bytes 196616 | tf_op jit(solution)/shard_map/ppermute | solution.py:369
  116.1 5.9 %collective-permute-start.3 = (bf16[2,64,256]{2,1,0:T(8,128)(2,1)S(1)}, bf16[2,64,256]{2,1,0:T(8,128)(2,1)S(1)}, u32[]{:S(2)}, u32[]{:S(2)}) collective-permute-start(bf16[2,64,256]{2,1,0:T(8,128)(2,1)S(1)} %get-tuple-element.23), channel_id=1, source_target_pairs={{0,2},{1,3},{2,0},{3,1},{4,6},{5,7},{6,4},{7,5},{8,10},{9,11},{10,... | collective-permute-start | bytes 196616 | tf_op jit(solution)/shard_map/ppermute | solution.py:369
  117.6 6.0 %collective-permute-start.4 = (bf16[2,64,256]{2,1,0:T(8,128)(2,1)S(1)}, bf16[2,64,256]{2,1,0:T(8,128)(2,1)S(1)}, u32[]{:S(2)}, u32[]{:S(2)}) collective-permute-start(bf16[2,64,256]{2,1,0:T(8,128)(2,1)S(1)} %get-tuple-element.24), channel_id=1, source_target_pairs={{0,3},{1,2},{2,1},{3,0},{4,7},{5,6},{6,5},{7,4},{8,11},{9,10},{10,... | collective-permute-start | bytes 196616 | tf_op jit(solution)/shard_map/ppermute | solution.py:369
  118.0 7.8 %collective-permute-start.5 = (bf16[2,64,256]{2,1,0:T(8,128)(2,1)S(1)}, bf16[2,64,256]{2,1,0:T(8,128)(2,1)S(1)}, u32[]{:S(2)}, u32[]{:S(2)}) collective-permute-start(bf16[2,64,256]{2,1,0:T(8,128)(2,1)S(1)} %get-tuple-element.25), channel_id=1, source_target_pairs={{0,4},{1,5},{2,6},{3,7},{4,0},{5,1},{6,2},{7,3},{8,12},{9,13},{10,... | collective-permute-start | bytes 196616 | tf_op jit(solution)/shard_map/ppermute | solution.py:369
  119.3 7.8 %collective-permute-start.6 = (bf16[2,64,256]{2,1,0:T(8,128)(2,1)S(1)}, bf16[2,64,256]{2,1,0:T(8,128)(2,1)S(1)}, u32[]{:S(2)}, u32[]{:S(2)}) collective-permute-start(bf16[2,64,256]{2,1,0:T(8,128)(2,1)S(1)} %get-tuple-element.26), channel_id=1, source_target_pairs={{0,5},{1,4},{2,7},{3,6},{4,1},{5,0},{6,3},{7,2},{8,13},{9,12},{10,... | collective-permute-start | bytes 196616 | tf_op jit(solution)/shard_map/ppermute | solution.py:369
  119.6 9.4 %collective-permute-start.7 = (bf16[2,64,256]{2,1,0:T(8,128)(2,1)S(1)}, bf16[2,64,256]{2,1,0:T(8,128)(2,1)S(1)}, u32[]{:S(2)}, u32[]{:S(2)}) collective-permute-start(bf16[2,64,256]{2,1,0:T(8,128)(2,1)S(1)} %get-tuple-element.27), channel_id=1, source_target_pairs={{0,6},{1,7},{2,4},{3,5},{4,2},{5,3},{6,0},{7,1},{8,14},{9,15},{10,... | collective-permute-start | bytes 196616 | tf_op jit(solution)/shard_map/ppermute | solution.py:369
  122.0 10.2 %collective-permute-start.8 = (bf16[2,64,256]{2,1,0:T(8,128)(2,1)S(1)}, bf16[2,64,256]{2,1,0:T(8,128)(2,1)S(1)}, u32[]{:S(2)}, u32[]{:S(2)}) collective-permute-start(bf16[2,64,256]{2,1,0:T(8,128)(2,1)S(1)} %get-tuple-element.28), channel_id=1, source_target_pairs={{0,7},{1,6},{2,5},{3,4},{4,3},{5,2},{6,1},{7,0},{8,15},{9,14},{10,... | collective-permute-start | bytes 196616 | tf_op jit(solution)/shard_map/ppermute | solution.py:369
  123.6 9.8 %collective-permute-start.9 = (bf16[2,64,256]{2,1,0:T(8,128)(2,1)S(1)}, bf16[2,64,256]{2,1,0:T(8,128)(2,1)S(1)}, u32[]{:S(2)}, u32[]{:S(2)}) collective-permute-start(bf16[2,64,256]{2,1,0:T(8,128)(2,1)S(1)} %get-tuple-element.29), channel_id=1, source_target_pairs={{0,8},{1,9},{2,10},{3,11},{4,12},{5,13},{6,14},{7,15},{8,0},{9,1},... | collective-permute-start | bytes 196616 | tf_op jit(solution)/shard_map/ppermute | solution.py:369
  125.8 12.3 %collective-permute-start.10 = (bf16[2,64,256]{2,1,0:T(8,128)(2,1)S(1)}, bf16[2,64,256]{2,1,0:T(8,128)(2,1)S(1)}, u32[]{:S(2)}, u32[]{:S(2)}) collective-permute-start(bf16[2,64,256]{2,1,0:T(8,128)(2,1)S(1)} %get-tuple-element.30), channel_id=1, source_target_pairs={{0,9},{1,8},{2,11},{3,10},{4,13},{5,12},{6,15},{7,14},{8,1},{9,0},... | collective-permute-start | bytes 196616 | tf_op jit(solution)/shard_map/ppermute | solution.py:369
  127.1 13.8 %collective-permute-start.11 = (bf16[2,64,256]{2,1,0:T(8,128)(2,1)S(1)}, bf16[2,64,256]{2,1,0:T(8,128)(2,1)S(1)}, u32[]{:S(2)}, u32[]{:S(2)}) collective-permute-start(bf16[2,64,256]{2,1,0:T(8,128)(2,1)S(1)} %get-tuple-element.31), channel_id=1, source_target_pairs={{0,10},{1,11},{2,8},{3,9},{4,14},{5,15},{6,12},{7,13},{8,2},{9,3},... | collective-permute-start | bytes 196616 | tf_op jit(solution)/shard_map/ppermute | solution.py:369
  129.0 19.0 %collective-permute-start.12 = (bf16[2,64,256]{2,1,0:T(8,128)(2,1)S(1)}, bf16[2,64,256]{2,1,0:T(8,128)(2,1)S(1)}, u32[]{:S(2)}, u32[]{:S(2)}) collective-permute-start(bf16[2,64,256]{2,1,0:T(8,128)(2,1)S(1)} %get-tuple-element.32), channel_id=1, source_target_pairs={{0,11},{1,10},{2,9},{3,8},{4,15},{5,14},{6,13},{7,12},{8,3},{9,2},... | collective-permute-start | bytes 196616 | tf_op jit(solution)/shard_map/ppermute | solution.py:369
  132.2 15.9 %collective-permute-start.13 = (bf16[2,64,256]{2,1,0:T(8,128)(2,1)S(1)}, bf16[2,64,256]{2,1,0:T(8,128)(2,1)S(1)}, u32[]{:S(2)}, u32[]{:S(2)}) collective-permute-start(bf16[2,64,256]{2,1,0:T(8,128)(2,1)S(1)} %get-tuple-element.33), channel_id=1, source_target_pairs={{0,12},{1,13},{2,14},{3,15},{4,8},{5,9},{6,10},{7,11},{8,4},{9,5},... | collective-permute-start | bytes 196616 | tf_op jit(solution)/shard_map/ppermute | solution.py:369
  133.4 14.6 %collective-permute-start.14 = (bf16[2,64,256]{2,1,0:T(8,128)(2,1)S(1)}, bf16[2,64,256]{2,1,0:T(8,128)(2,1)S(1)}, u32[]{:S(2)}, u32[]{:S(2)}) collective-permute-start(bf16[2,64,256]{2,1,0:T(8,128)(2,1)S(1)} %get-tuple-element.34), channel_id=1, source_target_pairs={{0,13},{1,12},{2,15},{3,14},{4,9},{5,8},{6,11},{7,10},{8,5},{9,4},... | collective-permute-start | bytes 196616 | tf_op jit(solution)/shard_map/ppermute | solution.py:369
  138.1 9.9 %collective-permute-start.15 = (bf16[2,64,256]{2,1,0:T(8,128)(2,1)S(1)}, bf16[2,64,256]{2,1,0:T(8,128)(2,1)S(1)}, u32[]{:S(2)}, u32[]{:S(2)}) collective-permute-start(bf16[2,64,256]{2,1,0:T(8,128)(2,1)S(1)} %get-tuple-element.35), channel_id=1, source_target_pairs={{0,14},{1,15},{2,12},{3,13},{4,10},{5,11},{6,8},{7,9},{8,6},{9,7},... | collective-permute-start | bytes 196616 | tf_op jit(solution)/shard_map/ppermute | solution.py:369
  140.9 7.2 %collective-permute-start.16 = (bf16[2,64,256]{2,1,0:T(8,128)(2,1)S(1)}, bf16[2,64,256]{2,1,0:T(8,128)(2,1)S(1)}, u32[]{:S(2)}, u32[]{:S(2)}) collective-permute-start(bf16[2,64,256]{2,1,0:T(8,128)(2,1)S(1)} %get-tuple-element.36), channel_id=1, source_target_pairs={{0,15},{1,14},{2,13},{3,12},{4,11},{5,10},{6,9},{7,8},{8,7},{9,6},... | collective-permute-start | bytes 196616 | tf_op jit(solution)/shard_map/ppermute | solution.py:369

commit v5 on v4

--- a/solution.py
+++ b/solution.py
@@ -200,17 +200,21 @@
     )(place, table, kept, *returned)
 
 
-def fill_body(spectra_ref, pick_ref, place_ref, keep_ref, out_ref):
+def fill_into(out_ref, spectra_ref, pick_ref, put_ref, keep_ref):
     devices, parts, rows, width = spectra_ref.shape
     count = pick_ref.shape[0] // 2
     for part in range(parts):
         recorded = spectra_ref[:, part].reshape(devices * rows, width)
         both = jnp.dot(pick_ref[...], recorded, preferred_element_type=jnp.float32)
         replaced = (both[:count] + both[count:]).astype(jnp.bfloat16)
-        placed = jnp.dot(place_ref[...], replaced, preferred_element_type=jnp.float32)
-        out_ref[:, part * width : (part + 1) * width] = (
-            placed + recorded.astype(jnp.float32) * keep_ref[...]
-        ).astype(jnp.bfloat16)
+        placed = jnp.dot(put_ref[...], replaced, preferred_element_type=jnp.float32)
+        out_ref[:, part * width : (part + 1) * width] = placed.astype(jnp.bfloat16) + recorded * keep_ref[
+            ...
+        ].astype(jnp.bfloat16)
+
+
+def fill_body(spectra_ref, pick_ref, put_ref, keep_ref, out_ref):
+    fill_into(out_ref, spectra_ref, pick_ref, put_ref, keep_ref)
 
 
 def fill(spectra, pick, place, keep):
@@ -317,6 +321,89 @@
     )(place, *own, *other)
 
 
+def opening_body(place_ref, spectra_ref, pick_ref, put_ref, keep_ref, *refs, sources, scale):
+    source_refs, refs = refs[:sources], refs[sources:]
+    out_ref, filled_ref = refs[:2]
+    held_refs, (right_ref, semaphores) = refs[2:-2], refs[-2:]
+    copies = [
+        pltpu.make_async_copy(source, held, semaphores.at[index])
+        for index, (source, held) in enumerate(zip(source_refs, held_refs))
+    ]
+    for copy in copies:
+        copy.start()
+    fill_into(filled_ref, spectra_ref, pick_ref, put_ref, keep_ref)
+    for copy in copies:
+        copy.wait()
+    order = filled_ref.shape[0]
+    half = order // 2
+    _, parts, rows, width = out_ref.shape
+    count = (sources + 1) // 2
+    lefts = list(held_refs) + [filled_ref]
+    own_ref = held_refs[0]
+    member = place_ref[0] % 2
+    line = 0
+    for index, left in enumerate(lefts):
+        if index % count == 0:
+            start = (member if index == 0 else 1 - member) * half
+        depth = left.shape[1] // 2
+        lines = pl.ds(pl.multiple_of(start, 128), depth)
+        real = own_ref[lines, :width]
+        imag = own_ref[lines, width:]
+        right_ref[line : line + depth, :width] = real
+        right_ref[line : line + depth, width:] = imag
+        right_ref[line + depth : line + 2 * depth, :width] = -imag
+        right_ref[line + depth : line + 2 * depth, width:] = real
+        line += 2 * depth
+        start += depth
+    block = math.gcd(order, 256)
+    for row in range(0, order, block):
+        total = None
+        line = 0
+        for left in lefts:
+            depth = left.shape[1]
+            term = jnp.dot(
+                left[row : row + block], right_ref[line : line + depth], preferred_element_type=jnp.float32
+            )
+            total = term if total is None else total + term
+            line += depth
+        total = (total * scale).astype(jnp.bfloat16)
+        first = row // rows
+        for part in range(parts):
+            out_ref[first : first + block // rows, part] = total[
+                :, part * width : (part + 1) * width
+            ].reshape(block // rows, rows, width)
+
+
+def opening(place, spectra, pick, put, keep, own, other, devices):
+    order = keep.shape[0]
+    rows = order // devices
+    width = own[0].shape[1] // 2
+    last = spectra.shape[3]
+    held = list(own) + list(other)
+    vmem = pl.BlockSpec(memory_space=pltpu.VMEM)
+    return pl.pallas_call(
+        functools.partial(opening_body, sources=len(held), scale=-1.0 / math.sqrt(order)),
+        in_specs=[pl.BlockSpec(memory_space=pltpu.SMEM)]
+        + [vmem] * 4
+        + [pl.BlockSpec(memory_space=pl.ANY)] * len(held),
+        out_specs=[vmem, vmem],
+        out_shape=[
+            jax.ShapeDtypeStruct((devices, 2, rows, width), jnp.bfloat16),
+            jax.ShapeDtypeStruct((order, 2 * last), jnp.bfloat16),
+        ],
+        scratch_shapes=[pltpu.VMEM(array.shape, jnp.bfloat16) for array in held]
+        + [
+            pltpu.VMEM((2 * order, 2 * width), jnp.bfloat16),
+            pltpu.SemaphoreType.DMA((len(held),)),
+        ],
+        compiler_params=pltpu.CompilerParams(vmem_limit_bytes=VMEM_LIMIT),
+        cost_estimate=pl.CostEstimate(
+            flops=16 * order * order * width, bytes_accessed=8 * order * order, transcendentals=0
+        ),
+        name="opening",
+    )(place, spectra, pick, put, keep, *held)
+
+
 def fill_tables(missing, neighbours, weights, order):
     shots = jnp.arange(order, dtype=jnp.int32)
     pick = jnp.zeros((missing.shape[0], order), jnp.float32)
@@ -351,17 +438,21 @@
     forward, inverse = tables(freq_bins, samples)
     pick, place, keep = fill_tables(missing, neighbours, weights, order)
     split = records.reshape(shot_rows, 2, half, samples)
-    own, other = [], []
+    own, raw = [], []
     for first, width in spread(half, OUTWARD):
         block = forward_chunk(split, forward, first, width)
         block = exchange(block.reshape(devices, 2, shot_rows, width))
-        block = fill(block, pick, place, keep)
-        own.append(block)
-        other.append(lax.ppermute(block, "shots", pairs))
+        raw.append(lax.ppermute(block, "shots", pairs))
+        own.append(fill(block, pick, place, keep))
+    other = [fill(block, pick, place, keep) for block in raw[:-1]]
     result = None
     for index, (first, width) in enumerate(spread(half, HOMEWARD)):
         loose = index == LOOSE and devices <= LOOSE_DEVICES
-        block = product(place_of, own, other, first, width, devices, loose)
+        if index == 0:
+            block, filled = opening(place_of, raw[-1], pick, place, keep, own, other, devices)
+            other = other + [filled]
+        else:
+            block = product(place_of, own, other, first, width, devices, loose)
         if loose:
             arrived = [block[0]]
             for step in range(1, devices):

time: 161 us -> 159 us (0.988)
  blocking collectives: 22.7 us -> 0 us
  waiting for transfers between devices: 45.5 us -> 56.4 us
  local copies, waits for them, and re-layouts: 0.29 us -> 7.77 us
  starting transfers between devices: 42.5 us -> 46.4 us
    all_to_all x1 -> x0, blocking collectives: 22.7 us -> none  [exchange(): lax.all_to_all(blocks, 'shots', split_axis=0, concat_axis=0, tiled=True)]
    all_to_all x3 -> x4, starting transfers between devices: 16.2 us -> 24.8 us  [exchange(): lax.all_to_all(blocks, 'shots', split_axis=0, concat_axis=0, tiled=True)]
    pallas_call x3 -> x2, Pallas kernels: 12.4 us -> 4.58 us  [product(): pl.pallas_call(functools.partial(product_body, count=len(own), first=firs...]
    unnamed x6 -> x24, local copies, waits for them, and re-layouts: 0.01 us -> 7.49 us
    all_to_all x3 -> x4, waiting for transfers between devices: 41.5 us -> 48.2 us  [exchange(): lax.all_to_all(blocks, 'shots', split_axis=0, concat_axis=0, tiled=True)]
    pallas_call x0 -> x1, Pallas kernels: none -> 5.72 us  [opening(): pl.pallas_call(functools.partial(opening_body, sources=len(held), scale=-...]
    ppermute x15, waiting for transfers between devices: 2.49 us -> 7.97 us  [predict(): arrived.append(lax.ppermute(block[step], 'shots', route))]
    ppermute x15, starting transfers between devices: 25.8 us -> 21.1 us  [predict(): arrived.append(lax.ppermute(block[step], 'shots', route))]
  transfers between devices with their start and end apart: 20 -> 21, of which waited for: 6 -> 8; matrix products, arithmetic and copies ran while one was open for 1% -> 1% of each run, Pallas kernels for 15% -> 15%
where the time goes in v5:
time: 159 us; the launch traced here: 157 us
  waiting for transfers between devices  56.4 us (35%)
  starting transfers between devices  46.4 us (29%)
  Pallas kernels  44.7 us (28%)
  local copies, waits for them, and re-layouts  7.77 us (5%)
    all_to_all x4, waiting for transfers between devices, exchange(): lax.all_to_all(blocks, 'shots', split_axis=0, concat_axis=0, tiled=True)  48.2 us
    all_to_all x4, starting transfers between devices, exchange(): lax.all_to_all(blocks, 'shots', split_axis=0, concat_axis=0, tiled=True)  24.8 us
    ppermute x15, starting transfers between devices, predict(): arrived.append(lax.ppermute(block[step], 'shots', route))  21.1 us
    pallas_call x2, Pallas kernels, forward_chunk(): pl.pallas_call(functools.partial(forward_body, first=first), in_specs=[pl...  16.5 us
    ppermute x15, waiting for transfers between devices, predict(): arrived.append(lax.ppermute(block[step], 'shots', route))  7.97 us
    pallas_call x2, Pallas kernels, inverse_chunk(): pl.pallas_call(functools.partial(inverse_body, first=first), in_specs=[vm...  7.75 us
    unnamed x24, local copies, waits for them, and re-layouts  7.49 us
    pallas_call x1, Pallas kernels, loose_inverse(): pl.pallas_call(functools.partial(loose_body, first=first), in_specs=[pl.B...  6.82 us
  transfers between devices with their start and end apart: 21, of which 8 were waited for; matrix products, arithmetic and copies ran while one was open for 1% of the time, Pallas kernels for 15%

profile of v5, /device:TPU:1, one launch (start us, length us, event | category | flops | bytes accessed | tf_op | source)
XLA Modules:
  0.0 157.1 jit_solution(817761913541965632)
XLA Ops:
  0.8 11.0 %shard_map.56 = bf16[8,2,2,64,384]{4,3,2,1,0:T(8,128)(2,1)} custom-call(bf16[64,2,512,256]{3,2,1,0:T(8,128)(2,1)} %bitcast.26, bf16[16,256]{1,0:T(8,128)(2,1)S(1)} %reshape.141.table_ref), custom_call_target="tpu_custom_call" | custom-call | flops 402653184 | bytes 25165824 | tf_op jit(solution)/shard_map/pallas_call | solution.py:73
  11.8 7.3 %all-to-all-start.1 = ((bf16[16,2,64,384]{3,2,1,0:T(8,128)(2,1)}), bf16[16,2,64,384]{3,2,1,0:T(8,128)(2,1)S(1)}, u32[]{:S(2)}, u32[]{:S(2)}) async-start(bf16[16,2,64,384]{3,2,1,0:T(8,128)(2,1)} %bitcast.11), calls=%async_computation.1 | async-start | bytes 3145728 | tf_op jit(solution)/shard_map/all_to_all | solution.py:436
  19.2 5.5 %shard_map.55 = bf16[8,2,2,64,128]{4,3,2,1,0:T(8,128)(2,1)} custom-call(bf16[64,2,512,256]{3,2,1,0:T(8,128)(2,1)} %bitcast.27, bf16[16,256]{1,0:T(8,128)(2,1)S(1)} %reshape.141.table_ref), custom_call_target="tpu_custom_call" | custom-call | flops 134217728 | bytes 8388608 | tf_op jit(solution)/shard_map/pallas_call | solution.py:73
  24.7 26.9 %all-to-all-done.1.spectra_ref = bf16[16,2,64,384]{3,2,1,0:T(8,128)(2,1)S(1)} async-done(((bf16[16,2,64,384]{3,2,1,0:T(8,128)(2,1)}), bf16[16,2,64,384]{3,2,1,0:T(8,128)(2,1)S(1)}, u32[]{:S(2)}, u32[]{:S(2)}) %all-to-all-start.1) | async-done | bytes 1572896 | tf_op jit(solution)/shard_map/all_to_all | solution.py:436
  51.6 8.6 %all-to-all-start = ((bf16[16,2,64,128]{3,2,1,0:T(8,128)(2,1)}), bf16[16,2,64,128]{3,2,1,0:T(8,128)(2,1)S(1)}, u32[]{:S(2)}, u32[]{:S(2)}) async-start(bf16[16,2,64,128]{3,2,1,0:T(8,128)(2,1)} %bitcast.3), calls=%async_computation | async-start | bytes 1048576 | tf_op jit(solution)/shard_map/all_to_all | solution.py:436
  60.8 13.3 %all-to-all-done.spectra_ref = bf16[16,2,64,128]{3,2,1,0:T(8,128)(2,1)S(1)} async-done(((bf16[16,2,64,128]{3,2,1,0:T(8,128)(2,1)}), bf16[16,2,64,128]{3,2,1,0:T(8,128)(2,1)S(1)}, u32[]{:S(2)}, u32[]{:S(2)}) %all-to-all-start) | async-done | bytes 524320 | tf_op jit(solution)/shard_map/all_to_all | solution.py:436
  77.0 1.5 fill.4.refs_1_
  78.5 5.7 %opening.1 = (bf16[16,2,64,128]{3,2,1,0:T(8,128)(2,1)}, bf16[1024,768]{1,0:T(8,128)(2,1)S(1)}) custom-call(s32[1]{0:T(128)} %bitcast.place_ref, bf16[16,2,64,384]{3,2,1,0:T(8,128)(2,1)} %collective-permute-done.1.spectra_ref, bf16[256,1024]{1,0:T(8,128)(2,1)S(1)} %pad_maximum_fusion.pick_ref, bf16[1024,128]{1,0:T(8,128)(2,1)S(1)} %get-tuple-element.52.put_ref, ...), custom_call_target="tpu_custom_call" | custom-call | flops 2147483648 | bytes 8388608 | tf_op jit(solution)/shard_map/opening/pallas_call | solution.py:384
  85.4 4.5 %all-to-all-start.3 = ((bf16[16,2,64,128]{3,2,1,0:T(8,128)(2,1)}), bf16[16,2,64,128]{3,2,1,0:T(8,128)(2,1)S(1)}, u32[]{:S(2)}, u32[]{:S(2)}) async-start(bf16[16,2,64,128]{3,2,1,0:T(8,128)(2,1)} %get-tuple-element.24), calls=%async_computation.3 | async-start | bytes 1048576 | tf_op jit(solution)/shard_map/all_to_all | solution.py:436
  93.7 2.2 %shard_map.57 = bf16[16,2,64,128]{3,2,1,0:T(8,128)(2,1)} custom-call(s32[1]{0:T(128)} %bitcast.place_ref, bf16[1024,256]{1,0:T(8,128)(2,1)S(1)} %fill.3.refs_0_, bf16[1024,768]{1,0:T(8,128)(2,1)S(1)} %copy-done.1, bf16[1024,256]{1,0:T(8,128)(2,1)S(1)} %copy-done.4, bf16[1024,768]{1,0:T(8,128)(2,1)S(1)} %copy-done.7), custom_call_target="tpu_custom_call" | custom-call | flops 2147483648 | bytes 8388608 | tf_op jit(solution)/shard_map/pallas_call | solution.py:301
  95.9 8.0 %all-to-all-done.3 = bf16[16,2,64,128]{3,2,1,0:T(8,128)(2,1)S(1)} async-done(((bf16[16,2,64,128]{3,2,1,0:T(8,128)(2,1)}), bf16[16,2,64,128]{3,2,1,0:T(8,128)(2,1)S(1)}, u32[]{:S(2)}, u32[]{:S(2)}) %all-to-all-start.3) | async-done | bytes 524320 | tf_op jit(solution)/shard_map/all_to_all | solution.py:436
  103.9 4.4 %all-to-all-start.2 = ((bf16[16,2,64,128]{3,2,1,0:T(8,128)(2,1)}), bf16[16,2,64,128]{3,2,1,0:T(8,128)(2,1)S(1)}, u32[]{:S(2)}, u32[]{:S(2)}) async-start(bf16[16,2,64,128]{3,2,1,0:T(8,128)(2,1)} %shard_map.57), calls=%async_computation.2 | async-start | bytes 1048576 | tf_op jit(solution)/shard_map/all_to_all | solution.py:436
  110.8 2.4 %shard_map.59 = (bf16[2,64,256]{2,1,0:T(8,128)(2,1)S(1)}, bf16[2,64,256]{2,1,0:T(8,128)(2,1)S(1)}, bf16[2,64,256]{2,1,0:T(8,128)(2,1)S(1)}, bf16[2,64,256]{2,1,0...) custom-call(s32[1]{0:T(128)} %bitcast.place_ref, ...), custom_call_target="tpu_custom_call" | custom-call | flops 4294967296 | bytes 8388608 | tf_op jit(solution)/shard_map/pallas_call | solution.py:301
  117.1 2.3 %collective-permute-start.7 = (bf16[2,64,256]{2,1,0:T(8,128)(2,1)S(1)}, bf16[2,64,256]{2,1,0:T(8,128)(2,1)S(1)}, u32[]{:S(2)}, u32[]{:S(2)}) collective-permute-start(bf16[2,64,256]{2,1,0:T(8,128)(2,1)S(1)} %get-tuple-element.31), channel_id=1, source_target_pairs={{0,6},{1,7},{2,4},{3,5},{4,2},{5,3},{6,0},{7,1},{8,14},{9,15},{10,... | collective-permute-start | bytes 196616 | tf_op jit(solution)/shard_map/ppermute | solution.py:460
  119.4 1.8 %collective-permute-start.8 = (bf16[2,64,256]{2,1,0:T(8,128)(2,1)S(1)}, bf16[2,64,256]{2,1,0:T(8,128)(2,1)S(1)}, u32[]{:S(2)}, u32[]{:S(2)}) collective-permute-start(bf16[2,64,256]{2,1,0:T(8,128)(2,1)S(1)} %get-tuple-element.32), channel_id=1, source_target_pairs={{0,7},{1,6},{2,5},{3,4},{4,3},{5,2},{6,1},{7,0},{8,15},{9,14},{10,... | collective-permute-start | bytes 196616 | tf_op jit(solution)/shard_map/ppermute | solution.py:460
  121.2 2.8 %collective-permute-start.9 = (bf16[2,64,256]{2,1,0:T(8,128)(2,1)S(1)}, bf16[2,64,256]{2,1,0:T(8,128)(2,1)S(1)}, u32[]{:S(2)}, u32[]{:S(2)}) collective-permute-start(bf16[2,64,256]{2,1,0:T(8,128)(2,1)S(1)} %get-tuple-element.33), channel_id=1, source_target_pairs={{0,8},{1,9},{2,10},{3,11},{4,12},{5,13},{6,14},{7,15},{8,0},{9,1},... | collective-permute-start | bytes 196616 | tf_op jit(solution)/shard_map/ppermute | solution.py:460
  124.0 3.1 %collective-permute-start.11 = (bf16[2,64,256]{2,1,0:T(8,128)(2,1)S(1)}, bf16[2,64,256]{2,1,0:T(8,128)(2,1)S(1)}, u32[]{:S(2)}, u32[]{:S(2)}) collective-permute-start(bf16[2,64,256]{2,1,0:T(8,128)(2,1)S(1)} %get-tuple-element.35), channel_id=1, source_target_pairs={{0,10},{1,11},{2,8},{3,9},{4,14},{5,15},{6,12},{7,13},{8,2},{9,3},... | collective-permute-start | bytes 196616 | tf_op jit(solution)/shard_map/ppermute | solution.py:460
  128.4 1.8 %collective-permute-start.13 = (bf16[2,64,256]{2,1,0:T(8,128)(2,1)S(1)}, bf16[2,64,256]{2,1,0:T(8,128)(2,1)S(1)}, u32[]{:S(2)}, u32[]{:S(2)}) collective-permute-start(bf16[2,64,256]{2,1,0:T(8,128)(2,1)S(1)} %get-tuple-element.37), channel_id=1, source_target_pairs={{0,12},{1,13},{2,14},{3,15},{4,8},{5,9},{6,10},{7,11},{8,4},{9,5},... | collective-permute-start | bytes 196616 | tf_op jit(solution)/shard_map/ppermute | solution.py:460
  130.2 1.7 %collective-permute-start.14 = (bf16[2,64,256]{2,1,0:T(8,128)(2,1)S(1)}, bf16[2,64,256]{2,1,0:T(8,128)(2,1)S(1)}, u32[]{:S(2)}, u32[]{:S(2)}) collective-permute-start(bf16[2,64,256]{2,1,0:T(8,128)(2,1)S(1)} %get-tuple-element.38), channel_id=1, source_target_pairs={{0,13},{1,12},{2,15},{3,14},{4,9},{5,8},{6,11},{7,10},{8,5},{9,4},... | collective-permute-start | bytes 196616 | tf_op jit(solution)/shard_map/ppermute | solution.py:460
  131.9 4.8 %collective-permute-done.10.refs_9_ = bf16[2,64,256]{2,1,0:T(8,128)(2,1)S(1)} collective-permute-done((bf16[2,64,256]{2,1,0:T(8,128)(2,1)S(1)}, bf16[2,64,256]{2,1,0:T(8,128)(2,1)S(1)}, u32[]{:S(2)}, u32[]{:S(2)}) %collective-permute-start.10) | collective-permute-done | bytes 65568 | tf_op jit(solution)/shard_map/ppermute | solution.py:460
  139.0 1.9 %collective-permute-start.16 = (bf16[2,64,256]{2,1,0:T(8,128)(2,1)S(1)}, bf16[2,64,256]{2,1,0:T(8,128)(2,1)S(1)}, u32[]{:S(2)}, u32[]{:S(2)}) collective-permute-start(bf16[2,64,256]{2,1,0:T(8,128)(2,1)S(1)} %get-tuple-element.40), channel_id=1, source_target_pairs={{0,15},{1,14},{2,13},{3,12},{4,11},{5,10},{6,9},{7,8},{8,7},{9,6},... | collective-permute-start | bytes 196616 | tf_op jit(solution)/shard_map/ppermute | solution.py:460
  140.9 3.9 %shard_map.58.kept_ref = bf16[64,2,512,256]{3,2,1,0:T(8,128)(2,1)} custom-call(bf16[8,2,2,64,128]{4,3,2,1,0:T(8,128)(2,1)S(1)} %bitcast.25, bf16[16,256]{1,0:T(8,128)(2,1)S(1)} %reshape.145.table_ref), custom_call_target="tpu_custom_call" | custom-call | flops 134217728 | bytes 8388608 | tf_op jit(solution)/shard_map/pallas_call | solution.py:127
  146.2 6.8 %shard_map.60.refs_0_ = bf16[64,2,512,256]{3,2,1,0:T(8,128)(2,1)} custom-call(s32[1]{0:T(128)} %bitcast.place_ref, bf16[16,256]{1,0:T(8,128)(2,1)S(1)} %reshape.145.table_ref, bf16[64,2,512,256]{3,2,1,0:T(8,128)(2,1)} %shard_map.58.kept_ref, bf16[2,64,256]{2,1,0:T(8,128)(2,1)S(1)} %get-tuple-element.25.refs_0_, ...), custom_call_target="tpu_custom_call", output_to_operand_aliasing={{}: (2, {})} | custom-call | flops 268435456 | bytes 16777216 | tf_op jit(solution)/shard_map/pallas_call | solution.py:183
  153.1 3.9 %shard_map.61 = bf16[64,2,512,256]{3,2,1,0:T(8,128)(2,1)} custom-call(bf16[8,2,2,64,128]{4,3,2,1,0:T(8,128)(2,1)S(1)} %bitcast.24, bf16[16,256]{1,0:T(8,128)(2,1)S(1)} %reshape.145.table_ref, bf16[64,2,512,256]{3,2,1,0:T(8,128)(2,1)} %shard_map.60.refs_0_), custom_call_target="tpu_custom_call", output_to_operand_aliasing={{}: (2, {})} | custom-call | flops 134217728 | bytes 8388608 | tf_op jit(solution)/shard_map/pallas_call | solution.py:127
  (66 shorter events, 20.7 us)
Async XLA Ops:
  11.8 39.7 %all-to-all-start.1 = ((bf16[16,2,64,384]{3,2,1,0:T(8,128)(2,1)}), bf16[16,2,64,384]{3,2,1,0:T(8,128)(2,1)S(1)}, u32[]{:S(2)}, u32[]{:S(2)}) async-start(bf16[16,2,64,384]{3,2,1,0:T(8,128)(2,1)} %bitcast.11), calls=%async_computation.1 | async-start | bytes 3145728 | tf_op jit(solution)/shard_map/all_to_all | solution.py:436
  19.2 41.1 %copy-start.11 = (s32[128]{0:T(128)S(1)}, s32[128]{0:T(128)}, u32[]{:S(2)}) copy-start(s32[128]{0:T(128)} %param.6) | copy-start | bytes 1540
  24.6 36.1 %copy-start.9 = (s32[128,3]{0,1:T(4,128)S(1)}, s32[128,3]{0,1:T(4,128)}, u32[]{:S(2)}) copy-start(s32[128,3]{0,1:T(4,128)} %param.7) | copy-start | bytes 4612
  24.6 49.8 %copy-start.10 = (f32[128,3]{0,1:T(4,128)S(1)}, f32[128,3]{0,1:T(4,128)}, u32[]{:S(2)}) copy-start(f32[128,3]{0,1:T(4,128)} %param.8) | copy-start | bytes 4612
  51.6 22.6 %all-to-all-start = ((bf16[16,2,64,128]{3,2,1,0:T(8,128)(2,1)}), bf16[16,2,64,128]{3,2,1,0:T(8,128)(2,1)S(1)}, u32[]{:S(2)}, u32[]{:S(2)}) async-start(bf16[16,2,64,128]{3,2,1,0:T(8,128)(2,1)} %bitcast.3), calls=%async_computation | async-start | bytes 1048576 | tf_op jit(solution)/shard_map/all_to_all | solution.py:436
  60.1 18.4 %collective-permute-start.1 = (bf16[16,2,64,384]{3,2,1,0:T(8,128)(2,1)S(1)}, bf16[16,2,64,384]{3,2,1,0:T(8,128)(2,1)}, u32[]{:S(2)}, u32[]{:S(2)}) collective-permute-start(bf16[16,2,64,384]{3,2,1,0:T(8,128)(2,1)S(1)} %all-to-all-done.1.spectra_ref), channel_id=1, source_target_pairs={{0,1},{1,0},{2,3},{3,2},{4,5},{5,4},{6,7},{7,6},{8,9},{9,8},{10,11... | collective-permute-start | bytes 4718600 | tf_op jit(solution)/shard_map/ppermute | solution.py:445
  74.1 1.9 %collective-permute-start = (bf16[16,2,64,128]{3,2,1,0:T(8,128)(2,1)S(1)}, bf16[16,2,64,128]{3,2,1,0:T(8,128)(2,1)S(1)}, u32[]{:S(2)}, u32[]{:S(2)}) collective-permute-start(bf16[16,2,64,128]{3,2,1,0:T(8,128)(2,1)S(1)} %all-to-all-done.spectra_ref), channel_id=1, source_target_pairs={{0,1},{1,0},{2,3},{3,2},{4,5},{5,4},{6,7},{7,6},{8,9},{9,8},{10,11... | collective-permute-start | bytes 1572872 | tf_op jit(solution)/shard_map/ppermute | solution.py:445
  85.4 18.5 %all-to-all-start.3 = ((bf16[16,2,64,128]{3,2,1,0:T(8,128)(2,1)}), bf16[16,2,64,128]{3,2,1,0:T(8,128)(2,1)S(1)}, u32[]{:S(2)}, u32[]{:S(2)}) async-start(bf16[16,2,64,128]{3,2,1,0:T(8,128)(2,1)} %get-tuple-element.24), calls=%async_computation.3 | async-start | bytes 1048576 | tf_op jit(solution)/shard_map/all_to_all | solution.py:436
  103.9 49.2 %all-to-all-start.2 = ((bf16[16,2,64,128]{3,2,1,0:T(8,128)(2,1)}), bf16[16,2,64,128]{3,2,1,0:T(8,128)(2,1)S(1)}, u32[]{:S(2)}, u32[]{:S(2)}) async-start(bf16[16,2,64,128]{3,2,1,0:T(8,128)(2,1)} %shard_map.57), calls=%async_computation.2 | async-start | bytes 1048576 | tf_op jit(solution)/shard_map/all_to_all | solution.py:436
  113.2 3.9 %collective-permute-start.2 = (bf16[2,64,256]{2,1,0:T(8,128)(2,1)S(1)}, bf16[2,64,256]{2,1,0:T(8,128)(2,1)S(1)}, u32[]{:S(2)}, u32[]{:S(2)}) collective-permute-start(bf16[2,64,256]{2,1,0:T(8,128)(2,1)S(1)} %get-tuple-element.26), channel_id=1, source_target_pairs={{0,1},{1,0},{2,3},{3,2},{4,5},{5,4},{6,7},{7,6},{8,9},{9,8},{10,11... | collective-permute-start | bytes 196616 | tf_op jit(solution)/shard_map/ppermute | solution.py:460
  113.6 5.8 %collective-permute-start.3 = (bf16[2,64,256]{2,1,0:T(8,128)(2,1)S(1)}, bf16[2,64,256]{2,1,0:T(8,128)(2,1)S(1)}, u32[]{:S(2)}, u32[]{:S(2)}) collective-permute-start(bf16[2,64,256]{2,1,0:T(8,128)(2,1)S(1)} %get-tuple-element.27), channel_id=1, source_target_pairs={{0,2},{1,3},{2,0},{3,1},{4,6},{5,7},{6,4},{7,5},{8,10},{9,11},{10,... | collective-permute-start | bytes 196616 | tf_op jit(solution)/shard_map/ppermute | solution.py:460
  115.0 6.2 %collective-permute-start.4 = (bf16[2,64,256]{2,1,0:T(8,128)(2,1)S(1)}, bf16[2,64,256]{2,1,0:T(8,128)(2,1)S(1)}, u32[]{:S(2)}, u32[]{:S(2)}) collective-permute-start(bf16[2,64,256]{2,1,0:T(8,128)(2,1)S(1)} %get-tuple-element.28), channel_id=1, source_target_pairs={{0,3},{1,2},{2,1},{3,0},{4,7},{5,6},{6,5},{7,4},{8,11},{9,10},{10,... | collective-permute-start | bytes 196616 | tf_op jit(solution)/shard_map/ppermute | solution.py:460
  115.4 8.6 %collective-permute-start.5 = (bf16[2,64,256]{2,1,0:T(8,128)(2,1)S(1)}, bf16[2,64,256]{2,1,0:T(8,128)(2,1)S(1)}, u32[]{:S(2)}, u32[]{:S(2)}) collective-permute-start(bf16[2,64,256]{2,1,0:T(8,128)(2,1)S(1)} %get-tuple-element.29), channel_id=1, source_target_pairs={{0,4},{1,5},{2,6},{3,7},{4,0},{5,1},{6,2},{7,3},{8,12},{9,13},{10,... | collective-permute-start | bytes 196616 | tf_op jit(solution)/shard_map/ppermute | solution.py:460
  116.8 7.2 %collective-permute-start.6 = (bf16[2,64,256]{2,1,0:T(8,128)(2,1)S(1)}, bf16[2,64,256]{2,1,0:T(8,128)(2,1)S(1)}, u32[]{:S(2)}, u32[]{:S(2)}) collective-permute-start(bf16[2,64,256]{2,1,0:T(8,128)(2,1)S(1)} %get-tuple-element.30), channel_id=1, source_target_pairs={{0,5},{1,4},{2,7},{3,6},{4,1},{5,0},{6,3},{7,2},{8,13},{9,12},{10,... | collective-permute-start | bytes 196616 | tf_op jit(solution)/shard_map/ppermute | solution.py:460
  117.1 10.0 %collective-permute-start.7 = (bf16[2,64,256]{2,1,0:T(8,128)(2,1)S(1)}, bf16[2,64,256]{2,1,0:T(8,128)(2,1)S(1)}, u32[]{:S(2)}, u32[]{:S(2)}) collective-permute-start(bf16[2,64,256]{2,1,0:T(8,128)(2,1)S(1)} %get-tuple-element.31), channel_id=1, source_target_pairs={{0,6},{1,7},{2,4},{3,5},{4,2},{5,3},{6,0},{7,1},{8,14},{9,15},{10,... | collective-permute-start | bytes 196616 | tf_op jit(solution)/shard_map/ppermute | solution.py:460
  119.4 9.0 %collective-permute-start.8 = (bf16[2,64,256]{2,1,0:T(8,128)(2,1)S(1)}, bf16[2,64,256]{2,1,0:T(8,128)(2,1)S(1)}, u32[]{:S(2)}, u32[]{:S(2)}) collective-permute-start(bf16[2,64,256]{2,1,0:T(8,128)(2,1)S(1)} %get-tuple-element.32), channel_id=1, source_target_pairs={{0,7},{1,6},{2,5},{3,4},{4,3},{5,2},{6,1},{7,0},{8,15},{9,14},{10,... | collective-permute-start | bytes 196616 | tf_op jit(solution)/shard_map/ppermute | solution.py:460
  121.2 9.0 %collective-permute-start.9 = (bf16[2,64,256]{2,1,0:T(8,128)(2,1)S(1)}, bf16[2,64,256]{2,1,0:T(8,128)(2,1)S(1)}, u32[]{:S(2)}, u32[]{:S(2)}) collective-permute-start(bf16[2,64,256]{2,1,0:T(8,128)(2,1)S(1)} %get-tuple-element.33), channel_id=1, source_target_pairs={{0,8},{1,9},{2,10},{3,11},{4,12},{5,13},{6,14},{7,15},{8,0},{9,1},... | collective-permute-start | bytes 196616 | tf_op jit(solution)/shard_map/ppermute | solution.py:460
  124.0 12.7 %collective-permute-start.10 = (bf16[2,64,256]{2,1,0:T(8,128)(2,1)S(1)}, bf16[2,64,256]{2,1,0:T(8,128)(2,1)S(1)}, u32[]{:S(2)}, u32[]{:S(2)}) collective-permute-start(bf16[2,64,256]{2,1,0:T(8,128)(2,1)S(1)} %get-tuple-element.34), channel_id=1, source_target_pairs={{0,9},{1,8},{2,11},{3,10},{4,13},{5,12},{6,15},{7,14},{8,1},{9,0},... | collective-permute-start | bytes 196616 | tf_op jit(solution)/shard_map/ppermute | solution.py:460
  124.0 15.0 %collective-permute-start.11 = (bf16[2,64,256]{2,1,0:T(8,128)(2,1)S(1)}, bf16[2,64,256]{2,1,0:T(8,128)(2,1)S(1)}, u32[]{:S(2)}, u32[]{:S(2)}) collective-permute-start(bf16[2,64,256]{2,1,0:T(8,128)(2,1)S(1)} %get-tuple-element.35), channel_id=1, source_target_pairs={{0,10},{1,11},{2,8},{3,9},{4,14},{5,15},{6,12},{7,13},{8,2},{9,3},... | collective-permute-start | bytes 196616 | tf_op jit(solution)/shard_map/ppermute | solution.py:460
  127.1 17.7 %collective-permute-start.12 = (bf16[2,64,256]{2,1,0:T(8,128)(2,1)S(1)}, bf16[2,64,256]{2,1,0:T(8,128)(2,1)S(1)}, u32[]{:S(2)}, u32[]{:S(2)}) collective-permute-start(bf16[2,64,256]{2,1,0:T(8,128)(2,1)S(1)} %get-tuple-element.36), channel_id=1, source_target_pairs={{0,11},{1,10},{2,9},{3,8},{4,15},{5,14},{6,13},{7,12},{8,3},{9,2},... | collective-permute-start | bytes 196616 | tf_op jit(solution)/shard_map/ppermute | solution.py:460
  128.4 16.4 %collective-permute-start.13 = (bf16[2,64,256]{2,1,0:T(8,128)(2,1)S(1)}, bf16[2,64,256]{2,1,0:T(8,128)(2,1)S(1)}, u32[]{:S(2)}, u32[]{:S(2)}) collective-permute-start(bf16[2,64,256]{2,1,0:T(8,128)(2,1)S(1)} %get-tuple-element.37), channel_id=1, source_target_pairs={{0,12},{1,13},{2,14},{3,15},{4,8},{5,9},{6,10},{7,11},{8,4},{9,5},... | collective-permute-start | bytes 196616 | tf_op jit(solution)/shard_map/ppermute | solution.py:460
  130.2 14.6 %collective-permute-start.14 = (bf16[2,64,256]{2,1,0:T(8,128)(2,1)S(1)}, bf16[2,64,256]{2,1,0:T(8,128)(2,1)S(1)}, u32[]{:S(2)}, u32[]{:S(2)}) collective-permute-start(bf16[2,64,256]{2,1,0:T(8,128)(2,1)S(1)} %get-tuple-element.38), channel_id=1, source_target_pairs={{0,13},{1,12},{2,15},{3,14},{4,9},{5,8},{6,11},{7,10},{8,5},{9,4},... | collective-permute-start | bytes 196616 | tf_op jit(solution)/shard_map/ppermute | solution.py:460
  136.7 8.1 %collective-permute-start.15 = (bf16[2,64,256]{2,1,0:T(8,128)(2,1)S(1)}, bf16[2,64,256]{2,1,0:T(8,128)(2,1)S(1)}, u32[]{:S(2)}, u32[]{:S(2)}) collective-permute-start(bf16[2,64,256]{2,1,0:T(8,128)(2,1)S(1)} %get-tuple-element.39), channel_id=1, source_target_pairs={{0,14},{1,15},{2,12},{3,13},{4,10},{5,11},{6,8},{7,9},{8,6},{9,7},... | collective-permute-start | bytes 196616 | tf_op jit(solution)/shard_map/ppermute | solution.py:460
  139.0 7.2 %collective-permute-start.16 = (bf16[2,64,256]{2,1,0:T(8,128)(2,1)S(1)}, bf16[2,64,256]{2,1,0:T(8,128)(2,1)S(1)}, u32[]{:S(2)}, u32[]{:S(2)}) collective-permute-start(bf16[2,64,256]{2,1,0:T(8,128)(2,1)S(1)} %get-tuple-element.40), channel_id=1, source_target_pairs={{0,15},{1,14},{2,13},{3,12},{4,11},{5,10},{6,9},{7,8},{8,7},{9,6},... | collective-permute-start | bytes 196616 | tf_op jit(solution)/shard_map/ppermute | solution.py:460
  (9 other events, 29.3 us)

commit v6 on v5

--- a/solution.py
+++ b/solution.py
@@ -12,8 +12,9 @@
 PARTS = 4
 OUTWARD = (1, 3)
 HOMEWARD = (1, 2, 1)
-LOOSE = 1
 LOOSE_DEVICES = 16
+CLOSING_VMEM = 62 * 1024 * 1024
+OPENING_VMEM = 60 * 1024 * 1024
 STREAM_VMEM = 36 * 1024 * 1024
 VMEM_LIMIT = 24 * 1024 * 1024
 
@@ -34,7 +35,9 @@
     return math.gcd(shot_rows, 16)
 
 
-def forward_body(records_ref, table_ref, out_ref, held_ref, rows_ref, semaphores, *, first):
+def forward_body(
+    records_ref, table_ref, out_ref, held_ref, rows_ref, sent_ref, semaphores, leaving, *, first
+):
     pieces, step, width, samples = held_ref.shape
     planes = table_ref.shape[0]
     halves = records_ref.shape[1]
@@ -59,9 +62,15 @@
         )
         for row in range(step):
             rows_ref[:, row, :] = spectra[:, row * width : (row + 1) * width]
-        out_ref[:, half, :, shot : shot + step, :] = (
-            rows_ref[...].astype(jnp.bfloat16).reshape(planes // 2, 2, step, width)
-        )
+        sent_ref[piece] = rows_ref[...].astype(jnp.bfloat16).reshape(planes // 2, 2, step, width)
+        copies[piece] = pltpu.make_async_copy(
+            sent_ref.at[piece],
+            out_ref.at[:, half, :, pl.ds(shot, step), :],
+            leaving.at[piece],
+        )
+        copies[piece].start()
+    for copy in copies:
+        copy.wait()
 
 
 def forward_chunk(records, table, first, width):
@@ -73,11 +82,13 @@
     return pl.pallas_call(
         functools.partial(forward_body, first=first),
         in_specs=[pl.BlockSpec(memory_space=pl.ANY), vmem],
-        out_specs=vmem,
+        out_specs=pl.BlockSpec(memory_space=pl.ANY),
         out_shape=jax.ShapeDtypeStruct((planes // 2, halves, 2, shot_rows, width), jnp.bfloat16),
         scratch_shapes=[
             pltpu.VMEM((pieces, step, width, samples), jnp.bfloat16),
             pltpu.VMEM((planes, step, width), jnp.float32),
+            pltpu.VMEM((pieces, planes // 2, 2, step, width), jnp.bfloat16),
+            pltpu.SemaphoreType.DMA((pieces,)),
             pltpu.SemaphoreType.DMA((pieces,)),
         ],
         compiler_params=pltpu.CompilerParams(vmem_limit_bytes=STREAM_VMEM),
@@ -233,98 +244,106 @@
     )(spectra, pick, place, keep)
 
 
-def product_body(place_ref, *refs, count, first, width, scale, loose):
-    sources, out_refs, right_ref, total_ref = refs[: 2 * count], refs[2 * count : -2], refs[-2], refs[-1]
-    order = right_ref.shape[0] // 2
+def closing_body(place_ref, *refs, sources, middle, scale):
+    source_refs, refs = refs[:sources], refs[sources:]
+    held_refs, (right_ref, total_ref, semaphores) = refs[-sources - 3 : -3], refs[-3:]
+    out_refs = refs[: -sources - 3]
+    count = sources // 2
+    column_ref = held_refs[count - 1]
+    order = column_ref.shape[0]
     half = order // 2
+    width = column_ref.shape[1] // 2
     position = place_ref[0]
     member = position % 2
-    spans = []
-    start = 0
-    for ref in sources[:count]:
-        size = ref.shape[1] // 2
-        low, high = max(start, first), min(start + size, first + width)
-        if low < high:
-            spans.append((ref, size, low - start, low - first, high - low))
-        start += size
+    copies = [
+        pltpu.make_async_copy(source, held, semaphores.at[index])
+        for index, (source, held) in enumerate(zip(source_refs, held_refs))
+    ]
+    for index in [count - 1] + [index for index in range(sources) if index != count - 1]:
+        copies[index].start()
+    copies[count - 1].wait()
     line = 0
-    for owner in range(2):
-        offset = (member if owner == 0 else 1 - member) * half
-        start = 0
-        for source in sources[:count]:
-            rows = source.shape[1] // 2
-            lines = pl.ds(pl.multiple_of(offset + start, 128), rows)
-            for ref, size, begin, at, span in spans:
-                real = ref[lines, begin : begin + span]
-                imag = ref[lines, size + begin : size + begin + span]
-                right_ref[line : line + rows, at : at + span] = real
-                right_ref[line : line + rows, width + at : width + at + span] = imag
-                right_ref[line + rows : line + 2 * rows, at : at + span] = -imag
-                right_ref[line + rows : line + 2 * rows, width + at : width + at + span] = real
-            line += 2 * rows
-            start += rows
-    block = math.gcd(order, 256)
+    for index, left in enumerate(held_refs):
+        if index % count == 0:
+            start = (member if index == 0 else 1 - member) * half
+        depth = left.shape[1] // 2
+        lines = pl.ds(pl.multiple_of(start, 128), depth)
+        real = column_ref[lines, :width]
+        imag = column_ref[lines, width:]
+        right_ref[line : line + depth, :width] = real
+        right_ref[line : line + depth, width:] = imag
+        right_ref[line + depth : line + 2 * depth, :width] = -imag
+        right_ref[line + depth : line + 2 * depth, width:] = real
+        line += 2 * depth
+        start += depth
+    for index in range(sources):
+        if index != count - 1:
+            copies[index].wait()
+    block = math.gcd(order, 512)
     for row in range(0, order, block):
         total = None
         line = 0
-        for ref in sources:
-            depth = ref.shape[1]
+        for left in held_refs:
+            depth = left.shape[1]
             term = jnp.dot(
-                ref[row : row + block], right_ref[line : line + depth], preferred_element_type=jnp.float32
+                left[row : row + block], right_ref[line : line + depth], preferred_element_type=jnp.float32
             )
             total = term if total is None else total + term
             line += depth
         total_ref[row : row + block] = (total * scale).astype(jnp.bfloat16)
-    if loose:
-        rows = order // len(out_refs)
-        for index, out_ref in enumerate(out_refs):
+    last_ref = out_refs[-1]
+    devices, parts, rows, _ = last_ref.shape
+    for part in range(parts):
+        begin = part * width
+        last_ref[:, part] = total_ref[:, begin + middle : begin + width].reshape(
+            devices, rows, width - middle
+        )
+        if len(out_refs) == 2:
+            out_refs[0][:, part] = total_ref[:, begin : begin + middle].reshape(devices, rows, middle)
+            continue
+        for index, out_ref in enumerate(out_refs[:-1]):
             target = jnp.bitwise_xor(position, index)
             lines = pl.ds(pl.multiple_of(target * rows, rows), rows)
-            for part in range(2):
-                out_ref[part] = total_ref[lines, part * width : (part + 1) * width]
-    else:
-        (out_ref,) = out_refs
-        devices, parts, rows, _ = out_ref.shape
-        for part in range(parts):
-            out_ref[:, part] = total_ref[:, part * width : (part + 1) * width].reshape(
-                devices, rows, width
-            )
-
-
-def product(place, own, other, first, width, devices, loose):
-    order, _ = own[0].shape
+            out_ref[part] = total_ref[lines, begin : begin + middle]
+
+
+def closing(place, own, other, middle, devices, loose):
+    order, columns = own[-1].shape
     rows = order // devices
+    width = columns // 2
+    held = list(own) + list(other)
     vmem = pl.BlockSpec(memory_space=pltpu.VMEM)
-    shape = jax.ShapeDtypeStruct((devices, 2, rows, width), jnp.bfloat16)
+    blocks = lambda size: jax.ShapeDtypeStruct((devices, 2, rows, size), jnp.bfloat16)
+    shapes = [blocks(middle)]
     if loose:
-        shape = [jax.ShapeDtypeStruct((2, rows, width), jnp.bfloat16)] * devices
+        shapes = [jax.ShapeDtypeStruct((2, rows, middle), jnp.bfloat16)] * devices
+    shapes = shapes + [blocks(width - middle)]
     return pl.pallas_call(
         functools.partial(
-            product_body,
-            count=len(own),
-            first=first,
-            width=width,
-            scale=-1.0 / math.sqrt(order),
-            loose=loose,
-        ),
-        in_specs=[pl.BlockSpec(memory_space=pltpu.SMEM)] + [vmem] * (2 * len(own)),
-        out_specs=[vmem] * devices if loose else vmem,
-        out_shape=shape,
-        scratch_shapes=[
-            pltpu.VMEM((2 * order, 2 * width), jnp.bfloat16),
-            pltpu.VMEM((order, 2 * width), jnp.bfloat16),
+            closing_body, sources=len(held), middle=middle, scale=-1.0 / math.sqrt(order)
+        ),
+        in_specs=[pl.BlockSpec(memory_space=pltpu.SMEM)]
+        + [pl.BlockSpec(memory_space=pl.ANY)] * len(held),
+        out_specs=[vmem] * len(shapes),
+        out_shape=shapes,
+        scratch_shapes=[pltpu.VMEM(array.shape, jnp.bfloat16) for array in held]
+        + [
+            pltpu.VMEM((2 * order, columns), jnp.bfloat16),
+            pltpu.VMEM((order, columns), jnp.bfloat16),
+            pltpu.SemaphoreType.DMA((len(held),)),
         ],
-        compiler_params=pltpu.CompilerParams(vmem_limit_bytes=VMEM_LIMIT),
+        compiler_params=pltpu.CompilerParams(vmem_limit_bytes=CLOSING_VMEM),
         cost_estimate=pl.CostEstimate(
             flops=16 * order * order * width, bytes_accessed=8 * order * order, transcendentals=0
         ),
-    )(place, *own, *other)
+        name="closing",
+    )(place, *held)
 
 
 def opening_body(place_ref, spectra_ref, pick_ref, put_ref, keep_ref, *refs, sources, scale):
     source_refs, refs = refs[:sources], refs[sources:]
-    out_ref, filled_ref = refs[:2]
-    held_refs, (right_ref, semaphores) = refs[2:-2], refs[-2:]
+    out_ref, filled_out = refs[:2]
+    held_refs, (filled_ref, sent_ref, right_ref, semaphores, leaving) = refs[2:-5], refs[-5:]
     copies = [
         pltpu.make_async_copy(source, held, semaphores.at[index])
         for index, (source, held) in enumerate(zip(source_refs, held_refs))
@@ -332,6 +351,8 @@
     for copy in copies:
         copy.start()
     fill_into(filled_ref, spectra_ref, pick_ref, put_ref, keep_ref)
+    departures = [pltpu.make_async_copy(filled_ref, filled_out, leaving.at[0])]
+    departures[0].start()
     for copy in copies:
         copy.wait()
     order = filled_ref.shape[0]
@@ -369,9 +390,16 @@
         total = (total * scale).astype(jnp.bfloat16)
         first = row // rows
         for part in range(parts):
-            out_ref[first : first + block // rows, part] = total[
+            sent_ref[first : first + block // rows, part] = total[
                 :, part * width : (part + 1) * width
             ].reshape(block // rows, rows, width)
+        span = pl.ds(first, block // rows)
+        departures.append(
+            pltpu.make_async_copy(sent_ref.at[span], out_ref.at[span], leaving.at[1 + row // block])
+        )
+        departures[-1].start()
+    for copy in departures:
+        copy.wait()
 
 
 def opening(place, spectra, pick, put, keep, own, other, devices):
@@ -386,17 +414,20 @@
         in_specs=[pl.BlockSpec(memory_space=pltpu.SMEM)]
         + [vmem] * 4
         + [pl.BlockSpec(memory_space=pl.ANY)] * len(held),
-        out_specs=[vmem, vmem],
+        out_specs=[pl.BlockSpec(memory_space=pl.ANY)] * 2,
         out_shape=[
             jax.ShapeDtypeStruct((devices, 2, rows, width), jnp.bfloat16),
             jax.ShapeDtypeStruct((order, 2 * last), jnp.bfloat16),
         ],
         scratch_shapes=[pltpu.VMEM(array.shape, jnp.bfloat16) for array in held]
         + [
+            pltpu.VMEM((order, 2 * last), jnp.bfloat16),
+            pltpu.VMEM((devices, 2, rows, width), jnp.bfloat16),
             pltpu.VMEM((2 * order, 2 * width), jnp.bfloat16),
             pltpu.SemaphoreType.DMA((len(held),)),
+            pltpu.SemaphoreType.DMA((1 + order // math.gcd(order, 256),)),
         ],
-        compiler_params=pltpu.CompilerParams(vmem_limit_bytes=VMEM_LIMIT),
+        compiler_params=pltpu.CompilerParams(vmem_limit_bytes=OPENING_VMEM),
         cost_estimate=pl.CostEstimate(
             flops=16 * order * order * width, bytes_accessed=8 * order * order, transcendentals=0
         ),
@@ -445,19 +476,24 @@
         raw.append(lax.ppermute(block, "shots", pairs))
         own.append(fill(block, pick, place, keep))
     other = [fill(block, pick, place, keep) for block in raw[:-1]]
+    mixed = devices <= LOOSE_DEVICES
+    homeward = spread(half, HOMEWARD)
     result = None
-    for index, (first, width) in enumerate(spread(half, HOMEWARD)):
-        loose = index == LOOSE and devices <= LOOSE_DEVICES
-        if index == 0:
-            block, filled = opening(place_of, raw[-1], pick, place, keep, own, other, devices)
-            other = other + [filled]
+    for index, (first, width) in enumerate(homeward):
+        if index != 2:
+            if index == 0:
+                block, filled = opening(place_of, raw[-1], pick, place, keep, own, other, devices)
+                other = other + [filled]
+            else:
+                *blocks, final = closing(place_of, own, other, width, devices, mixed)
+                block = blocks[0]
         else:
-            block = product(place_of, own, other, first, width, devices, loose)
-        if loose:
-            arrived = [block[0]]
+            block = final
+        if index == 1 and mixed:
+            arrived = [block]
             for step in range(1, devices):
                 route = [(i, i ^ step) for i in range(devices)]
-                arrived.append(lax.ppermute(block[step], "shots", route))
+                arrived.append(lax.ppermute(blocks[step], "shots", route))
             result = loose_inverse(place_of, arrived, inverse, result, first)
         else:
             block = exchange(block)

time: 159 us -> 157 us (0.987)
  local copies, waits for them, and re-layouts: 7.77 us -> 3.03 us
  starting transfers between devices: 46.4 us -> 50.1 us
  waiting for transfers between devices: 56.4 us -> 54.6 us
  Pallas kernels: 44.7 us -> 46.3 us
    unnamed x24 -> x20, local copies, waits for them, and re-layouts: 7.49 us -> 2.76 us
    ppermute x15, starting transfers between devices: 21.1 us -> 24.8 us  [predict(): arrived.append(lax.ppermute(blocks[step], 'shots', route))]
    pallas_call x2 -> x1, Pallas kernels: 4.58 us -> 6.94 us  [closing(): pl.pallas_call(functools.partial(closing_body, sources=len(held), middle=...]
  transfers between devices with their start and end apart: 21 -> 21, of which waited for: 8 -> 8; matrix products, arithmetic and copies ran while one was open for 1% -> 1% of each run, Pallas kernels for 15% -> 17%
where the time goes in v6:
time: 157 us; the launch traced here: 156 us
  waiting for transfers between devices  54.6 us (35%)
  starting transfers between devices  50.1 us (32%)
  Pallas kernels  46.3 us (29%)
  local copies, waits for them, and re-layouts  3.03 us (2%)
    all_to_all x4, waiting for transfers between devices, exchange(): lax.all_to_all(blocks, 'shots', split_axis=0, concat_axis=0, tiled=True)  47.4 us
    all_to_all x4, starting transfers between devices, exchange(): lax.all_to_all(blocks, 'shots', split_axis=0, concat_axis=0, tiled=True)  24.8 us
    ppermute x15, starting transfers between devices, predict(): arrived.append(lax.ppermute(blocks[step], 'shots', route))  24.8 us
    pallas_call x2, Pallas kernels, forward_chunk(): pl.pallas_call(functools.partial(forward_body, first=first), in_specs=[pl...  16 us
    pallas_call x2, Pallas kernels, inverse_chunk(): pl.pallas_call(functools.partial(inverse_body, first=first), in_specs=[vm...  7.75 us
    ppermute x15, waiting for transfers between devices, predict(): arrived.append(lax.ppermute(blocks[step], 'shots', route))  7.17 us
    pallas_call x1, Pallas kernels, closing(): pl.pallas_call(functools.partial(closing_body, sources=len(held), middle=...  6.94 us
    pallas_call x1, Pallas kernels, loose_inverse(): pl.pallas_call(functools.partial(loose_body, first=first), in_specs=[pl.B...  6.83 us
  transfers between devices with their start and end apart: 21, of which 8 were waited for; matrix products, arithmetic and copies ran while one was open for 1% of the time, Pallas kernels for 17%

profile of v6, /device:TPU:1, one launch (start us, length us, event | category | flops | bytes accessed | tf_op | source)
XLA Modules:
  0.0 155.8 jit_solution(18234216286682704400)
XLA Ops:
  0.8 10.6 %shard_map.56 = bf16[8,2,2,64,384]{4,3,2,1,0:T(8,128)(2,1)} custom-call(bf16[64,2,512,256]{3,2,1,0:T(8,128)(2,1)} %bitcast.26, bf16[16,256]{1,0:T(8,128)(2,1)S(1)} %reshape.141.table_ref), custom_call_target="tpu_custom_call" | custom-call | flops 402653184 | bytes 25165824 | tf_op jit(solution)/shard_map/pallas_call | solution.py:82
  11.4 7.3 %all-to-all-start.1 = ((bf16[16,2,64,384]{3,2,1,0:T(8,128)(2,1)}), bf16[16,2,64,384]{3,2,1,0:T(8,128)(2,1)S(1)}, u32[]{:S(2)}, u32[]{:S(2)}) async-start(bf16[16,2,64,384]{3,2,1,0:T(8,128)(2,1)} %bitcast.11), calls=%async_computation.1 | async-start | bytes 3145728 | tf_op jit(solution)/shard_map/all_to_all | solution.py:467
  18.8 5.4 %shard_map.55 = bf16[8,2,2,64,128]{4,3,2,1,0:T(8,128)(2,1)} custom-call(bf16[64,2,512,256]{3,2,1,0:T(8,128)(2,1)} %bitcast.27, bf16[16,256]{1,0:T(8,128)(2,1)S(1)} %reshape.141.table_ref), custom_call_target="tpu_custom_call" | custom-call | flops 134217728 | bytes 8388608 | tf_op jit(solution)/shard_map/pallas_call | solution.py:82
  24.2 27.0 %all-to-all-done.1.spectra_ref = bf16[16,2,64,384]{3,2,1,0:T(8,128)(2,1)S(1)} async-done(((bf16[16,2,64,384]{3,2,1,0:T(8,128)(2,1)}), bf16[16,2,64,384]{3,2,1,0:T(8,128)(2,1)S(1)}, u32[]{:S(2)}, u32[]{:S(2)}) %all-to-all-start.1) | async-done | bytes 1572896 | tf_op jit(solution)/shard_map/all_to_all | solution.py:467
  51.2 8.6 %all-to-all-start = ((bf16[16,2,64,128]{3,2,1,0:T(8,128)(2,1)}), bf16[16,2,64,128]{3,2,1,0:T(8,128)(2,1)S(1)}, u32[]{:S(2)}, u32[]{:S(2)}) async-start(bf16[16,2,64,128]{3,2,1,0:T(8,128)(2,1)} %bitcast.3), calls=%async_computation | async-start | bytes 1048576 | tf_op jit(solution)/shard_map/all_to_all | solution.py:467
  60.4 13.3 %all-to-all-done.spectra_ref = bf16[16,2,64,128]{3,2,1,0:T(8,128)(2,1)S(1)} async-done(((bf16[16,2,64,128]{3,2,1,0:T(8,128)(2,1)}), bf16[16,2,64,128]{3,2,1,0:T(8,128)(2,1)S(1)}, u32[]{:S(2)}, u32[]{:S(2)}) %all-to-all-start) | async-done | bytes 524320 | tf_op jit(solution)/shard_map/all_to_all | solution.py:467
  80.6 5.5 %opening.1 = (bf16[16,2,64,128]{3,2,1,0:T(8,128)(2,1)}, bf16[1024,768]{1,0:T(8,128)(2,1)}) custom-call(s32[1]{0:T(128)} %bitcast.place_ref, bf16[16,2,64,384]{3,2,1,0:T(8,128)(2,1)} %collective-permute-done.1.spectra_ref, bf16[256,1024]{1,0:T(8,128)(2,1)} %copy-done.1, bf16[1024,128]{1,0:T(8,128)(2,1)} %copy-done.2, f32[1024,1]{1,0:T(8,128)} %copy-done, ...), custom_call_target="tpu_custom_call" | custom-call | flops 2147483648 | bytes 8388608 | tf_op jit(solution)/shard_map/opening/pallas_call | solution.py:412
  86.0 4.5 %all-to-all-start.3 = ((bf16[16,2,64,128]{3,2,1,0:T(8,128)(2,1)}), bf16[16,2,64,128]{3,2,1,0:T(8,128)(2,1)S(1)}, u32[]{:S(2)}, u32[]{:S(2)}) async-start(bf16[16,2,64,128]{3,2,1,0:T(8,128)(2,1)} %get-tuple-element.26), calls=%async_computation.3 | async-start | bytes 1048576 | tf_op jit(solution)/shard_map/all_to_all | solution.py:467
  90.5 6.9 %closing.1 = (bf16[2,64,256]{2,1,0:T(8,128)(2,1)}, bf16[2,64,256]{2,1,0:T(8,128)(2,1)}, bf16[2,64,256]{2,1,0:T(8,128)(2,1)}, bf16[2,64,256]{2,1,0:T(8,128)(2,1)}...) custom-call(s32[1]{0:T(128)} %bitcast.place_ref, ...), custom_call_target="tpu_custom_call" | custom-call | flops 6442450944 | bytes 8388608 | tf_op jit(solution)/shard_map/closing/pallas_call | solution.py:321
  97.5 7.1 %all-to-all-done.3 = bf16[16,2,64,128]{3,2,1,0:T(8,128)(2,1)S(1)} async-done(((bf16[16,2,64,128]{3,2,1,0:T(8,128)(2,1)}), bf16[16,2,64,128]{3,2,1,0:T(8,128)(2,1)S(1)}, u32[]{:S(2)}, u32[]{:S(2)}) %all-to-all-start.3) | async-done | bytes 524320 | tf_op jit(solution)/shard_map/all_to_all | solution.py:467
  104.5 4.4 %all-to-all-start.2 = ((bf16[16,2,64,128]{3,2,1,0:T(8,128)(2,1)}), bf16[16,2,64,128]{3,2,1,0:T(8,128)(2,1)S(1)}, u32[]{:S(2)}, u32[]{:S(2)}) async-start(bf16[16,2,64,128]{3,2,1,0:T(8,128)(2,1)} %get-tuple-element.25), calls=%async_computation.2 | async-start | bytes 1048576 | tf_op jit(solution)/shard_map/all_to_all | solution.py:467
  112.8 2.4 %collective-permute-start.7 = (bf16[2,64,256]{2,1,0:T(8,128)(2,1)}, bf16[2,64,256]{2,1,0:T(8,128)(2,1)S(1)}, u32[]{:S(2)}, u32[]{:S(2)}) collective-permute-start(bf16[2,64,256]{2,1,0:T(8,128)(2,1)} %get-tuple-element.33), channel_id=1, source_target_pairs={{0,6},{1,7},{2,4},{3,5},{4,2},{5,3},{6,0},{7,1},{8,14},{9,15},{10,... | collective-permute-start | bytes 196616 | tf_op jit(solution)/shard_map/ppermute | solution.py:496
  115.6 2.0 %collective-permute-start.8 = (bf16[2,64,256]{2,1,0:T(8,128)(2,1)}, bf16[2,64,256]{2,1,0:T(8,128)(2,1)S(1)}, u32[]{:S(2)}, u32[]{:S(2)}) collective-permute-start(bf16[2,64,256]{2,1,0:T(8,128)(2,1)} %get-tuple-element.34), channel_id=1, source_target_pairs={{0,7},{1,6},{2,5},{3,4},{4,3},{5,2},{6,1},{7,0},{8,15},{9,14},{10,... | collective-permute-start | bytes 196616 | tf_op jit(solution)/shard_map/ppermute | solution.py:496
  118.5 2.3 %collective-permute-start.9 = (bf16[2,64,256]{2,1,0:T(8,128)(2,1)}, bf16[2,64,256]{2,1,0:T(8,128)(2,1)S(1)}, u32[]{:S(2)}, u32[]{:S(2)}) collective-permute-start(bf16[2,64,256]{2,1,0:T(8,128)(2,1)} %get-tuple-element.35), channel_id=1, source_target_pairs={{0,8},{1,9},{2,10},{3,11},{4,12},{5,13},{6,14},{7,15},{8,0},{9,1},... | collective-permute-start | bytes 196616 | tf_op jit(solution)/shard_map/ppermute | solution.py:496
  120.8 3.8 %collective-permute-start.10 = (bf16[2,64,256]{2,1,0:T(8,128)(2,1)}, bf16[2,64,256]{2,1,0:T(8,128)(2,1)S(1)}, u32[]{:S(2)}, u32[]{:S(2)}) collective-permute-start(bf16[2,64,256]{2,1,0:T(8,128)(2,1)} %get-tuple-element.36), channel_id=1, source_target_pairs={{0,9},{1,8},{2,11},{3,10},{4,13},{5,12},{6,15},{7,14},{8,1},{9,0},... | collective-permute-start | bytes 196616 | tf_op jit(solution)/shard_map/ppermute | solution.py:496
  124.6 1.7 %collective-permute-start.11 = (bf16[2,64,256]{2,1,0:T(8,128)(2,1)}, bf16[2,64,256]{2,1,0:T(8,128)(2,1)S(1)}, u32[]{:S(2)}, u32[]{:S(2)}) collective-permute-start(bf16[2,64,256]{2,1,0:T(8,128)(2,1)} %get-tuple-element.37), channel_id=1, source_target_pairs={{0,10},{1,11},{2,8},{3,9},{4,14},{5,15},{6,12},{7,13},{8,2},{9,3},... | collective-permute-start | bytes 196616 | tf_op jit(solution)/shard_map/ppermute | solution.py:496
  126.3 2.7 %collective-permute-start.12 = (bf16[2,64,256]{2,1,0:T(8,128)(2,1)}, bf16[2,64,256]{2,1,0:T(8,128)(2,1)S(1)}, u32[]{:S(2)}, u32[]{:S(2)}) collective-permute-start(bf16[2,64,256]{2,1,0:T(8,128)(2,1)} %get-tuple-element.38), channel_id=1, source_target_pairs={{0,11},{1,10},{2,9},{3,8},{4,15},{5,14},{6,13},{7,12},{8,3},{9,2},... | collective-permute-start | bytes 196616 | tf_op jit(solution)/shard_map/ppermute | solution.py:496
  129.8 1.7 %collective-permute-start.13 = (bf16[2,64,256]{2,1,0:T(8,128)(2,1)}, bf16[2,64,256]{2,1,0:T(8,128)(2,1)S(1)}, u32[]{:S(2)}, u32[]{:S(2)}) collective-permute-start(bf16[2,64,256]{2,1,0:T(8,128)(2,1)} %get-tuple-element.39), channel_id=1, source_target_pairs={{0,12},{1,13},{2,14},{3,15},{4,8},{5,9},{6,10},{7,11},{8,4},{9,5},... | collective-permute-start | bytes 196616 | tf_op jit(solution)/shard_map/ppermute | solution.py:496
  133.0 2.9 %collective-permute-start.15 = (bf16[2,64,256]{2,1,0:T(8,128)(2,1)}, bf16[2,64,256]{2,1,0:T(8,128)(2,1)S(1)}, u32[]{:S(2)}, u32[]{:S(2)}) collective-permute-start(bf16[2,64,256]{2,1,0:T(8,128)(2,1)} %get-tuple-element.41), channel_id=1, source_target_pairs={{0,14},{1,15},{2,12},{3,13},{4,10},{5,11},{6,8},{7,9},{8,6},{9,7},... | collective-permute-start | bytes 196616 | tf_op jit(solution)/shard_map/ppermute | solution.py:496
  135.9 2.3 %collective-permute-done.11.refs_10_ = bf16[2,64,256]{2,1,0:T(8,128)(2,1)S(1)} collective-permute-done((bf16[2,64,256]{2,1,0:T(8,128)(2,1)}, bf16[2,64,256]{2,1,0:T(8,128)(2,1)S(1)}, u32[]{:S(2)}, u32[]{:S(2)}) %collective-permute-start.11) | collective-permute-done | bytes 65568 | tf_op jit(solution)/shard_map/ppermute | solution.py:496
  138.2 3.9 %shard_map.57.kept_ref = bf16[64,2,512,256]{3,2,1,0:T(8,128)(2,1)} custom-call(bf16[8,2,2,64,128]{4,3,2,1,0:T(8,128)(2,1)S(1)} %bitcast.25, bf16[16,256]{1,0:T(8,128)(2,1)S(1)} %reshape.145.table_ref), custom_call_target="tpu_custom_call" | custom-call | flops 134217728 | bytes 8388608 | tf_op jit(solution)/shard_map/pallas_call | solution.py:138
  142.2 2.7 %collective-permute-done.16.refs_15_ = bf16[2,64,256]{2,1,0:T(8,128)(2,1)S(1)} collective-permute-done((bf16[2,64,256]{2,1,0:T(8,128)(2,1)}, bf16[2,64,256]{2,1,0:T(8,128)(2,1)S(1)}, u32[]{:S(2)}, u32[]{:S(2)}) %collective-permute-start.16) | collective-permute-done | bytes 65568 | tf_op jit(solution)/shard_map/ppermute | solution.py:496
  144.9 6.8 %shard_map.58.refs_0_ = bf16[64,2,512,256]{3,2,1,0:T(8,128)(2,1)} custom-call(s32[1]{0:T(128)} %bitcast.place_ref, bf16[16,256]{1,0:T(8,128)(2,1)S(1)} %reshape.145.table_ref, bf16[64,2,512,256]{3,2,1,0:T(8,128)(2,1)} %shard_map.57.kept_ref, bf16[2,64,256]{2,1,0:T(8,128)(2,1)S(1)} %copy-done.6, ...), custom_call_target="tpu_custom_call", output_to_operand_aliasing={{}: (2, {})} | custom-call | flops 268435456 | bytes 16777216 | tf_op jit(solution)/shard_map/pallas_call | solution.py:194
  151.7 3.9 %shard_map.59 = bf16[64,2,512,256]{3,2,1,0:T(8,128)(2,1)} custom-call(bf16[8,2,2,64,128]{4,3,2,1,0:T(8,128)(2,1)S(1)} %bitcast.24, bf16[16,256]{1,0:T(8,128)(2,1)S(1)} %reshape.145.table_ref, bf16[64,2,512,256]{3,2,1,0:T(8,128)(2,1)} %shard_map.58.refs_0_), custom_call_target="tpu_custom_call", output_to_operand_aliasing={{}: (2, {})} | custom-call | flops 134217728 | bytes 8388608 | tf_op jit(solution)/shard_map/pallas_call | solution.py:138
  (61 shorter events, 15.6 us)
Async XLA Ops:
  11.4 39.7 %all-to-all-start.1 = ((bf16[16,2,64,384]{3,2,1,0:T(8,128)(2,1)}), bf16[16,2,64,384]{3,2,1,0:T(8,128)(2,1)S(1)}, u32[]{:S(2)}, u32[]{:S(2)}) async-start(bf16[16,2,64,384]{3,2,1,0:T(8,128)(2,1)} %bitcast.11), calls=%async_computation.1 | async-start | bytes 3145728 | tf_op jit(solution)/shard_map/all_to_all | solution.py:467
  18.8 41.1 %copy-start.9 = (s32[128]{0:T(128)S(1)}, s32[128]{0:T(128)}, u32[]{:S(2)}) copy-start(s32[128]{0:T(128)} %param.6) | copy-start | bytes 1540
  24.1 36.2 %copy-start.7 = (s32[128,3]{0,1:T(4,128)S(1)}, s32[128,3]{0,1:T(4,128)}, u32[]{:S(2)}) copy-start(s32[128,3]{0,1:T(4,128)} %param.7) | copy-start | bytes 4612
  24.2 49.9 %copy-start.8 = (f32[128,3]{0,1:T(4,128)S(1)}, f32[128,3]{0,1:T(4,128)}, u32[]{:S(2)}) copy-start(f32[128,3]{0,1:T(4,128)} %param.8) | copy-start | bytes 4612
  51.2 22.6 %all-to-all-start = ((bf16[16,2,64,128]{3,2,1,0:T(8,128)(2,1)}), bf16[16,2,64,128]{3,2,1,0:T(8,128)(2,1)S(1)}, u32[]{:S(2)}, u32[]{:S(2)}) async-start(bf16[16,2,64,128]{3,2,1,0:T(8,128)(2,1)} %bitcast.3), calls=%async_computation | async-start | bytes 1048576 | tf_op jit(solution)/shard_map/all_to_all | solution.py:467
  59.7 20.8 %collective-permute-start.1 = (bf16[16,2,64,384]{3,2,1,0:T(8,128)(2,1)S(1)}, bf16[16,2,64,384]{3,2,1,0:T(8,128)(2,1)}, u32[]{:S(2)}, u32[]{:S(2)}) collective-permute-start(bf16[16,2,64,384]{3,2,1,0:T(8,128)(2,1)S(1)} %all-to-all-done.1.spectra_ref), channel_id=1, source_target_pairs={{0,1},{1,0},{2,3},{3,2},{4,5},{5,4},{6,7},{7,6},{8,9},{9,8},{10,11... | collective-permute-start | bytes 4718600 | tf_op jit(solution)/shard_map/ppermute | solution.py:476
  73.7 2.5 %collective-permute-start = (bf16[16,2,64,128]{3,2,1,0:T(8,128)(2,1)S(1)}, bf16[16,2,64,128]{3,2,1,0:T(8,128)(2,1)S(1)}, u32[]{:S(2)}, u32[]{:S(2)}) collective-permute-start(bf16[16,2,64,128]{3,2,1,0:T(8,128)(2,1)S(1)} %all-to-all-done.spectra_ref), channel_id=1, source_target_pairs={{0,1},{1,0},{2,3},{3,2},{4,5},{5,4},{6,7},{7,6},{8,9},{9,8},{10,11... | collective-permute-start | bytes 1572872 | tf_op jit(solution)/shard_map/ppermute | solution.py:476
  86.0 18.5 %all-to-all-start.3 = ((bf16[16,2,64,128]{3,2,1,0:T(8,128)(2,1)}), bf16[16,2,64,128]{3,2,1,0:T(8,128)(2,1)S(1)}, u32[]{:S(2)}, u32[]{:S(2)}) async-start(bf16[16,2,64,128]{3,2,1,0:T(8,128)(2,1)} %get-tuple-element.26), calls=%async_computation.3 | async-start | bytes 1048576 | tf_op jit(solution)/shard_map/all_to_all | solution.py:467
  104.5 47.2 %all-to-all-start.2 = ((bf16[16,2,64,128]{3,2,1,0:T(8,128)(2,1)}), bf16[16,2,64,128]{3,2,1,0:T(8,128)(2,1)S(1)}, u32[]{:S(2)}, u32[]{:S(2)}) async-start(bf16[16,2,64,128]{3,2,1,0:T(8,128)(2,1)} %get-tuple-element.25), calls=%async_computation.2 | async-start | bytes 1048576 | tf_op jit(solution)/shard_map/all_to_all | solution.py:467
  109.0 3.8 %collective-permute-start.2 = (bf16[2,64,256]{2,1,0:T(8,128)(2,1)}, bf16[2,64,256]{2,1,0:T(8,128)(2,1)S(1)}, u32[]{:S(2)}, u32[]{:S(2)}) collective-permute-start(bf16[2,64,256]{2,1,0:T(8,128)(2,1)} %get-tuple-element.28), channel_id=1, source_target_pairs={{0,1},{1,0},{2,3},{3,2},{4,5},{5,4},{6,7},{7,6},{8,9},{9,8},{10,11... | collective-permute-start | bytes 196616 | tf_op jit(solution)/shard_map/ppermute | solution.py:496
  109.1 6.4 %collective-permute-start.3 = (bf16[2,64,256]{2,1,0:T(8,128)(2,1)}, bf16[2,64,256]{2,1,0:T(8,128)(2,1)S(1)}, u32[]{:S(2)}, u32[]{:S(2)}) collective-permute-start(bf16[2,64,256]{2,1,0:T(8,128)(2,1)} %get-tuple-element.29), channel_id=1, source_target_pairs={{0,2},{1,3},{2,0},{3,1},{4,6},{5,7},{6,4},{7,5},{8,10},{9,11},{10,... | collective-permute-start | bytes 196616 | tf_op jit(solution)/shard_map/ppermute | solution.py:496
  110.8 7.7 %collective-permute-start.4 = (bf16[2,64,256]{2,1,0:T(8,128)(2,1)}, bf16[2,64,256]{2,1,0:T(8,128)(2,1)S(1)}, u32[]{:S(2)}, u32[]{:S(2)}) collective-permute-start(bf16[2,64,256]{2,1,0:T(8,128)(2,1)} %get-tuple-element.30), channel_id=1, source_target_pairs={{0,3},{1,2},{2,1},{3,0},{4,7},{5,6},{6,5},{7,4},{8,11},{9,10},{10,... | collective-permute-start | bytes 196616 | tf_op jit(solution)/shard_map/ppermute | solution.py:496
  111.2 9.6 %collective-permute-start.5 = (bf16[2,64,256]{2,1,0:T(8,128)(2,1)}, bf16[2,64,256]{2,1,0:T(8,128)(2,1)S(1)}, u32[]{:S(2)}, u32[]{:S(2)}) collective-permute-start(bf16[2,64,256]{2,1,0:T(8,128)(2,1)} %get-tuple-element.31), channel_id=1, source_target_pairs={{0,4},{1,5},{2,6},{3,7},{4,0},{5,1},{6,2},{7,3},{8,12},{9,13},{10,... | collective-permute-start | bytes 196616 | tf_op jit(solution)/shard_map/ppermute | solution.py:496
  112.5 12.1 %collective-permute-start.6 = (bf16[2,64,256]{2,1,0:T(8,128)(2,1)}, bf16[2,64,256]{2,1,0:T(8,128)(2,1)S(1)}, u32[]{:S(2)}, u32[]{:S(2)}) collective-permute-start(bf16[2,64,256]{2,1,0:T(8,128)(2,1)} %get-tuple-element.32), channel_id=1, source_target_pairs={{0,5},{1,4},{2,7},{3,6},{4,1},{5,0},{6,3},{7,2},{8,13},{9,12},{10,... | collective-permute-start | bytes 196616 | tf_op jit(solution)/shard_map/ppermute | solution.py:496
  112.8 13.5 %collective-permute-start.7 = (bf16[2,64,256]{2,1,0:T(8,128)(2,1)}, bf16[2,64,256]{2,1,0:T(8,128)(2,1)S(1)}, u32[]{:S(2)}, u32[]{:S(2)}) collective-permute-start(bf16[2,64,256]{2,1,0:T(8,128)(2,1)} %get-tuple-element.33), channel_id=1, source_target_pairs={{0,6},{1,7},{2,4},{3,5},{4,2},{5,3},{6,0},{7,1},{8,14},{9,15},{10,... | collective-permute-start | bytes 196616 | tf_op jit(solution)/shard_map/ppermute | solution.py:496
  115.6 14.3 %collective-permute-start.8 = (bf16[2,64,256]{2,1,0:T(8,128)(2,1)}, bf16[2,64,256]{2,1,0:T(8,128)(2,1)S(1)}, u32[]{:S(2)}, u32[]{:S(2)}) collective-permute-start(bf16[2,64,256]{2,1,0:T(8,128)(2,1)} %get-tuple-element.34), channel_id=1, source_target_pairs={{0,7},{1,6},{2,5},{3,4},{4,3},{5,2},{6,1},{7,0},{8,15},{9,14},{10,... | collective-permute-start | bytes 196616 | tf_op jit(solution)/shard_map/ppermute | solution.py:496
  118.5 13.1 %collective-permute-start.9 = (bf16[2,64,256]{2,1,0:T(8,128)(2,1)}, bf16[2,64,256]{2,1,0:T(8,128)(2,1)S(1)}, u32[]{:S(2)}, u32[]{:S(2)}) collective-permute-start(bf16[2,64,256]{2,1,0:T(8,128)(2,1)} %get-tuple-element.35), channel_id=1, source_target_pairs={{0,8},{1,9},{2,10},{3,11},{4,12},{5,13},{6,14},{7,15},{8,0},{9,1},... | collective-permute-start | bytes 196616 | tf_op jit(solution)/shard_map/ppermute | solution.py:496
  120.8 12.2 %collective-permute-start.10 = (bf16[2,64,256]{2,1,0:T(8,128)(2,1)}, bf16[2,64,256]{2,1,0:T(8,128)(2,1)S(1)}, u32[]{:S(2)}, u32[]{:S(2)}) collective-permute-start(bf16[2,64,256]{2,1,0:T(8,128)(2,1)} %get-tuple-element.36), channel_id=1, source_target_pairs={{0,9},{1,8},{2,11},{3,10},{4,13},{5,12},{6,15},{7,14},{8,1},{9,0},... | collective-permute-start | bytes 196616 | tf_op jit(solution)/shard_map/ppermute | solution.py:496
  124.6 13.6 %collective-permute-start.11 = (bf16[2,64,256]{2,1,0:T(8,128)(2,1)}, bf16[2,64,256]{2,1,0:T(8,128)(2,1)S(1)}, u32[]{:S(2)}, u32[]{:S(2)}) collective-permute-start(bf16[2,64,256]{2,1,0:T(8,128)(2,1)} %get-tuple-element.37), channel_id=1, source_target_pairs={{0,10},{1,11},{2,8},{3,9},{4,14},{5,15},{6,12},{7,13},{8,2},{9,3},... | collective-permute-start | bytes 196616 | tf_op jit(solution)/shard_map/ppermute | solution.py:496
  126.3 15.8 %collective-permute-start.12 = (bf16[2,64,256]{2,1,0:T(8,128)(2,1)}, bf16[2,64,256]{2,1,0:T(8,128)(2,1)S(1)}, u32[]{:S(2)}, u32[]{:S(2)}) collective-permute-start(bf16[2,64,256]{2,1,0:T(8,128)(2,1)} %get-tuple-element.38), channel_id=1, source_target_pairs={{0,11},{1,10},{2,9},{3,8},{4,15},{5,14},{6,13},{7,12},{8,3},{9,2},... | collective-permute-start | bytes 196616 | tf_op jit(solution)/shard_map/ppermute | solution.py:496
  129.8 12.3 %collective-permute-start.13 = (bf16[2,64,256]{2,1,0:T(8,128)(2,1)}, bf16[2,64,256]{2,1,0:T(8,128)(2,1)S(1)}, u32[]{:S(2)}, u32[]{:S(2)}) collective-permute-start(bf16[2,64,256]{2,1,0:T(8,128)(2,1)} %get-tuple-element.39), channel_id=1, source_target_pairs={{0,12},{1,13},{2,14},{3,15},{4,8},{5,9},{6,10},{7,11},{8,4},{9,5},... | collective-permute-start | bytes 196616 | tf_op jit(solution)/shard_map/ppermute | solution.py:496
  131.5 10.6 %collective-permute-start.14 = (bf16[2,64,256]{2,1,0:T(8,128)(2,1)}, bf16[2,64,256]{2,1,0:T(8,128)(2,1)S(1)}, u32[]{:S(2)}, u32[]{:S(2)}) collective-permute-start(bf16[2,64,256]{2,1,0:T(8,128)(2,1)} %get-tuple-element.40), channel_id=1, source_target_pairs={{0,13},{1,12},{2,15},{3,14},{4,9},{5,8},{6,11},{7,10},{8,5},{9,4},... | collective-permute-start | bytes 196616 | tf_op jit(solution)/shard_map/ppermute | solution.py:496
  133.0 9.2 %collective-permute-start.15 = (bf16[2,64,256]{2,1,0:T(8,128)(2,1)}, bf16[2,64,256]{2,1,0:T(8,128)(2,1)S(1)}, u32[]{:S(2)}, u32[]{:S(2)}) collective-permute-start(bf16[2,64,256]{2,1,0:T(8,128)(2,1)} %get-tuple-element.41), channel_id=1, source_target_pairs={{0,14},{1,15},{2,12},{3,13},{4,10},{5,11},{6,8},{7,9},{8,6},{9,7},... | collective-permute-start | bytes 196616 | tf_op jit(solution)/shard_map/ppermute | solution.py:496
  138.2 6.7 %collective-permute-start.16 = (bf16[2,64,256]{2,1,0:T(8,128)(2,1)}, bf16[2,64,256]{2,1,0:T(8,128)(2,1)S(1)}, u32[]{:S(2)}, u32[]{:S(2)}) collective-permute-start(bf16[2,64,256]{2,1,0:T(8,128)(2,1)} %get-tuple-element.42), channel_id=1, source_target_pairs={{0,15},{1,14},{2,13},{3,12},{4,11},{5,10},{6,9},{7,8},{8,7},{9,6},... | collective-permute-start | bytes 196616 | tf_op jit(solution)/shard_map/ppermute | solution.py:496
  (7 other events, 45.9 us)

commit v7 on v6

--- a/solution.py
+++ b/solution.py
@@ -340,7 +340,51 @@
     )(place, *held)
 
 
-def opening_body(place_ref, spectra_ref, pick_ref, put_ref, keep_ref, *refs, sources, scale):
+def fill_right(right_ref, own_ref, depths, start):
+    width = own_ref.shape[1] // 2
+    line = 0
+    for depth in depths:
+        lines = pl.ds(pl.multiple_of(start, 128), depth)
+        real = own_ref[lines, :width]
+        imag = own_ref[lines, width:]
+        right_ref[line : line + depth, :width] = real
+        right_ref[line : line + depth, width:] = imag
+        right_ref[line + depth : line + 2 * depth, :width] = -imag
+        right_ref[line + depth : line + 2 * depth, width:] = real
+        line += 2 * depth
+        start += depth
+
+
+def early_body(place_ref, one_ref, two_ref, out_ref, right_ref):
+    order = out_ref.shape[0]
+    depths = [one_ref.shape[1] // 2, two_ref.shape[1] // 2]
+    fill_right(right_ref, one_ref, depths, place_ref[0] % 2 * (order // 2))
+    cut = 2 * depths[0]
+    block = math.gcd(order, 256)
+    for row in range(0, order, block):
+        out_ref[row : row + block] = jnp.dot(
+            one_ref[row : row + block], right_ref[:cut], preferred_element_type=jnp.float32
+        ) + jnp.dot(two_ref[row : row + block], right_ref[cut:], preferred_element_type=jnp.float32)
+
+
+def early(place, one, two):
+    order, columns = one.shape
+    vmem = pl.BlockSpec(memory_space=pltpu.VMEM)
+    return pl.pallas_call(
+        early_body,
+        in_specs=[pl.BlockSpec(memory_space=pltpu.SMEM), vmem, vmem],
+        out_specs=vmem,
+        out_shape=jax.ShapeDtypeStruct((order, columns), jnp.float32),
+        scratch_shapes=[pltpu.VMEM((order, columns), jnp.bfloat16)],
+        compiler_params=pltpu.CompilerParams(vmem_limit_bytes=VMEM_LIMIT),
+        cost_estimate=pl.CostEstimate(
+            flops=2 * order * order * columns, bytes_accessed=4 * order * order, transcendentals=0
+        ),
+        name="early",
+    )(place, one, two)
+
+
+def opening_body(place_ref, spectra_ref, pick_ref, put_ref, keep_ref, grown_ref, *refs, sources, scale):
     source_refs, refs = refs[:sources], refs[sources:]
     out_ref, filled_out = refs[:2]
     held_refs, (filled_ref, sent_ref, right_ref, semaphores, leaving) = refs[2:-5], refs[-5:]
@@ -358,34 +402,19 @@
     order = filled_ref.shape[0]
     half = order // 2
     _, parts, rows, width = out_ref.shape
-    count = (sources + 1) // 2
-    lefts = list(held_refs) + [filled_ref]
     own_ref = held_refs[0]
-    member = place_ref[0] % 2
-    line = 0
-    for index, left in enumerate(lefts):
-        if index % count == 0:
-            start = (member if index == 0 else 1 - member) * half
-        depth = left.shape[1] // 2
-        lines = pl.ds(pl.multiple_of(start, 128), depth)
-        real = own_ref[lines, :width]
-        imag = own_ref[lines, width:]
-        right_ref[line : line + depth, :width] = real
-        right_ref[line : line + depth, width:] = imag
-        right_ref[line + depth : line + 2 * depth, :width] = -imag
-        right_ref[line + depth : line + 2 * depth, width:] = real
-        line += 2 * depth
-        start += depth
+    lefts = [held_refs[1], filled_ref]
+    fill_right(right_ref, own_ref, [left.shape[1] // 2 for left in lefts], (1 - place_ref[0] % 2) * half)
     block = math.gcd(order, 256)
     for row in range(0, order, block):
-        total = None
+        total = grown_ref[row : row + block]
         line = 0
         for left in lefts:
             depth = left.shape[1]
             term = jnp.dot(
                 left[row : row + block], right_ref[line : line + depth], preferred_element_type=jnp.float32
             )
-            total = term if total is None else total + term
+            total = total + term
             line += depth
         total = (total * scale).astype(jnp.bfloat16)
         first = row // rows
@@ -402,17 +431,17 @@
         copy.wait()
 
 
-def opening(place, spectra, pick, put, keep, own, other, devices):
+def opening(place, spectra, pick, put, keep, own, other, grown, devices):
     order = keep.shape[0]
     rows = order // devices
     width = own[0].shape[1] // 2
     last = spectra.shape[3]
-    held = list(own) + list(other)
+    held = [own[0], other[0]]
     vmem = pl.BlockSpec(memory_space=pltpu.VMEM)
     return pl.pallas_call(
         functools.partial(opening_body, sources=len(held), scale=-1.0 / math.sqrt(order)),
         in_specs=[pl.BlockSpec(memory_space=pltpu.SMEM)]
-        + [vmem] * 4
+        + [vmem] * 5
         + [pl.BlockSpec(memory_space=pl.ANY)] * len(held),
         out_specs=[pl.BlockSpec(memory_space=pl.ANY)] * 2,
         out_shape=[
@@ -423,7 +452,7 @@
         + [
             pltpu.VMEM((order, 2 * last), jnp.bfloat16),
             pltpu.VMEM((devices, 2, rows, width), jnp.bfloat16),
-            pltpu.VMEM((2 * order, 2 * width), jnp.bfloat16),
+            pltpu.VMEM((order, 2 * width), jnp.bfloat16),
             pltpu.SemaphoreType.DMA((len(held),)),
             pltpu.SemaphoreType.DMA((1 + order // math.gcd(order, 256),)),
         ],
@@ -432,7 +461,7 @@
             flops=16 * order * order * width, bytes_accessed=8 * order * order, transcendentals=0
         ),
         name="opening",
-    )(place, spectra, pick, put, keep, *held)
+    )(place, spectra, pick, put, keep, grown, *held)
 
 
 def fill_tables(missing, neighbours, weights, order):
@@ -475,6 +504,7 @@
         block = exchange(block.reshape(devices, 2, shot_rows, width))
         raw.append(lax.ppermute(block, "shots", pairs))
         own.append(fill(block, pick, place, keep))
+    grown = early(place_of, own[0], own[1])
     other = [fill(block, pick, place, keep) for block in raw[:-1]]
     mixed = devices <= LOOSE_DEVICES
     homeward = spread(half, HOMEWARD)
@@ -482,7 +512,7 @@
     for index, (first, width) in enumerate(homeward):
         if index != 2:
             if index == 0:
-                block, filled = opening(place_of, raw[-1], pick, place, keep, own, other, devices)
+                block, filled = opening(place_of, raw[-1], pick, place, keep, own, other, grown, devices)
                 other = other + [filled]
             else:
                 *blocks, final = closing(place_of, own, other, width, devices, mixed)

time: 157 us -> 157 us (level)
  transfers between devices with their start and end apart: 21 -> 21, of which waited for: 8 -> 9; matrix products, arithmetic and copies ran while one was open for 1% -> 1% of each run, Pallas kernels for 17% -> 17%
where the time goes in v7:
time: 157 us; the launch traced here: 155 us
  waiting for transfers between devices  54.8 us (35%)
  starting transfers between devices  50.1 us (32%)
  Pallas kernels  46.6 us (30%)
  local copies, waits for them, and re-layouts  1.69 us (1%)
    all_to_all x4, waiting for transfers between devices, exchange(): lax.all_to_all(blocks, 'shots', split_axis=0, concat_axis=0, tiled=True)  47.4 us
    all_to_all x4, starting transfers between devices, exchange(): lax.all_to_all(blocks, 'shots', split_axis=0, concat_axis=0, tiled=True)  24.8 us
    ppermute x15, starting transfers between devices, predict(): arrived.append(lax.ppermute(blocks[step], 'shots', route))  24.8 us
    pallas_call x2, Pallas kernels, forward_chunk(): pl.pallas_call(functools.partial(forward_body, first=first), in_specs=[pl...  16 us
    pallas_call x2, Pallas kernels, inverse_chunk(): pl.pallas_call(functools.partial(inverse_body, first=first), in_specs=[vm...  7.76 us
    ppermute x15, waiting for transfers between devices, predict(): arrived.append(lax.ppermute(blocks[step], 'shots', route))  7.17 us
    pallas_call x1, Pallas kernels, closing(): pl.pallas_call(functools.partial(closing_body, sources=len(held), middle=...  6.94 us
    pallas_call x1, Pallas kernels, loose_inverse(): pl.pallas_call(functools.partial(loose_body, first=first), in_specs=[pl.B...  6.83 us
  transfers between devices with their start and end apart: 21, of which 9 were waited for; matrix products, arithmetic and copies ran while one was open for 1% of the time, Pallas kernels for 17%

profile of v7, /device:TPU:1, one launch (start us, length us, event | category | flops | bytes accessed | tf_op | source)
XLA Modules:
  0.0 155.0 jit_solution(1192128359702190900)
XLA Ops:
  0.8 10.6 %shard_map.56 = bf16[8,2,2,64,384]{4,3,2,1,0:T(8,128)(2,1)} custom-call(bf16[64,2,512,256]{3,2,1,0:T(8,128)(2,1)} %bitcast.26, bf16[16,256]{1,0:T(8,128)(2,1)S(1)} %reshape.141.table_ref), custom_call_target="tpu_custom_call" | custom-call | flops 402653184 | bytes 25165824 | tf_op jit(solution)/shard_map/pallas_call | solution.py:82
  11.4 7.3 %all-to-all-start.1 = ((bf16[16,2,64,384]{3,2,1,0:T(8,128)(2,1)}), bf16[16,2,64,384]{3,2,1,0:T(8,128)(2,1)S(1)}, u32[]{:S(2)}, u32[]{:S(2)}) async-start(bf16[16,2,64,384]{3,2,1,0:T(8,128)(2,1)} %bitcast.11), calls=%async_computation.1 | async-start | bytes 3145728 | tf_op jit(solution)/shard_map/all_to_all | solution.py:496
  18.8 5.4 %shard_map.55 = bf16[8,2,2,64,128]{4,3,2,1,0:T(8,128)(2,1)} custom-call(bf16[64,2,512,256]{3,2,1,0:T(8,128)(2,1)} %bitcast.27, bf16[16,256]{1,0:T(8,128)(2,1)S(1)} %reshape.141.table_ref), custom_call_target="tpu_custom_call" | custom-call | flops 134217728 | bytes 8388608 | tf_op jit(solution)/shard_map/pallas_call | solution.py:82
  24.2 27.0 %all-to-all-done.1.spectra_ref = bf16[16,2,64,384]{3,2,1,0:T(8,128)(2,1)S(1)} async-done(((bf16[16,2,64,384]{3,2,1,0:T(8,128)(2,1)}), bf16[16,2,64,384]{3,2,1,0:T(8,128)(2,1)S(1)}, u32[]{:S(2)}, u32[]{:S(2)}) %all-to-all-start.1) | async-done | bytes 1572896 | tf_op jit(solution)/shard_map/all_to_all | solution.py:496
  51.2 8.6 %all-to-all-start = ((bf16[16,2,64,128]{3,2,1,0:T(8,128)(2,1)}), bf16[16,2,64,128]{3,2,1,0:T(8,128)(2,1)S(1)}, u32[]{:S(2)}, u32[]{:S(2)}) async-start(bf16[16,2,64,128]{3,2,1,0:T(8,128)(2,1)} %bitcast.3), calls=%async_computation | async-start | bytes 1048576 | tf_op jit(solution)/shard_map/all_to_all | solution.py:496
  60.4 13.3 %all-to-all-done.spectra_ref = bf16[16,2,64,128]{3,2,1,0:T(8,128)(2,1)S(1)} async-done(((bf16[16,2,64,128]{3,2,1,0:T(8,128)(2,1)}), bf16[16,2,64,128]{3,2,1,0:T(8,128)(2,1)S(1)}, u32[]{:S(2)}, u32[]{:S(2)}) %all-to-all-start) | async-done | bytes 524320 | tf_op jit(solution)/shard_map/all_to_all | solution.py:496
  80.2 5.0 %opening.1 = (bf16[16,2,64,128]{3,2,1,0:T(8,128)(2,1)}, bf16[1024,768]{1,0:T(8,128)(2,1)}) custom-call(s32[1]{0:T(128)} %bitcast.place_ref, bf16[16,2,64,384]{3,2,1,0:T(8,128)(2,1)} %collective-permute-done.1.spectra_ref, bf16[256,1024]{1,0:T(8,128)(2,1)} %copy-done.1, bf16[1024,128]{1,0:T(8,128)(2,1)} %copy-done.3, f32[1024,1]{1,0:T(8,128)} %copy-done, ...), custom_call_target="tpu_custom_call" | custom-call | flops 2147483648 | bytes 8388608 | tf_op jit(solution)/shard_map/opening/pallas_call | solution.py:441
  85.3 4.5 %all-to-all-start.3 = ((bf16[16,2,64,128]{3,2,1,0:T(8,128)(2,1)}), bf16[16,2,64,128]{3,2,1,0:T(8,128)(2,1)S(1)}, u32[]{:S(2)}, u32[]{:S(2)}) async-start(bf16[16,2,64,128]{3,2,1,0:T(8,128)(2,1)} %get-tuple-element.26), calls=%async_computation.3 | async-start | bytes 1048576 | tf_op jit(solution)/shard_map/all_to_all | solution.py:496
  89.8 6.9 %closing.1 = (bf16[2,64,256]{2,1,0:T(8,128)(2,1)}, bf16[2,64,256]{2,1,0:T(8,128)(2,1)}, bf16[2,64,256]{2,1,0:T(8,128)(2,1)}, bf16[2,64,256]{2,1,0:T(8,128)(2,1)}...) custom-call(s32[1]{0:T(128)} %bitcast.place_ref, ...), custom_call_target="tpu_custom_call" | custom-call | flops 6442450944 | bytes 8388608 | tf_op jit(solution)/shard_map/closing/pallas_call | solution.py:321
  96.7 7.1 %all-to-all-done.3 = bf16[16,2,64,128]{3,2,1,0:T(8,128)(2,1)S(1)} async-done(((bf16[16,2,64,128]{3,2,1,0:T(8,128)(2,1)}), bf16[16,2,64,128]{3,2,1,0:T(8,128)(2,1)S(1)}, u32[]{:S(2)}, u32[]{:S(2)}) %all-to-all-start.3) | async-done | bytes 524320 | tf_op jit(solution)/shard_map/all_to_all | solution.py:496
  103.8 4.4 %all-to-all-start.2 = ((bf16[16,2,64,128]{3,2,1,0:T(8,128)(2,1)}), bf16[16,2,64,128]{3,2,1,0:T(8,128)(2,1)S(1)}, u32[]{:S(2)}, u32[]{:S(2)}) async-start(bf16[16,2,64,128]{3,2,1,0:T(8,128)(2,1)} %get-tuple-element.25), calls=%async_computation.2 | async-start | bytes 1048576 | tf_op jit(solution)/shard_map/all_to_all | solution.py:496
  112.0 2.4 %collective-permute-start.7 = (bf16[2,64,256]{2,1,0:T(8,128)(2,1)}, bf16[2,64,256]{2,1,0:T(8,128)(2,1)S(1)}, u32[]{:S(2)}, u32[]{:S(2)}) collective-permute-start(bf16[2,64,256]{2,1,0:T(8,128)(2,1)} %get-tuple-element.33), channel_id=1, source_target_pairs={{0,6},{1,7},{2,4},{3,5},{4,2},{5,3},{6,0},{7,1},{8,14},{9,15},{10,... | collective-permute-start | bytes 196616 | tf_op jit(solution)/shard_map/ppermute | solution.py:526
  114.8 2.0 %collective-permute-start.8 = (bf16[2,64,256]{2,1,0:T(8,128)(2,1)}, bf16[2,64,256]{2,1,0:T(8,128)(2,1)S(1)}, u32[]{:S(2)}, u32[]{:S(2)}) collective-permute-start(bf16[2,64,256]{2,1,0:T(8,128)(2,1)} %get-tuple-element.34), channel_id=1, source_target_pairs={{0,7},{1,6},{2,5},{3,4},{4,3},{5,2},{6,1},{7,0},{8,15},{9,14},{10,... | collective-permute-start | bytes 196616 | tf_op jit(solution)/shard_map/ppermute | solution.py:526
  117.7 2.3 %collective-permute-start.9 = (bf16[2,64,256]{2,1,0:T(8,128)(2,1)}, bf16[2,64,256]{2,1,0:T(8,128)(2,1)S(1)}, u32[]{:S(2)}, u32[]{:S(2)}) collective-permute-start(bf16[2,64,256]{2,1,0:T(8,128)(2,1)} %get-tuple-element.35), channel_id=1, source_target_pairs={{0,8},{1,9},{2,10},{3,11},{4,12},{5,13},{6,14},{7,15},{8,0},{9,1},... | collective-permute-start | bytes 196616 | tf_op jit(solution)/shard_map/ppermute | solution.py:526
  120.0 3.8 %collective-permute-start.10 = (bf16[2,64,256]{2,1,0:T(8,128)(2,1)}, bf16[2,64,256]{2,1,0:T(8,128)(2,1)S(1)}, u32[]{:S(2)}, u32[]{:S(2)}) collective-permute-start(bf16[2,64,256]{2,1,0:T(8,128)(2,1)} %get-tuple-element.36), channel_id=1, source_target_pairs={{0,9},{1,8},{2,11},{3,10},{4,13},{5,12},{6,15},{7,14},{8,1},{9,0},... | collective-permute-start | bytes 196616 | tf_op jit(solution)/shard_map/ppermute | solution.py:526
  123.8 1.7 %collective-permute-start.11 = (bf16[2,64,256]{2,1,0:T(8,128)(2,1)}, bf16[2,64,256]{2,1,0:T(8,128)(2,1)S(1)}, u32[]{:S(2)}, u32[]{:S(2)}) collective-permute-start(bf16[2,64,256]{2,1,0:T(8,128)(2,1)} %get-tuple-element.37), channel_id=1, source_target_pairs={{0,10},{1,11},{2,8},{3,9},{4,14},{5,15},{6,12},{7,13},{8,2},{9,3},... | collective-permute-start | bytes 196616 | tf_op jit(solution)/shard_map/ppermute | solution.py:526
  125.6 2.7 %collective-permute-start.12 = (bf16[2,64,256]{2,1,0:T(8,128)(2,1)}, bf16[2,64,256]{2,1,0:T(8,128)(2,1)S(1)}, u32[]{:S(2)}, u32[]{:S(2)}) collective-permute-start(bf16[2,64,256]{2,1,0:T(8,128)(2,1)} %get-tuple-element.38), channel_id=1, source_target_pairs={{0,11},{1,10},{2,9},{3,8},{4,15},{5,14},{6,13},{7,12},{8,3},{9,2},... | collective-permute-start | bytes 196616 | tf_op jit(solution)/shard_map/ppermute | solution.py:526
  129.1 1.7 %collective-permute-start.13 = (bf16[2,64,256]{2,1,0:T(8,128)(2,1)}, bf16[2,64,256]{2,1,0:T(8,128)(2,1)S(1)}, u32[]{:S(2)}, u32[]{:S(2)}) collective-permute-start(bf16[2,64,256]{2,1,0:T(8,128)(2,1)} %get-tuple-element.39), channel_id=1, source_target_pairs={{0,12},{1,13},{2,14},{3,15},{4,8},{5,9},{6,10},{7,11},{8,4},{9,5},... | collective-permute-start | bytes 196616 | tf_op jit(solution)/shard_map/ppermute | solution.py:526
  132.2 2.9 %collective-permute-start.15 = (bf16[2,64,256]{2,1,0:T(8,128)(2,1)}, bf16[2,64,256]{2,1,0:T(8,128)(2,1)S(1)}, u32[]{:S(2)}, u32[]{:S(2)}) collective-permute-start(bf16[2,64,256]{2,1,0:T(8,128)(2,1)} %get-tuple-element.41), channel_id=1, source_target_pairs={{0,14},{1,15},{2,12},{3,13},{4,10},{5,11},{6,8},{7,9},{8,6},{9,7},... | collective-permute-start | bytes 196616 | tf_op jit(solution)/shard_map/ppermute | solution.py:526
  135.1 2.3 %collective-permute-done.11.refs_10_ = bf16[2,64,256]{2,1,0:T(8,128)(2,1)S(1)} collective-permute-done((bf16[2,64,256]{2,1,0:T(8,128)(2,1)}, bf16[2,64,256]{2,1,0:T(8,128)(2,1)S(1)}, u32[]{:S(2)}, u32[]{:S(2)}) %collective-permute-start.11) | collective-permute-done | bytes 65568 | tf_op jit(solution)/shard_map/ppermute | solution.py:526
  137.5 3.9 %shard_map.57.kept_ref = bf16[64,2,512,256]{3,2,1,0:T(8,128)(2,1)} custom-call(bf16[8,2,2,64,128]{4,3,2,1,0:T(8,128)(2,1)S(1)} %bitcast.25, bf16[16,256]{1,0:T(8,128)(2,1)S(1)} %reshape.145.table_ref), custom_call_target="tpu_custom_call" | custom-call | flops 134217728 | bytes 8388608 | tf_op jit(solution)/shard_map/pallas_call | solution.py:138
  141.4 2.7 %collective-permute-done.16.refs_15_ = bf16[2,64,256]{2,1,0:T(8,128)(2,1)S(1)} collective-permute-done((bf16[2,64,256]{2,1,0:T(8,128)(2,1)}, bf16[2,64,256]{2,1,0:T(8,128)(2,1)S(1)}, u32[]{:S(2)}, u32[]{:S(2)}) %collective-permute-start.16) | collective-permute-done | bytes 65568 | tf_op jit(solution)/shard_map/ppermute | solution.py:526
  144.1 6.8 %shard_map.58.refs_0_ = bf16[64,2,512,256]{3,2,1,0:T(8,128)(2,1)} custom-call(s32[1]{0:T(128)} %bitcast.place_ref, bf16[16,256]{1,0:T(8,128)(2,1)S(1)} %reshape.145.table_ref, bf16[64,2,512,256]{3,2,1,0:T(8,128)(2,1)} %shard_map.57.kept_ref, bf16[2,64,256]{2,1,0:T(8,128)(2,1)S(1)} %copy-done.7, ...), custom_call_target="tpu_custom_call", output_to_operand_aliasing={{}: (2, {})} | custom-call | flops 268435456 | bytes 16777216 | tf_op jit(solution)/shard_map/pallas_call | solution.py:194
  151.0 3.9 %shard_map.59 = bf16[64,2,512,256]{3,2,1,0:T(8,128)(2,1)} custom-call(bf16[8,2,2,64,128]{4,3,2,1,0:T(8,128)(2,1)S(1)} %bitcast.24, bf16[16,256]{1,0:T(8,128)(2,1)S(1)} %reshape.145.table_ref, bf16[64,2,512,256]{3,2,1,0:T(8,128)(2,1)} %shard_map.58.refs_0_), custom_call_target="tpu_custom_call", output_to_operand_aliasing={{}: (2, {})} | custom-call | flops 134217728 | bytes 8388608 | tf_op jit(solution)/shard_map/pallas_call | solution.py:138
  (64 shorter events, 15.3 us)
Async XLA Ops:
  11.4 39.7 %all-to-all-start.1 = ((bf16[16,2,64,384]{3,2,1,0:T(8,128)(2,1)}), bf16[16,2,64,384]{3,2,1,0:T(8,128)(2,1)S(1)}, u32[]{:S(2)}, u32[]{:S(2)}) async-start(bf16[16,2,64,384]{3,2,1,0:T(8,128)(2,1)} %bitcast.11), calls=%async_computation.1 | async-start | bytes 3145728 | tf_op jit(solution)/shard_map/all_to_all | solution.py:496
  18.8 41.1 %copy-start.10 = (s32[128]{0:T(128)S(1)}, s32[128]{0:T(128)}, u32[]{:S(2)}) copy-start(s32[128]{0:T(128)} %param.6) | copy-start | bytes 1540
  24.2 36.2 %copy-start.8 = (s32[128,3]{0,1:T(4,128)S(1)}, s32[128,3]{0,1:T(4,128)}, u32[]{:S(2)}) copy-start(s32[128,3]{0,1:T(4,128)} %param.7) | copy-start | bytes 4612
  24.2 49.9 %copy-start.9 = (f32[128,3]{0,1:T(4,128)S(1)}, f32[128,3]{0,1:T(4,128)}, u32[]{:S(2)}) copy-start(f32[128,3]{0,1:T(4,128)} %param.8) | copy-start | bytes 4612
  51.2 22.6 %all-to-all-start = ((bf16[16,2,64,128]{3,2,1,0:T(8,128)(2,1)}), bf16[16,2,64,128]{3,2,1,0:T(8,128)(2,1)S(1)}, u32[]{:S(2)}, u32[]{:S(2)}) async-start(bf16[16,2,64,128]{3,2,1,0:T(8,128)(2,1)} %bitcast.3), calls=%async_computation | async-start | bytes 1048576 | tf_op jit(solution)/shard_map/all_to_all | solution.py:496
  59.7 20.5 %collective-permute-start.1 = (bf16[16,2,64,384]{3,2,1,0:T(8,128)(2,1)S(1)}, bf16[16,2,64,384]{3,2,1,0:T(8,128)(2,1)}, u32[]{:S(2)}, u32[]{:S(2)}) collective-permute-start(bf16[16,2,64,384]{3,2,1,0:T(8,128)(2,1)S(1)} %all-to-all-done.1.spectra_ref), channel_id=1, source_target_pairs={{0,1},{1,0},{2,3},{3,2},{4,5},{5,4},{6,7},{7,6},{8,9},{9,8},{10,11... | collective-permute-start | bytes 4718600 | tf_op jit(solution)/shard_map/ppermute | solution.py:505
  73.7 1.9 %collective-permute-start = (bf16[16,2,64,128]{3,2,1,0:T(8,128)(2,1)S(1)}, bf16[16,2,64,128]{3,2,1,0:T(8,128)(2,1)S(1)}, u32[]{:S(2)}, u32[]{:S(2)}) collective-permute-start(bf16[16,2,64,128]{3,2,1,0:T(8,128)(2,1)S(1)} %all-to-all-done.spectra_ref), channel_id=1, source_target_pairs={{0,1},{1,0},{2,3},{3,2},{4,5},{5,4},{6,7},{7,6},{8,9},{9,8},{10,11... | collective-permute-start | bytes 1572872 | tf_op jit(solution)/shard_map/ppermute | solution.py:505
  85.3 18.5 %all-to-all-start.3 = ((bf16[16,2,64,128]{3,2,1,0:T(8,128)(2,1)}), bf16[16,2,64,128]{3,2,1,0:T(8,128)(2,1)S(1)}, u32[]{:S(2)}, u32[]{:S(2)}) async-start(bf16[16,2,64,128]{3,2,1,0:T(8,128)(2,1)} %get-tuple-element.26), calls=%async_computation.3 | async-start | bytes 1048576 | tf_op jit(solution)/shard_map/all_to_all | solution.py:496
  103.8 47.2 %all-to-all-start.2 = ((bf16[16,2,64,128]{3,2,1,0:T(8,128)(2,1)}), bf16[16,2,64,128]{3,2,1,0:T(8,128)(2,1)S(1)}, u32[]{:S(2)}, u32[]{:S(2)}) async-start(bf16[16,2,64,128]{3,2,1,0:T(8,128)(2,1)} %get-tuple-element.25), calls=%async_computation.2 | async-start | bytes 1048576 | tf_op jit(solution)/shard_map/all_to_all | solution.py:496
  108.2 3.8 %collective-permute-start.2 = (bf16[2,64,256]{2,1,0:T(8,128)(2,1)}, bf16[2,64,256]{2,1,0:T(8,128)(2,1)S(1)}, u32[]{:S(2)}, u32[]{:S(2)}) collective-permute-start(bf16[2,64,256]{2,1,0:T(8,128)(2,1)} %get-tuple-element.28), channel_id=1, source_target_pairs={{0,1},{1,0},{2,3},{3,2},{4,5},{5,4},{6,7},{7,6},{8,9},{9,8},{10,11... | collective-permute-start | bytes 196616 | tf_op jit(solution)/shard_map/ppermute | solution.py:526
  108.4 6.4 %collective-permute-start.3 = (bf16[2,64,256]{2,1,0:T(8,128)(2,1)}, bf16[2,64,256]{2,1,0:T(8,128)(2,1)S(1)}, u32[]{:S(2)}, u32[]{:S(2)}) collective-permute-start(bf16[2,64,256]{2,1,0:T(8,128)(2,1)} %get-tuple-element.29), channel_id=1, source_target_pairs={{0,2},{1,3},{2,0},{3,1},{4,6},{5,7},{6,4},{7,5},{8,10},{9,11},{10,... | collective-permute-start | bytes 196616 | tf_op jit(solution)/shard_map/ppermute | solution.py:526
  110.0 7.7 %collective-permute-start.4 = (bf16[2,64,256]{2,1,0:T(8,128)(2,1)}, bf16[2,64,256]{2,1,0:T(8,128)(2,1)S(1)}, u32[]{:S(2)}, u32[]{:S(2)}) collective-permute-start(bf16[2,64,256]{2,1,0:T(8,128)(2,1)} %get-tuple-element.30), channel_id=1, source_target_pairs={{0,3},{1,2},{2,1},{3,0},{4,7},{5,6},{6,5},{7,4},{8,11},{9,10},{10,... | collective-permute-start | bytes 196616 | tf_op jit(solution)/shard_map/ppermute | solution.py:526
  110.4 9.6 %collective-permute-start.5 = (bf16[2,64,256]{2,1,0:T(8,128)(2,1)}, bf16[2,64,256]{2,1,0:T(8,128)(2,1)S(1)}, u32[]{:S(2)}, u32[]{:S(2)}) collective-permute-start(bf16[2,64,256]{2,1,0:T(8,128)(2,1)} %get-tuple-element.31), channel_id=1, source_target_pairs={{0,4},{1,5},{2,6},{3,7},{4,0},{5,1},{6,2},{7,3},{8,12},{9,13},{10,... | collective-permute-start | bytes 196616 | tf_op jit(solution)/shard_map/ppermute | solution.py:526
  111.8 12.1 %collective-permute-start.6 = (bf16[2,64,256]{2,1,0:T(8,128)(2,1)}, bf16[2,64,256]{2,1,0:T(8,128)(2,1)S(1)}, u32[]{:S(2)}, u32[]{:S(2)}) collective-permute-start(bf16[2,64,256]{2,1,0:T(8,128)(2,1)} %get-tuple-element.32), channel_id=1, source_target_pairs={{0,5},{1,4},{2,7},{3,6},{4,1},{5,0},{6,3},{7,2},{8,13},{9,12},{10,... | collective-permute-start | bytes 196616 | tf_op jit(solution)/shard_map/ppermute | solution.py:526
  112.0 13.5 %collective-permute-start.7 = (bf16[2,64,256]{2,1,0:T(8,128)(2,1)}, bf16[2,64,256]{2,1,0:T(8,128)(2,1)S(1)}, u32[]{:S(2)}, u32[]{:S(2)}) collective-permute-start(bf16[2,64,256]{2,1,0:T(8,128)(2,1)} %get-tuple-element.33), channel_id=1, source_target_pairs={{0,6},{1,7},{2,4},{3,5},{4,2},{5,3},{6,0},{7,1},{8,14},{9,15},{10,... | collective-permute-start | bytes 196616 | tf_op jit(solution)/shard_map/ppermute | solution.py:526
  114.8 14.3 %collective-permute-start.8 = (bf16[2,64,256]{2,1,0:T(8,128)(2,1)}, bf16[2,64,256]{2,1,0:T(8,128)(2,1)S(1)}, u32[]{:S(2)}, u32[]{:S(2)}) collective-permute-start(bf16[2,64,256]{2,1,0:T(8,128)(2,1)} %get-tuple-element.34), channel_id=1, source_target_pairs={{0,7},{1,6},{2,5},{3,4},{4,3},{5,2},{6,1},{7,0},{8,15},{9,14},{10,... | collective-permute-start | bytes 196616 | tf_op jit(solution)/shard_map/ppermute | solution.py:526
  117.7 13.1 %collective-permute-start.9 = (bf16[2,64,256]{2,1,0:T(8,128)(2,1)}, bf16[2,64,256]{2,1,0:T(8,128)(2,1)S(1)}, u32[]{:S(2)}, u32[]{:S(2)}) collective-permute-start(bf16[2,64,256]{2,1,0:T(8,128)(2,1)} %get-tuple-element.35), channel_id=1, source_target_pairs={{0,8},{1,9},{2,10},{3,11},{4,12},{5,13},{6,14},{7,15},{8,0},{9,1},... | collective-permute-start | bytes 196616 | tf_op jit(solution)/shard_map/ppermute | solution.py:526
  120.0 12.2 %collective-permute-start.10 = (bf16[2,64,256]{2,1,0:T(8,128)(2,1)}, bf16[2,64,256]{2,1,0:T(8,128)(2,1)S(1)}, u32[]{:S(2)}, u32[]{:S(2)}) collective-permute-start(bf16[2,64,256]{2,1,0:T(8,128)(2,1)} %get-tuple-element.36), channel_id=1, source_target_pairs={{0,9},{1,8},{2,11},{3,10},{4,13},{5,12},{6,15},{7,14},{8,1},{9,0},... | collective-permute-start | bytes 196616 | tf_op jit(solution)/shard_map/ppermute | solution.py:526
  123.8 13.6 %collective-permute-start.11 = (bf16[2,64,256]{2,1,0:T(8,128)(2,1)}, bf16[2,64,256]{2,1,0:T(8,128)(2,1)S(1)}, u32[]{:S(2)}, u32[]{:S(2)}) collective-permute-start(bf16[2,64,256]{2,1,0:T(8,128)(2,1)} %get-tuple-element.37), channel_id=1, source_target_pairs={{0,10},{1,11},{2,8},{3,9},{4,14},{5,15},{6,12},{7,13},{8,2},{9,3},... | collective-permute-start | bytes 196616 | tf_op jit(solution)/shard_map/ppermute | solution.py:526
  125.6 15.8 %collective-permute-start.12 = (bf16[2,64,256]{2,1,0:T(8,128)(2,1)}, bf16[2,64,256]{2,1,0:T(8,128)(2,1)S(1)}, u32[]{:S(2)}, u32[]{:S(2)}) collective-permute-start(bf16[2,64,256]{2,1,0:T(8,128)(2,1)} %get-tuple-element.38), channel_id=1, source_target_pairs={{0,11},{1,10},{2,9},{3,8},{4,15},{5,14},{6,13},{7,12},{8,3},{9,2},... | collective-permute-start | bytes 196616 | tf_op jit(solution)/shard_map/ppermute | solution.py:526
  129.1 12.3 %collective-permute-start.13 = (bf16[2,64,256]{2,1,0:T(8,128)(2,1)}, bf16[2,64,256]{2,1,0:T(8,128)(2,1)S(1)}, u32[]{:S(2)}, u32[]{:S(2)}) collective-permute-start(bf16[2,64,256]{2,1,0:T(8,128)(2,1)} %get-tuple-element.39), channel_id=1, source_target_pairs={{0,12},{1,13},{2,14},{3,15},{4,8},{5,9},{6,10},{7,11},{8,4},{9,5},... | collective-permute-start | bytes 196616 | tf_op jit(solution)/shard_map/ppermute | solution.py:526
  130.8 10.6 %collective-permute-start.14 = (bf16[2,64,256]{2,1,0:T(8,128)(2,1)}, bf16[2,64,256]{2,1,0:T(8,128)(2,1)S(1)}, u32[]{:S(2)}, u32[]{:S(2)}) collective-permute-start(bf16[2,64,256]{2,1,0:T(8,128)(2,1)} %get-tuple-element.40), channel_id=1, source_target_pairs={{0,13},{1,12},{2,15},{3,14},{4,9},{5,8},{6,11},{7,10},{8,5},{9,4},... | collective-permute-start | bytes 196616 | tf_op jit(solution)/shard_map/ppermute | solution.py:526
  132.2 9.2 %collective-permute-start.15 = (bf16[2,64,256]{2,1,0:T(8,128)(2,1)}, bf16[2,64,256]{2,1,0:T(8,128)(2,1)S(1)}, u32[]{:S(2)}, u32[]{:S(2)}) collective-permute-start(bf16[2,64,256]{2,1,0:T(8,128)(2,1)} %get-tuple-element.41), channel_id=1, source_target_pairs={{0,14},{1,15},{2,12},{3,13},{4,10},{5,11},{6,8},{7,9},{8,6},{9,7},... | collective-permute-start | bytes 196616 | tf_op jit(solution)/shard_map/ppermute | solution.py:526
  137.4 6.7 %collective-permute-start.16 = (bf16[2,64,256]{2,1,0:T(8,128)(2,1)}, bf16[2,64,256]{2,1,0:T(8,128)(2,1)S(1)}, u32[]{:S(2)}, u32[]{:S(2)}) collective-permute-start(bf16[2,64,256]{2,1,0:T(8,128)(2,1)} %get-tuple-element.42), channel_id=1, source_target_pairs={{0,15},{1,14},{2,13},{3,12},{4,11},{5,10},{6,9},{7,8},{8,7},{9,6},... | collective-permute-start | bytes 196616 | tf_op jit(solution)/shard_map/ppermute | solution.py:526
  (8 other events, 47.8 us)
